TPU v7x, 512 devices: a whole 4x8x8 slice. The times are simulated.
512 devices in a mesh: aux: 64 (over z, y), occ: 8 (over x, core).
Axes of the slice: x: 4, y: 8, z: 8, core: 2. Of those that a mesh axis runs over, the one named last changes fastest.
Arguments:
- integrals: bfloat16 [128, 21, 512, 512], P('aux', None, 'occ'), may hold values from -0.40234375 to 0.40234375
- orbitals: bfloat16 [3072, 384], replicated, may hold values from -0.109375 to 0.109375
Outputs:
- k_tiles: float32 [512, 21, 512], P('aux', None, 'occ')
All inputs are finite; a program needn't handle non-finite values.
Results may differ from a plain program's by a relative error of at most 0.0017.
Values may be sent and summed in bfloat16 or wider, within the bound.
No kernel may reach another device: no remote copies, remote signals or barrier semaphores. Data moves between devices by JAX's collectives and lax.ppermute only.
A program may use at most 64 MiB of HBM per device.

v0:
```python
import jax
import jax.numpy as jnp
import numpy as np
from jax import lax
from jax.experimental import pallas as pl
from jax.experimental.pallas import tpu as pltpu
from jax.sharding import Mesh
from jax.sharding import PartitionSpec as P


NB = 6
AXES = ("z", "y", "x", "core")
F32 = jnp.float32
BF16 = jnp.bfloat16
VMEM = pl.BlockSpec(memory_space=pltpu.VMEM)
HBM = pl.BlockSpec(memory_space=pltpu.HBM)


def tile_of(a, b):
    return a * NB - a * (a - 1) // 2 + b - a


OFF = [(a, b) for a in range(NB) for b in range(a + 1, NB)]
OFF_AT = {pair: at for at, pair in enumerate(OFF)}


def call(kernel, out_shape, args, flops, nbytes, vmem_mib, **options):
    options.setdefault("in_specs", [VMEM] * len(args))
    options.setdefault("out_specs", jax.tree.map(lambda _: VMEM, out_shape))
    return pl.pallas_call(
        kernel,
        out_shape=out_shape,
        compiler_params=pltpu.CompilerParams(vmem_limit_bytes=vmem_mib * 2**20),
        cost_estimate=pl.CostEstimate(flops=flops, bytes_accessed=nbytes, transcendentals=0),
        **options,
    )(*args)


def pack_kernel(tiles, out):
    parts = out.shape[0]
    width = tiles.shape[3] // parts
    for at, (a, b) in enumerate(OFF):
        t = tile_of(a, b)
        first, second = tiles[0, t], tiles[1, t]
        for d in range(parts):
            cols = slice(d * width, (d + 1) * width)
            out[d, at] = jnp.concatenate([first[:, cols], second[:, cols]], axis=1)


def own_kernel(tiles, coeffs, out):
    size = tiles.shape[3]
    rows = 2 * tiles.shape[2]
    for m in range(NB):
        lhs = jnp.concatenate([tiles[:, tile_of(a, m)].reshape(rows, size) for a in range(m + 1)], axis=0)
        part = jnp.dot(lhs, coeffs[m * size : (m + 1) * size], preferred_element_type=F32)
        part = part.reshape(m + 1, rows, part.shape[1])
        if m:
            out[:m] = out[:m] + part[:m]
        out[m] = part[m]


def lower_kernel(received, coeffs_hbm, own_hbm, out, out_a, out_b, coeffs, own, sems):
    size = received.shape[0] * received.shape[2]
    lanes = received.shape[3]
    half = lanes // 2
    occ = coeffs.shape[1]
    copies = []
    for a in range(NB - 1):
        rows = pl.ds(a * size, size)
        copies.append(pltpu.make_async_copy(coeffs_hbm.at[rows], coeffs.at[rows], sems.at[a]))
    own_copy = pltpu.make_async_copy(own_hbm, own, sems.at[NB - 1])
    copies[0].start()
    own_copy.start()
    for copy in copies[1:]:
        copy.start()
    sums = [None] * NB
    for a in range(NB - 1):
        copies[a].wait()
        lhs = jnp.concatenate(
            [received[:, OFF_AT[a, b]].reshape(size, lanes) for b in range(a + 1, NB)], axis=1
        )
        part = lax.dot_general(
            lhs, coeffs[a * size : (a + 1) * size], (((0,), (0,)), ((), ())), preferred_element_type=F32
        )
        if a == 0:
            own_copy.wait()
            sums = [own[b] for b in range(NB)]
        for b in range(a + 1, NB):
            at = (b - a - 1) * lanes
            sums[b] = sums[b] + part[at : at + lanes]
    for b in range(NB):
        both = sums[b].astype(BF16)
        side = out_a if b < NB // 2 else out_b
        for ref, at in ((out, b), (side, b % (NB // 2))):
            ref[at * half : (at + 1) * half, :occ] = both[:half]
            ref[at * half : (at + 1) * half, occ:] = both[half:]


def tiles_kernel(pieces, mine, sib, out_mine, out_sib):
    width = mine.shape[0] // NB
    high = out_mine.shape[1]
    groups = width // high
    for cols, out in ((mine, out_mine), (sib, out_sib)):
        right = cols[...]
        for piece, first, count, place in pieces:
            full = lax.dot_general(
                piece[...], right, (((1,), (1,)), ((), ())), preferred_element_type=F32
            ).astype(BF16)
            for k in range(count):
                a = first + k
                part = full[k * width : (k + 1) * width, a * width :]
                begin = tile_of(a, a) * width
                out[place * groups : (place + 1) * groups, :, begin : begin + part.shape[1]] = part.reshape(
                    groups, high, part.shape[1]
                )


def near_kernel(own, left_a, left_b, right_a, right_b, sib, out_mine, out_sib):
    pieces = [(own, 0, NB, 0)]
    for place, (low, high) in ((1, (left_a, left_b)), (2, (right_a, right_b))):
        pieces += [(low, 0, NB // 2, place), (high, NB // 2, NB // 2, place)]
    tiles_kernel(pieces, own, sib, out_mine, out_sib)


def far_kernel(far_a, far_b, own, sib, out_mine, out_sib):
    pieces = [(far_a, 0, NB // 2, 0), (far_b, NB // 2, NB // 2, 0)]
    tiles_kernel(pieces, own, sib, out_mine, out_sib)


def gather_kernel(near, far, near_s, far_s, out):
    xs, cores = lax.axis_size("x"), lax.axis_size("core")
    zs, ys = lax.axis_size("z"), lax.axis_size("y")
    x, core = lax.axis_index("x"), lax.axis_index("core")
    for dc, sources in ((0, (near, far)), (1, (near_s, far_s))):
        for at, dx in enumerate((0, xs - 1, 1, 2)):
            source, first = (sources[0], at * ys) if at < 3 else (sources[1], 0)
            z = lax.rem(x + dx, xs) * cores + lax.rem(core + dc, cores)
            for y in range(ys):
                out[jnp.where(core == 0, z * ys + y, y * zs + z)] = source[first + y]


def sum_of(received):
    total = received[0].astype(F32)
    for k in range(1, received.shape[0]):
        total = total + received[k].astype(F32)
    return total


def sum_kernel(received, out):
    out[...] = sum_of(received)


def last_kernel(received, out):
    total = sum_of(received)
    width = out.shape[2]
    for t in range(out.shape[0]):
        out[t] = total[:, t * width : (t + 1) * width]


def body(integrals, orbitals):
    slabs, tile_count, width, size = integrals.shape
    occ = orbitals.shape[1]
    xs, cores, zs, ys = (lax.axis_size(name) for name in ("x", "core", "z", "y"))
    parts = xs * cores
    rows = size // (zs * ys)
    flops = 2 * slabs * width * size * occ

    lane_block = size // xs
    packed = call(
        pack_kernel,
        jax.ShapeDtypeStruct((parts, len(OFF), width, slabs * width), BF16),
        (integrals,),
        0,
        2 * integrals.size * 2,
        56,
        grid=(xs,),
        in_specs=[pl.BlockSpec((slabs, tile_count, width, lane_block), lambda i: (0, 0, 0, i))],
        out_specs=pl.BlockSpec((cores, len(OFF), width, slabs * width), lambda i: (i, 0, 0, 0)),
    )
    received = lax.all_to_all(packed, ("x", "core"), 0, 0)
    own = call(
        own_kernel,
        jax.ShapeDtypeStruct((NB, slabs * width, occ), F32),
        (integrals, orbitals),
        flops * tile_count,
        2 * integrals.size + 2 * orbitals.size,
        56,
    )
    share = jax.ShapeDtypeStruct((NB * width, slabs * occ), BF16)
    side = jax.ShapeDtypeStruct((NB // 2 * width, slabs * occ), BF16)
    half, half_a, half_b = call(
        lower_kernel,
        (share, side, side),
        (received, orbitals, own),
        flops * len(OFF),
        2 * received.size + 2 * orbitals.size,
        20,
        in_specs=[VMEM, HBM, HBM],
        scratch_shapes=[
            pltpu.VMEM(orbitals.shape, BF16),
            pltpu.VMEM(own.shape, F32),
            pltpu.SemaphoreType.DMA((NB,)),
        ],
    )

    up = [(i, (i + 1) % xs) for i in range(xs)]
    down = [(i, (i - 1) % xs) for i in range(xs)]
    swap = [(i, (i + 1) % cores) for i in range(cores)]
    left_a = lax.ppermute(half_a, "x", up)
    right_b = lax.ppermute(half_b, "x", down)
    left_b = lax.ppermute(half_b, "x", up)
    right_a = lax.ppermute(half_a, "x", down)
    far_a = lax.ppermute(left_a, "x", up)
    far_b = lax.ppermute(right_b, "x", down)
    sib = lax.ppermute(half, "core", swap)

    product = 2 * share.shape[0] ** 2 * share.shape[1]
    near_shape = jax.ShapeDtypeStruct((3 * ys, rows, tile_count * width), BF16)
    far_shape = jax.ShapeDtypeStruct((ys, rows, tile_count * width), BF16)
    near, near_s = call(
        near_kernel,
        (near_shape, near_shape),
        (half, left_a, left_b, right_a, right_b, sib),
        6 * product,
        8 * half.size,
        16,
    )
    near_s = lax.ppermute(near_s, "core", swap)
    far, far_s = call(
        far_kernel, (far_shape, far_shape), (far_a, far_b, half, sib), 2 * product, 6 * half.size, 12
    )
    far_s = lax.ppermute(far_s, "core", swap)
    partial = call(
        gather_kernel,
        jax.ShapeDtypeStruct((zs * ys, rows, tile_count * width), BF16),
        (near, far, near_s, far_s),
        0,
        8 * near.size,
        12,
    )

    at = np.arange(zs * ys * parts).reshape(zs, ys, xs, cores)
    along_z = [[at[:, y, x, c].tolist() for x in range(xs) for y in range(ys)] for c in range(2)]
    along_y = [[at[z, :, x, c].tolist() for x in range(xs) for z in range(zs)] for c in range(2)]
    arrived = lax.all_to_all(
        partial.reshape(zs, ys * rows, tile_count * width), AXES, 0, 0, axis_index_groups=along_z[0] + along_y[1]
    )
    summed = call(
        sum_kernel,
        jax.ShapeDtypeStruct(arrived.shape[1:], F32),
        (arrived,),
        arrived.size,
        2 * arrived.size,
        8,
    )
    arrived = lax.all_to_all(
        summed.reshape(ys, rows, tile_count * width), AXES, 0, 0, axis_index_groups=along_y[0] + along_z[1]
    )
    tiles = call(
        last_kernel,
        jax.ShapeDtypeStruct((tile_count, rows, width), F32),
        (arrived,),
        arrived.size,
        4 * arrived.size,
        8,
    )
    return jnp.transpose(tiles, (1, 0, 2))


def solution(mesh):
    grid = Mesh(mesh.devices.reshape(8, 8, 4, 2), AXES)
    return jax.shard_map(
        body,
        mesh=grid,
        in_specs=(P(("z", "y"), None, ("x", "core"), None), P()),
        out_specs=P(("z", "y"), None, ("x", "core")),
        check_vma=False,
    )
```

profile of v0, /device:TPU:6, one launch (start us, length us, event | category | flops | bytes accessed | tf_op | source)
XLA Modules:
  0.0 139.3 jit_solution(16949894571428231911)
XLA Ops:
  0.0 4.2 %shard_map.28 = bf16[8,15,64,128]{3,2,1,0:T(8,128)(2,1)} custom-call(bf16[2,21,64,512]{3,2,1,0:T(8,128)(2,1)} %tiles.3), custom_call_target="tpu_custom_call" | custom-call | bytes 5505024 | tf_op jit(solution)/shard_map/pallas_call | solution.py:30
  4.2 10.1 %all-to-all-start = ((bf16[8,15,64,128]{3,2,1,0:T(8,128)(2,1)}), bf16[8,15,64,128]{3,2,1,0:T(8,128)(2,1)}, u32[]{:S(2)}, u32[]{:S(2)}) async-start(bf16[8,15,64,128]{3,2,1,0:T(8,128)(2,1)} %shard_map.28), calls=%async_computation | async-start | bytes 3932160 | tf_op jit(solution)/shard_map/all_to_all | solution.py:180
  14.3 0.0 copy-start
  14.3 5.2 %shard_map.29.own_hbm = f32[6,128,384]{2,1,0:T(8,128)} custom-call(bf16[2,21,64,512]{3,2,1,0:T(8,128)(2,1)} %tiles.3, bf16[3072,384]{1,0:T(8,128)(2,1)} %coeffs_hbm.1), custom_call_target="tpu_custom_call" | custom-call | flops 1056964608 | bytes 5111808 | tf_op jit(solution)/shard_map/pallas_call | solution.py:30
  19.5 18.5 %all-to-all-done.received = bf16[8,15,64,128]{3,2,1,0:T(8,128)(2,1)} async-done(((bf16[8,15,64,128]{3,2,1,0:T(8,128)(2,1)}), bf16[8,15,64,128]{3,2,1,0:T(8,128)(2,1)}, u32[]{:S(2)}, u32[]{:S(2)}) %all-to-all-start) | async-done | bytes 1966112 | tf_op jit(solution)/shard_map/all_to_all | solution.py:180
  38.1 0.0 copy-done
  38.1 0.0 copy-start.1
  38.1 1.3 copy-done.1
  39.3 4.9 %shard_map.30 = (bf16[384,768]{1,0:T(8,128)(2,1)S(1)}, bf16[192,768]{1,0:T(8,128)(2,1)S(1)}, bf16[192,768]{1,0:T(8,128)(2,1)S(1)}) custom-call(bf16[8,15,64,128]{3,2,1,0:T(8,128)(2,1)} %all-to-all-done.received, bf16[3072,384]{1,0:T(8,128)(2,1)S(1)} %copy-done, f32[6,128,384]{2,1,0:T(8,128)S(1)} %copy-done.1), custom_call_target="tpu_custom_call" | custom-call | flops 754974720 | bytes 4325376 | tf_op jit(solution)/shard_map/pallas_call | solution.py:30
  44.2 1.9 %collective-permute-start.4 = (bf16[384,768]{1,0:T(8,128)(2,1)S(1)}, bf16[384,768]{1,0:T(8,128)(2,1)S(1)}, u32[]{:S(2)}, u32[]{:S(2)}) collective-permute-start(bf16[384,768]{1,0:T(8,128)(2,1)S(1)} %get-tuple-element.12.own), channel_id=1, source_target_pairs={{0,1},{1,0},{2,3},{3,2},{4,5},{5,4},{6,7},{7,6},{8,9},{9,8},{10,11... | collective-permute-start | bytes 1769480 | tf_op jit(solution)/shard_map/ppermute | solution.py:215
  46.2 4.0 %collective-permute-start = (bf16[192,768]{1,0:T(8,128)(2,1)S(1)}, bf16[192,768]{1,0:T(8,128)(2,1)S(1)}, u32[]{:S(2)}, u32[]{:S(2)}) collective-permute-start(bf16[192,768]{1,0:T(8,128)(2,1)S(1)} %get-tuple-element.13), channel_id=1, source_target_pairs={{0,2},{2,4},{4,6},{6,0},{1,3},{3,5},{5,7},{7,1},{8,10},{10,12},{12... | collective-permute-start | bytes 884744 | tf_op jit(solution)/shard_map/ppermute | solution.py:209
  50.2 1.9 %collective-permute-start.3 = (bf16[192,768]{1,0:T(8,128)(2,1)S(1)}, bf16[192,768]{1,0:T(8,128)(2,1)S(1)}, u32[]{:S(2)}, u32[]{:S(2)}) collective-permute-start(bf16[192,768]{1,0:T(8,128)(2,1)S(1)} %get-tuple-element.14), channel_id=1, source_target_pairs={{0,6},{2,0},{4,2},{6,4},{1,7},{3,1},{5,3},{7,5},{8,14},{10,8},{12,... | collective-permute-start | bytes 884744 | tf_op jit(solution)/shard_map/ppermute | solution.py:210
  52.1 5.1 %collective-permute-start.1 = (bf16[192,768]{1,0:T(8,128)(2,1)S(1)}, bf16[192,768]{1,0:T(8,128)(2,1)S(1)}, u32[]{:S(2)}, u32[]{:S(2)}) collective-permute-start(bf16[192,768]{1,0:T(8,128)(2,1)S(1)} %get-tuple-element.14), channel_id=1, source_target_pairs={{0,2},{2,4},{4,6},{6,0},{1,3},{3,5},{5,7},{7,1},{8,10},{10,12},{12... | collective-permute-start | bytes 884744 | tf_op jit(solution)/shard_map/ppermute | solution.py:211
  57.2 1.9 %collective-permute-start.2 = (bf16[192,768]{1,0:T(8,128)(2,1)S(1)}, bf16[192,768]{1,0:T(8,128)(2,1)S(1)}, u32[]{:S(2)}, u32[]{:S(2)}) collective-permute-start(bf16[192,768]{1,0:T(8,128)(2,1)S(1)} %get-tuple-element.13), channel_id=1, source_target_pairs={{0,6},{2,0},{4,2},{6,4},{1,7},{3,1},{5,3},{7,5},{8,14},{10,8},{12,... | collective-permute-start | bytes 884744 | tf_op jit(solution)/shard_map/ppermute | solution.py:212
  59.2 0.0 collective-permute-done.left_a
  59.2 3.2 %collective-permute-done.3.right_b = bf16[192,768]{1,0:T(8,128)(2,1)S(1)} collective-permute-done((bf16[192,768]{1,0:T(8,128)(2,1)S(1)}, bf16[192,768]{1,0:T(8,128)(2,1)S(1)}, u32[]{:S(2)}, u32[]{:S(2)}) %collective-permute-start.3) | collective-permute-done | bytes 294944 | tf_op jit(solution)/shard_map/ppermute | solution.py:210
  62.4 1.4 %collective-permute-done.1.left_b = bf16[192,768]{1,0:T(8,128)(2,1)S(1)} collective-permute-done((bf16[192,768]{1,0:T(8,128)(2,1)S(1)}, bf16[192,768]{1,0:T(8,128)(2,1)S(1)}, u32[]{:S(2)}, u32[]{:S(2)}) %collective-permute-start.1) | collective-permute-done | bytes 294944 | tf_op jit(solution)/shard_map/ppermute | solution.py:211
  63.8 5.1 %collective-permute-done.2.right_a = bf16[192,768]{1,0:T(8,128)(2,1)S(1)} collective-permute-done((bf16[192,768]{1,0:T(8,128)(2,1)S(1)}, bf16[192,768]{1,0:T(8,128)(2,1)S(1)}, u32[]{:S(2)}, u32[]{:S(2)}) %collective-permute-start.2) | collective-permute-done | bytes 294944 | tf_op jit(solution)/shard_map/ppermute | solution.py:212
  68.9 0.0 collective-permute-done.4.sib
  68.9 2.3 %shard_map.31 = (bf16[24,8,1344]{2,1,0:T(8,128)(2,1)S(1)}, bf16[24,8,1344]{2,1,0:T(8,128)(2,1)S(1)}) custom-call(bf16[384,768]{1,0:T(8,128)(2,1)S(1)} %get-tuple-element.12.own, bf16[192,768]{1,0:T(8,128)(2,1)S(1)} %collective-permute-done.left_a, bf16[192,768]{1,0:T(8,128)(2,1)S(1)} %collective-permute-done.1.left_b, ...), custom_call_target="tpu_custom_call" | custom-call | flops 1358954496 | bytes 2359296 | tf_op jit(solution)/shard_map/pallas_call | solution.py:30
  71.3 1.9 %collective-permute-start.7 = (bf16[24,8,1344]{2,1,0:T(8,128)(2,1)S(1)}, bf16[24,8,1344]{2,1,0:T(8,128)(2,1)S(1)}, u32[]{:S(2)}, u32[]{:S(2)}) collective-permute-start(bf16[24,8,1344]{2,1,0:T(8,128)(2,1)S(1)} %get-tuple-element.17), channel_id=1, source_target_pairs={{0,1},{1,0},{2,3},{3,2},{4,5},{5,4},{6,7},{7,6},{8,9},{9,8},{10,11... | collective-permute-start | bytes 1548296 | tf_op jit(solution)/shard_map/ppermute | solution.py:228
  73.2 1.9 %collective-permute-start.5 = (bf16[192,768]{1,0:T(8,128)(2,1)S(1)}, bf16[192,768]{1,0:T(8,128)(2,1)S(1)}, u32[]{:S(2)}, u32[]{:S(2)}) collective-permute-start(bf16[192,768]{1,0:T(8,128)(2,1)S(1)} %collective-permute-done.left_a), channel_id=1, source_target_pairs={{0,2},{2,4},{4,6},{6,0},{1,3},{3,5},{5,7},{7,1},{8,10},{10,12},{12... | collective-permute-start | bytes 884744 | tf_op jit(solution)/shard_map/ppermute | solution.py:213
  75.1 3.9 %collective-permute-start.6 = (bf16[192,768]{1,0:T(8,128)(2,1)S(1)}, bf16[192,768]{1,0:T(8,128)(2,1)S(1)}, u32[]{:S(2)}, u32[]{:S(2)}) collective-permute-start(bf16[192,768]{1,0:T(8,128)(2,1)S(1)} %collective-permute-done.3.right_b), channel_id=1, source_target_pairs={{0,6},{2,0},{4,2},{6,4},{1,7},{3,1},{5,3},{7,5},{8,14},{10,8},{12,... | collective-permute-start | bytes 884744 | tf_op jit(solution)/shard_map/ppermute | solution.py:214
  79.0 5.4 %collective-permute-done.5.far_a = bf16[192,768]{1,0:T(8,128)(2,1)S(1)} collective-permute-done((bf16[192,768]{1,0:T(8,128)(2,1)S(1)}, bf16[192,768]{1,0:T(8,128)(2,1)S(1)}, u32[]{:S(2)}, u32[]{:S(2)}) %collective-permute-start.5) | collective-permute-done | bytes 294944 | tf_op jit(solution)/shard_map/ppermute | solution.py:213
  84.5 3.1 %collective-permute-done.6.far_b = bf16[192,768]{1,0:T(8,128)(2,1)S(1)} collective-permute-done((bf16[192,768]{1,0:T(8,128)(2,1)S(1)}, bf16[192,768]{1,0:T(8,128)(2,1)S(1)}, u32[]{:S(2)}, u32[]{:S(2)}) %collective-permute-start.6) | collective-permute-done | bytes 294944 | tf_op jit(solution)/shard_map/ppermute | solution.py:214
  87.6 1.0 shard_map.32
  88.6 1.9 %collective-permute-start.8 = (bf16[8,8,1344]{2,1,0:T(8,128)(2,1)S(1)}, bf16[8,8,1344]{2,1,0:T(8,128)(2,1)S(1)}, u32[]{:S(2)}, u32[]{:S(2)}) collective-permute-start(bf16[8,8,1344]{2,1,0:T(8,128)(2,1)S(1)} %get-tuple-element.18), channel_id=1, source_target_pairs={{0,1},{1,0},{2,3},{3,2},{4,5},{5,4},{6,7},{7,6},{8,9},{9,8},{10,11... | collective-permute-start | bytes 516104 | tf_op jit(solution)/shard_map/ppermute | solution.py:232
  90.5 1.4 collective-permute-done.8.far_s
  91.9 0.0 collective-permute-done.7.near_s
  91.9 0.1 shard_map.33
  92.0 28.0 %all_to_all.15.received = bf16[8,64,1344]{2,1,0:T(8,128)(2,1)S(1)} all-to-all(bf16[8,64,1344]{2,1,0:T(8,128)(2,1)S(1)} %bitcast.3), channel_id=1, replica_groups={{0,64,128,192,256,320,384,448},{8,72,136,200,264,328,392,456},{16,80,14..., dimensions={0} | all-to-all | bytes 2752512 | tf_op jit(solution)/shard_map/all_to_all | solution.py:245
  120.0 0.2 shard_map.34
  120.2 18.4 %all_to_all.16.received = f32[8,8,1344]{2,1,0:T(8,128)S(1)} all-to-all(f32[8,8,1344]{2,1,0:T(8,128)S(1)} %bitcast.4), channel_id=1, replica_groups={{0,8,16,24,32,40,48,56},{64,72,80,88,96,104,112,120},{128,136,144,152,1..., dimensions={0} | all-to-all | bytes 688128 | tf_op jit(solution)/shard_map/all_to_all | solution.py:256
  138.6 0.7 shard_map.35
Async XLA Ops:
  4.2 33.9 %all-to-all-start = ((bf16[8,15,64,128]{3,2,1,0:T(8,128)(2,1)}), bf16[8,15,64,128]{3,2,1,0:T(8,128)(2,1)}, u32[]{:S(2)}, u32[]{:S(2)}) async-start(bf16[8,15,64,128]{3,2,1,0:T(8,128)(2,1)} %shard_map.28), calls=%async_computation | async-start | bytes 3932160 | tf_op jit(solution)/shard_map/all_to_all | solution.py:180
  14.3 23.8 %copy-start = (bf16[3072,384]{1,0:T(8,128)(2,1)S(1)}, bf16[3072,384]{1,0:T(8,128)(2,1)}, u32[]{:S(2)}) copy-start(bf16[3072,384]{1,0:T(8,128)(2,1)} %coeffs_hbm.1) | copy-start | bytes 7077892
  38.1 1.3 copy-start.1
  44.2 24.7 %collective-permute-start.4 = (bf16[384,768]{1,0:T(8,128)(2,1)S(1)}, bf16[384,768]{1,0:T(8,128)(2,1)S(1)}, u32[]{:S(2)}, u32[]{:S(2)}) collective-permute-start(bf16[384,768]{1,0:T(8,128)(2,1)S(1)} %get-tuple-element.12.own), channel_id=1, source_target_pairs={{0,1},{1,0},{2,3},{3,2},{4,5},{5,4},{6,7},{7,6},{8,9},{9,8},{10,11... | collective-permute-start | bytes 1769480 | tf_op jit(solution)/shard_map/ppermute | solution.py:215
  46.2 13.0 %collective-permute-start = (bf16[192,768]{1,0:T(8,128)(2,1)S(1)}, bf16[192,768]{1,0:T(8,128)(2,1)S(1)}, u32[]{:S(2)}, u32[]{:S(2)}) collective-permute-start(bf16[192,768]{1,0:T(8,128)(2,1)S(1)} %get-tuple-element.13), channel_id=1, source_target_pairs={{0,2},{2,4},{4,6},{6,0},{1,3},{3,5},{5,7},{7,1},{8,10},{10,12},{12... | collective-permute-start | bytes 884744 | tf_op jit(solution)/shard_map/ppermute | solution.py:209
  50.2 12.2 %collective-permute-start.3 = (bf16[192,768]{1,0:T(8,128)(2,1)S(1)}, bf16[192,768]{1,0:T(8,128)(2,1)S(1)}, u32[]{:S(2)}, u32[]{:S(2)}) collective-permute-start(bf16[192,768]{1,0:T(8,128)(2,1)S(1)} %get-tuple-element.14), channel_id=1, source_target_pairs={{0,6},{2,0},{4,2},{6,4},{1,7},{3,1},{5,3},{7,5},{8,14},{10,8},{12,... | collective-permute-start | bytes 884744 | tf_op jit(solution)/shard_map/ppermute | solution.py:210
  52.1 11.7 %collective-permute-start.1 = (bf16[192,768]{1,0:T(8,128)(2,1)S(1)}, bf16[192,768]{1,0:T(8,128)(2,1)S(1)}, u32[]{:S(2)}, u32[]{:S(2)}) collective-permute-start(bf16[192,768]{1,0:T(8,128)(2,1)S(1)} %get-tuple-element.14), channel_id=1, source_target_pairs={{0,2},{2,4},{4,6},{6,0},{1,3},{3,5},{5,7},{7,1},{8,10},{10,12},{12... | collective-permute-start | bytes 884744 | tf_op jit(solution)/shard_map/ppermute | solution.py:211
  57.2 11.7 %collective-permute-start.2 = (bf16[192,768]{1,0:T(8,128)(2,1)S(1)}, bf16[192,768]{1,0:T(8,128)(2,1)S(1)}, u32[]{:S(2)}, u32[]{:S(2)}) collective-permute-start(bf16[192,768]{1,0:T(8,128)(2,1)S(1)} %get-tuple-element.13), channel_id=1, source_target_pairs={{0,6},{2,0},{4,2},{6,4},{1,7},{3,1},{5,3},{7,5},{8,14},{10,8},{12,... | collective-permute-start | bytes 884744 | tf_op jit(solution)/shard_map/ppermute | solution.py:212
  71.3 20.6 %collective-permute-start.7 = (bf16[24,8,1344]{2,1,0:T(8,128)(2,1)S(1)}, bf16[24,8,1344]{2,1,0:T(8,128)(2,1)S(1)}, u32[]{:S(2)}, u32[]{:S(2)}) collective-permute-start(bf16[24,8,1344]{2,1,0:T(8,128)(2,1)S(1)} %get-tuple-element.17), channel_id=1, source_target_pairs={{0,1},{1,0},{2,3},{3,2},{4,5},{5,4},{6,7},{7,6},{8,9},{9,8},{10,11... | collective-permute-start | bytes 1548296 | tf_op jit(solution)/shard_map/ppermute | solution.py:228
  73.2 11.3 %collective-permute-start.5 = (bf16[192,768]{1,0:T(8,128)(2,1)S(1)}, bf16[192,768]{1,0:T(8,128)(2,1)S(1)}, u32[]{:S(2)}, u32[]{:S(2)}) collective-permute-start(bf16[192,768]{1,0:T(8,128)(2,1)S(1)} %collective-permute-done.left_a), channel_id=1, source_target_pairs={{0,2},{2,4},{4,6},{6,0},{1,3},{3,5},{5,7},{7,1},{8,10},{10,12},{12... | collective-permute-start | bytes 884744 | tf_op jit(solution)/shard_map/ppermute | solution.py:213
  75.1 12.5 %collective-permute-start.6 = (bf16[192,768]{1,0:T(8,128)(2,1)S(1)}, bf16[192,768]{1,0:T(8,128)(2,1)S(1)}, u32[]{:S(2)}, u32[]{:S(2)}) collective-permute-start(bf16[192,768]{1,0:T(8,128)(2,1)S(1)} %collective-permute-done.3.right_b), channel_id=1, source_target_pairs={{0,6},{2,0},{4,2},{6,4},{1,7},{3,1},{5,3},{7,5},{8,14},{10,8},{12,... | collective-permute-start | bytes 884744 | tf_op jit(solution)/shard_map/ppermute | solution.py:214
  88.6 3.3 %collective-permute-start.8 = (bf16[8,8,1344]{2,1,0:T(8,128)(2,1)S(1)}, bf16[8,8,1344]{2,1,0:T(8,128)(2,1)S(1)}, u32[]{:S(2)}, u32[]{:S(2)}) collective-permute-start(bf16[8,8,1344]{2,1,0:T(8,128)(2,1)S(1)} %get-tuple-element.18), channel_id=1, source_target_pairs={{0,1},{1,0},{2,3},{3,2},{4,5},{5,4},{6,7},{7,6},{8,9},{9,8},{10,11... | collective-permute-start | bytes 516104 | tf_op jit(solution)/shard_map/ppermute | solution.py:232
where the time goes:
time: 140 us; the launch traced here: 139 us
  blocking collectives  46.4 us (33%)
  waiting for transfers between devices  38.3 us (27%)
  starting transfers between devices  34.6 us (25%)
  Pallas kernels  18.7 us (13%)
    all_to_all x1, blocking collectives, body(): lax.all_to_all(partial.reshape(zs, ys * rows, tile_count * width), AXES,...  28 us
    pallas_call x8, Pallas kernels, call(): pl.pallas_call(kernel, out_shape=out_shape, compiler_params=pltpu.Compile...  18.7 us
    all_to_all x1, waiting for transfers between devices, body(): received = lax.all_to_all(packed, ('x', 'core'), 0, 0)  18.5 us
    all_to_all x1, blocking collectives, body(): lax.all_to_all(summed.reshape(ys, rows, tile_count * width), AXES, 0, 0,...  18.4 us
    all_to_all x1, starting transfers between devices, body(): received = lax.all_to_all(packed, ('x', 'core'), 0, 0)  10.1 us
    ppermute x1, waiting for transfers between devices, body(): far_a = lax.ppermute(left_a, 'x', up)  5.45 us
    ppermute x1, starting transfers between devices, body(): left_b = lax.ppermute(half_b, 'x', up)  5.13 us
    ppermute x1, waiting for transfers between devices, body(): right_a = lax.ppermute(half_a, 'x', down)  5.11 us
  transfers between devices with their start and end apart: 10, of which 7 were waited for; matrix products, arithmetic and copies ran while one was open for 0% of the time, Pallas kernels for 4%

commit v1 on v0

v1 whole, which is shorter than its diff:
```python
import jax
import jax.numpy as jnp
import numpy as np
from jax import lax
from jax.experimental import pallas as pl
from jax.experimental.pallas import tpu as pltpu
from jax.sharding import Mesh
from jax.sharding import PartitionSpec as P


NB = 6
AXES = ("z", "y", "x", "core")
F32 = jnp.float32
BF16 = jnp.bfloat16
VMEM = pl.BlockSpec(memory_space=pltpu.VMEM)
ANY = pl.BlockSpec(memory_space=pl.ANY)


def tile_of(a, b):
    return a * NB - a * (a - 1) // 2 + b - a


OFF = [(a, b) for a in range(NB) for b in range(a + 1, NB)]
OFF_AT = {pair: at for at, pair in enumerate(OFF)}


def call(kernel, out_shape, args, flops, nbytes, vmem_mib, **options):
    options.setdefault("in_specs", [VMEM] * len(args))
    options.setdefault("out_specs", jax.tree.map(lambda _: VMEM, out_shape))
    return pl.pallas_call(
        kernel,
        out_shape=out_shape,
        compiler_params=pltpu.CompilerParams(vmem_limit_bytes=vmem_mib * 2**20),
        cost_estimate=pl.CostEstimate(flops=flops, bytes_accessed=nbytes, transcendentals=0),
        **options,
    )(*args)


def pack_kernel(tiles_hbm, out_hbm, tiles, out, sems):
    parts = out.shape[0]
    width = tiles.shape[3] // parts
    loads, stores = [], []
    for a in range(NB - 1):
        stored = pl.ds(tile_of(a, a + 1), NB - 1 - a)
        held = pl.ds(OFF_AT[a, a + 1], NB - 1 - a)
        loads.append(pltpu.make_async_copy(tiles_hbm.at[:, stored], tiles.at[:, held], sems.at[0, a]))
        stores.append(pltpu.make_async_copy(out.at[:, held], out_hbm.at[:, held], sems.at[1, a]))
    for load in loads:
        load.start()
    for at, (a, b) in enumerate(OFF):
        if b == a + 1:
            loads[a].wait()
        first, second = tiles[0, at], tiles[1, at]
        for d in range(parts):
            cols = slice(d * width, (d + 1) * width)
            out[d, at] = jnp.concatenate([first[:, cols], second[:, cols]], axis=1)
        if b == NB - 1:
            stores[a].start()
    for store in stores:
        store.wait()


def own_kernel(tiles, coeffs, out):
    size = tiles.shape[3]
    rows = 2 * tiles.shape[2]
    for m in range(NB):
        lhs = jnp.concatenate([tiles[:, tile_of(a, m)].reshape(rows, size) for a in range(m + 1)], axis=0)
        part = jnp.dot(lhs, coeffs[m * size : (m + 1) * size], preferred_element_type=F32)
        part = part.reshape(m + 1, rows, part.shape[1])
        if m:
            out[:m] = out[:m] + part[:m]
        out[m] = part[m]


def lower_kernel(received_hbm, coeffs_hbm, own_hbm, out, received, coeffs, own, sems):
    size = received.shape[0] * received.shape[2]
    lanes = received.shape[3]
    half = lanes // 2
    occ = coeffs.shape[1]
    loads = []
    for a in range(NB - 1):
        tiles = pl.ds(OFF_AT[a, a + 1], NB - 1 - a)
        rows = pl.ds(a * size, size)
        loads.append(
            (
                pltpu.make_async_copy(received_hbm.at[:, tiles], received.at[:, tiles], sems.at[0, a]),
                pltpu.make_async_copy(coeffs_hbm.at[rows], coeffs.at[rows], sems.at[1, a]),
            )
        )
    own_load = pltpu.make_async_copy(own_hbm, own, sems.at[0, NB - 1])
    order = list(range(NB - 1))
    for a in order:
        for load in loads[a]:
            load.start()
    own_load.start()
    sums = [None] * NB
    for a in order:
        for load in loads[a]:
            load.wait()
        lhs = jnp.concatenate(
            [received[:, OFF_AT[a, b]].reshape(size, lanes) for b in range(a + 1, NB)], axis=1
        )
        part = lax.dot_general(
            lhs, coeffs[a * size : (a + 1) * size], (((0,), (0,)), ((), ())), preferred_element_type=F32
        )
        for b in range(a + 1, NB):
            at = (b - a - 1) * lanes
            term = part[at : at + lanes]
            sums[b] = term if sums[b] is None else sums[b] + term
    own_load.wait()
    for b in range(NB):
        both = own[b] if sums[b] is None else sums[b] + own[b]
        both = both.astype(BF16)
        out[b * half : (b + 1) * half, :occ] = both[:half]
        out[b * half : (b + 1) * half, occ:] = both[half:]


def tiles_kernel(pieces, mine, sib, out_mine, out_sib):
    width = mine.shape[0] // NB
    high = out_mine.shape[1]
    groups = width // high
    for cols, out in ((mine, out_mine), (sib, out_sib)):
        right = cols[...]
        for place, piece in enumerate(pieces):
            full = lax.dot_general(
                piece[...], right, (((1,), (1,)), ((), ())), preferred_element_type=F32
            ).astype(BF16)
            for a in range(NB):
                part = full[a * width : (a + 1) * width, a * width :]
                begin = tile_of(a, a) * width
                out[place * groups : (place + 1) * groups, :, begin : begin + part.shape[1]] = part.reshape(
                    groups, high, part.shape[1]
                )


def near_kernel(own, first, second, sib, out_mine, out_sib):
    tiles_kernel((own, first, second), own, sib, out_mine, out_sib)


def far_kernel(far, own, sib, out_mine, out_sib):
    tiles_kernel((far,), own, sib, out_mine, out_sib)


def gather_kernel(near, far, near_s, far_s, out):
    cores = lax.axis_size("core")
    zs, ys = lax.axis_size("z"), lax.axis_size("y")
    x, core = lax.axis_index("x"), lax.axis_index("core")
    even = core == 0
    first, second = jnp.where(even, x ^ 1, x ^ 3), jnp.where(even, x ^ 3, x ^ 1)
    for places, source, parity in (
        ((x, first, second), near, core),
        ((x ^ 2,), far, core),
        ((x, second, first), near_s, 1 - core),
        ((x ^ 2,), far_s, 1 - core),
    ):
        for at, place in enumerate(places):
            z = place * cores + parity
            for y in range(ys):
                out[jnp.where(even, z * ys + y, y * zs + z)] = source[at * ys + y]


def sum_of(received):
    total = received[0].astype(F32)
    for k in range(1, received.shape[0]):
        total = total + received[k].astype(F32)
    return total


def sum_kernel(received, out):
    out[...] = sum_of(received)


def last_kernel(received, out):
    total = sum_of(received)
    width = out.shape[2]
    for t in range(out.shape[0]):
        out[t] = total[:, t * width : (t + 1) * width]


def body(integrals, orbitals):
    slabs, tile_count, width, size = integrals.shape
    occ = orbitals.shape[1]
    xs, cores, zs, ys = (lax.axis_size(name) for name in ("x", "core", "z", "y"))
    parts = xs * cores
    rows = size // (zs * ys)
    flops = 2 * slabs * width * size * occ

    packed = call(
        pack_kernel,
        jax.ShapeDtypeStruct((parts, len(OFF), width, slabs * width), BF16),
        (integrals,),
        0,
        2 * integrals.size * 2,
        63,
        in_specs=[ANY],
        out_specs=ANY,
        scratch_shapes=[
            pltpu.VMEM((slabs, len(OFF), width, size), BF16),
            pltpu.VMEM((parts, len(OFF), width, slabs * width), BF16),
            pltpu.SemaphoreType.DMA((2, NB - 1)),
        ],
    )
    received = lax.all_to_all(packed, ("x", "core"), 0, 0)
    own = call(
        own_kernel,
        jax.ShapeDtypeStruct((NB, slabs * width, occ), F32),
        (integrals, orbitals),
        flops * tile_count,
        2 * integrals.size + 2 * orbitals.size,
        63,
    )
    half = call(
        lower_kernel,
        jax.ShapeDtypeStruct((NB * width, slabs * occ), BF16),
        (received, orbitals, own),
        flops * len(OFF),
        2 * received.size + 2 * orbitals.size,
        63,
        in_specs=[ANY] * 3,
        scratch_shapes=[
            pltpu.VMEM(received.shape, BF16),
            pltpu.VMEM(orbitals.shape, BF16),
            pltpu.VMEM(own.shape, F32),
            pltpu.SemaphoreType.DMA((2, NB)),
        ],
    )

    def exchange(array, turn):
        pairs = [((x, c), (x ^ (3 if (c + turn) % 2 else 1), c)) for x in range(xs) for c in range(cores)]
        return lax.ppermute(array, ("x", "core"), [(a * cores + c, b * cores + d) for (a, c), (b, d) in pairs])

    swap = [(i, (i + 1) % cores) for i in range(cores)]
    first = exchange(half, 0)
    second = exchange(half, 1)
    sib = lax.ppermute(half, "core", swap)
    far = exchange(first, 1)

    product = 2 * half.shape[0] ** 2 * half.shape[1]
    near_shape = jax.ShapeDtypeStruct((3 * ys, rows, tile_count * width), BF16)
    far_shape = jax.ShapeDtypeStruct((ys, rows, tile_count * width), BF16)
    near, near_s = call(
        near_kernel,
        (near_shape, near_shape),
        (half, first, second, sib),
        6 * product,
        8 * half.size,
        16,
    )
    near_s = lax.ppermute(near_s, "core", swap)
    far, far_s = call(far_kernel, (far_shape, far_shape), (far, half, sib), 2 * product, 6 * half.size, 12)
    far_s = lax.ppermute(far_s, "core", swap)
    partial = call(
        gather_kernel,
        jax.ShapeDtypeStruct((zs * ys, rows, tile_count * width), BF16),
        (near, far, near_s, far_s),
        0,
        8 * near.size,
        12,
    )

    at = np.arange(zs * ys * parts).reshape(zs, ys, xs, cores)
    along_z = [[at[:, y, x, c].tolist() for x in range(xs) for y in range(ys)] for c in range(2)]
    along_y = [[at[z, :, x, c].tolist() for x in range(xs) for z in range(zs)] for c in range(2)]
    arrived = lax.all_to_all(
        partial.reshape(zs, ys * rows, tile_count * width), AXES, 0, 0, axis_index_groups=along_z[0] + along_y[1]
    )
    summed = call(
        sum_kernel,
        jax.ShapeDtypeStruct(arrived.shape[1:], F32),
        (arrived,),
        arrived.size,
        2 * arrived.size,
        8,
    )
    arrived = lax.all_to_all(
        summed.reshape(ys, rows, tile_count * width), AXES, 0, 0, axis_index_groups=along_y[0] + along_z[1]
    )
    tiles = call(
        last_kernel,
        jax.ShapeDtypeStruct((tile_count, rows, width), F32),
        (arrived,),
        arrived.size,
        4 * arrived.size,
        8,
    )
    return jnp.transpose(tiles, (1, 0, 2))


def solution(mesh):
    grid = Mesh(mesh.devices.reshape(8, 8, 4, 2), AXES)
    return jax.shard_map(
        body,
        mesh=grid,
        in_specs=(P(("z", "y"), None, ("x", "core"), None), P()),
        out_specs=P(("z", "y"), None, ("x", "core")),
        check_vma=False,
    )
```

time: 140 us -> 121 us (0.86)
  the two profiles are of different devices: /device:TPU:6 before, /device:TPU:8 now
where the time goes in v1:
time: 121 us; the launch traced here: 120 us
  blocking collectives  50.7 us (42%)
  waiting for transfers between devices  33.2 us (27%)
  starting transfers between devices  19.3 us (16%)
  Pallas kernels  16 us (13%)
    all_to_all x1, blocking collectives, body(): lax.all_to_all(partial.reshape(zs, ys * rows, tile_count * width), AXES,...  33.2 us
    all_to_all x1, waiting for transfers between devices, body(): received = lax.all_to_all(packed, ('x', 'core'), 0, 0)  20.7 us
    all_to_all x1, blocking collectives, body(): lax.all_to_all(summed.reshape(ys, rows, tile_count * width), AXES, 0, 0,...  17.4 us
    pallas_call x8, Pallas kernels, call(): pl.pallas_call(kernel, out_shape=out_shape, compiler_params=pltpu.Compile...  16 us
    ppermute x3, waiting for transfers between devices, exchange(): lax.ppermute(array, ('x', 'core'), [(a * cores + c, b * cores + d) for (a...  11.1 us
    ppermute x3, starting transfers between devices, exchange(): lax.ppermute(array, ('x', 'core'), [(a * cores + c, b * cores + d) for (a...  9.1 us
    all_to_all x1, starting transfers between devices, body(): received = lax.all_to_all(packed, ('x', 'core'), 0, 0)  4.34 us
  transfers between devices with their start and end apart: 7, of which 5 were waited for; matrix products, arithmetic and copies ran while one was open for 0% of the time, Pallas kernels for 7%

profile of v1, /device:TPU:8, one launch (start us, length us, event | category | flops | bytes accessed | tf_op | source)
XLA Modules:
  0.0 120.4 jit_solution(15693307770631297739)
XLA Ops:
  0.0 2.7 %shard_map.28 = bf16[8,15,64,128]{3,2,1,0:T(8,128)(2,1)} custom-call(bf16[2,21,64,512]{3,2,1,0:T(8,128)(2,1)} %tiles.1), custom_call_target="tpu_custom_call" | custom-call | bytes 5505024 | tf_op jit(solution)/shard_map/pallas_call | solution.py:30
  2.7 4.3 %all-to-all-start = ((bf16[8,15,64,128]{3,2,1,0:T(8,128)(2,1)}), bf16[8,15,64,128]{3,2,1,0:T(8,128)(2,1)}, u32[]{:S(2)}, u32[]{:S(2)}) async-start(bf16[8,15,64,128]{3,2,1,0:T(8,128)(2,1)} %shard_map.28), calls=%async_computation | async-start | bytes 3932160 | tf_op jit(solution)/shard_map/all_to_all | solution.py:203
  7.1 5.1 %shard_map.29.own_hbm = f32[6,128,384]{2,1,0:T(8,128)} custom-call(bf16[2,21,64,512]{3,2,1,0:T(8,128)(2,1)} %tiles.1, bf16[3072,384]{1,0:T(8,128)(2,1)} %coeffs_hbm.1), custom_call_target="tpu_custom_call" | custom-call | flops 1056964608 | bytes 5111808 | tf_op jit(solution)/shard_map/pallas_call | solution.py:30
  12.2 20.7 %all-to-all-done.received_hbm = bf16[8,15,64,128]{3,2,1,0:T(8,128)(2,1)} async-done(((bf16[8,15,64,128]{3,2,1,0:T(8,128)(2,1)}), bf16[8,15,64,128]{3,2,1,0:T(8,128)(2,1)}, u32[]{:S(2)}, u32[]{:S(2)}) %all-to-all-start) | async-done | bytes 1966112 | tf_op jit(solution)/shard_map/all_to_all | solution.py:203
  32.9 4.2 %shard_map.30.own = bf16[384,768]{1,0:T(8,128)(2,1)} custom-call(bf16[8,15,64,128]{3,2,1,0:T(8,128)(2,1)} %all-to-all-done.received_hbm, bf16[3072,384]{1,0:T(8,128)(2,1)} %coeffs_hbm.1, f32[6,128,384]{2,1,0:T(8,128)} %shard_map.29.own_hbm), custom_call_target="tpu_custom_call" | custom-call | flops 754974720 | bytes 4325376 | tf_op jit(solution)/shard_map/pallas_call | solution.py:30
  37.1 2.5 %collective-permute-start = (bf16[384,768]{1,0:T(8,128)(2,1)}, bf16[384,768]{1,0:T(8,128)(2,1)S(1)}, u32[]{:S(2)}, u32[]{:S(2)}) collective-permute-start(bf16[384,768]{1,0:T(8,128)(2,1)} %shard_map.30.own), channel_id=1, source_target_pairs={{0,2},{1,7},{2,0},{3,5},{4,6},{5,3},{6,4},{7,1},{8,10},{9,15},{10,... | collective-permute-start | bytes 1769480 | tf_op jit(solution)/shard_map/ppermute | solution.py:230
  39.6 1.9 %collective-permute-start.2 = (bf16[384,768]{1,0:T(8,128)(2,1)}, bf16[384,768]{1,0:T(8,128)(2,1)S(1)}, u32[]{:S(2)}, u32[]{:S(2)}) collective-permute-start(bf16[384,768]{1,0:T(8,128)(2,1)} %shard_map.30.own), channel_id=1, source_target_pairs={{0,1},{1,0},{2,3},{3,2},{4,5},{5,4},{6,7},{7,6},{8,9},{9,8},{10,11... | collective-permute-start | bytes 1769480 | tf_op jit(solution)/shard_map/ppermute | solution.py:235
  41.5 3.8 %collective-permute-start.1 = (bf16[384,768]{1,0:T(8,128)(2,1)}, bf16[384,768]{1,0:T(8,128)(2,1)S(1)}, u32[]{:S(2)}, u32[]{:S(2)}) collective-permute-start(bf16[384,768]{1,0:T(8,128)(2,1)} %shard_map.30.own), channel_id=1, source_target_pairs={{0,6},{1,3},{2,4},{3,1},{4,2},{5,7},{6,0},{7,5},{8,14},{9,11},{10,... | collective-permute-start | bytes 1769480 | tf_op jit(solution)/shard_map/ppermute | solution.py:230
  45.3 6.1 %collective-permute-done.first = bf16[384,768]{1,0:T(8,128)(2,1)S(1)} collective-permute-done((bf16[384,768]{1,0:T(8,128)(2,1)}, bf16[384,768]{1,0:T(8,128)(2,1)S(1)}, u32[]{:S(2)}, u32[]{:S(2)}) %collective-permute-start) | collective-permute-done | bytes 589856 | tf_op jit(solution)/shard_map/ppermute | solution.py:230
  51.5 2.8 %collective-permute-start.3 = (bf16[384,768]{1,0:T(8,128)(2,1)S(1)}, bf16[384,768]{1,0:T(8,128)(2,1)S(1)}, u32[]{:S(2)}, u32[]{:S(2)}) collective-permute-start(bf16[384,768]{1,0:T(8,128)(2,1)S(1)} %collective-permute-done.first), channel_id=1, source_target_pairs={{0,6},{1,3},{2,4},{3,1},{4,2},{5,7},{6,0},{7,5},{8,14},{9,11},{10,... | collective-permute-start | bytes 1769480 | tf_op jit(solution)/shard_map/ppermute | solution.py:230
  54.3 0.0 collective-permute-done.2.sib
  54.3 0.9 collective-permute-done.1.second
  55.2 0.0 copy-start
  55.2 1.1 copy-done
  56.3 2.1 %shard_map.31 = (bf16[24,8,1344]{2,1,0:T(8,128)(2,1)S(1)}, bf16[24,8,1344]{2,1,0:T(8,128)(2,1)S(1)}) custom-call(bf16[384,768]{1,0:T(8,128)(2,1)S(1)} %copy-done, bf16[384,768]{1,0:T(8,128)(2,1)S(1)} %collective-permute-done.first, bf16[384,768]{1,0:T(8,128)(2,1)S(1)} %collective-permute-done.1.second, bf16[384,768]{1,0:T(8,128)(2,1)S(1)} %collective-permute-done.2.sib), custom_call_target="tpu_custom_call" | custom-call | flops 1358954496 | bytes 2359296 | tf_op jit(solution)/shard_map/pallas_call | solution.py:30
  58.3 2.0 %collective-permute-start.4 = (bf16[24,8,1344]{2,1,0:T(8,128)(2,1)S(1)}, bf16[24,8,1344]{2,1,0:T(8,128)(2,1)S(1)}, u32[]{:S(2)}, u32[]{:S(2)}) collective-permute-start(bf16[24,8,1344]{2,1,0:T(8,128)(2,1)S(1)} %get-tuple-element.11), channel_id=1, source_target_pairs={{0,1},{1,0},{2,3},{3,2},{4,5},{5,4},{6,7},{7,6},{8,9},{9,8},{10,11... | collective-permute-start | bytes 1548296 | tf_op jit(solution)/shard_map/ppermute | solution.py:249
  60.4 4.1 %collective-permute-done.3.far = bf16[384,768]{1,0:T(8,128)(2,1)S(1)} collective-permute-done((bf16[384,768]{1,0:T(8,128)(2,1)S(1)}, bf16[384,768]{1,0:T(8,128)(2,1)S(1)}, u32[]{:S(2)}, u32[]{:S(2)}) %collective-permute-start.3) | collective-permute-done | bytes 589856 | tf_op jit(solution)/shard_map/ppermute | solution.py:230
  64.5 0.8 shard_map.32
  65.3 1.9 %collective-permute-start.5 = (bf16[8,8,1344]{2,1,0:T(8,128)(2,1)S(1)}, bf16[8,8,1344]{2,1,0:T(8,128)(2,1)S(1)}, u32[]{:S(2)}, u32[]{:S(2)}) collective-permute-start(bf16[8,8,1344]{2,1,0:T(8,128)(2,1)S(1)} %get-tuple-element.12), channel_id=1, source_target_pairs={{0,1},{1,0},{2,3},{3,2},{4,5},{5,4},{6,7},{7,6},{8,9},{9,8},{10,11... | collective-permute-start | bytes 516104 | tf_op jit(solution)/shard_map/ppermute | solution.py:251
  67.2 0.0 collective-permute-done.4.near_s
  67.2 1.4 %collective-permute-done.5.far_s = bf16[8,8,1344]{2,1,0:T(8,128)(2,1)S(1)} collective-permute-done((bf16[8,8,1344]{2,1,0:T(8,128)(2,1)S(1)}, bf16[8,8,1344]{2,1,0:T(8,128)(2,1)S(1)}, u32[]{:S(2)}, u32[]{:S(2)}) %collective-permute-start.5) | collective-permute-done | bytes 172064 | tf_op jit(solution)/shard_map/ppermute | solution.py:251
  68.6 0.2 shard_map.33
  68.8 33.2 %all_to_all.15.received = bf16[8,64,1344]{2,1,0:T(8,128)(2,1)S(1)} all-to-all(bf16[8,64,1344]{2,1,0:T(8,128)(2,1)S(1)} %bitcast.3), channel_id=1, replica_groups={{0,64,128,192,256,320,384,448},{8,72,136,200,264,328,392,456},{16,80,14..., dimensions={0} | all-to-all | bytes 2752512 | tf_op jit(solution)/shard_map/all_to_all | solution.py:264
  102.0 0.2 shard_map.34
  102.2 17.4 %all_to_all.16.received = f32[8,8,1344]{2,1,0:T(8,128)S(1)} all-to-all(f32[8,8,1344]{2,1,0:T(8,128)S(1)} %bitcast.4), channel_id=1, replica_groups={{0,8,16,24,32,40,48,56},{64,72,80,88,96,104,112,120},{128,136,144,152,1..., dimensions={0} | all-to-all | bytes 688128 | tf_op jit(solution)/shard_map/all_to_all | solution.py:275
  119.6 0.7 shard_map.35
Async XLA Ops:
  2.7 30.2 %all-to-all-start = ((bf16[8,15,64,128]{3,2,1,0:T(8,128)(2,1)}), bf16[8,15,64,128]{3,2,1,0:T(8,128)(2,1)}, u32[]{:S(2)}, u32[]{:S(2)}) async-start(bf16[8,15,64,128]{3,2,1,0:T(8,128)(2,1)} %shard_map.28), calls=%async_computation | async-start | bytes 3932160 | tf_op jit(solution)/shard_map/all_to_all | solution.py:203
  37.1 14.4 %collective-permute-start = (bf16[384,768]{1,0:T(8,128)(2,1)}, bf16[384,768]{1,0:T(8,128)(2,1)S(1)}, u32[]{:S(2)}, u32[]{:S(2)}) collective-permute-start(bf16[384,768]{1,0:T(8,128)(2,1)} %shard_map.30.own), channel_id=1, source_target_pairs={{0,2},{1,7},{2,0},{3,5},{4,6},{5,3},{6,4},{7,1},{8,10},{9,15},{10,... | collective-permute-start | bytes 1769480 | tf_op jit(solution)/shard_map/ppermute | solution.py:230
  39.6 14.7 %collective-permute-start.2 = (bf16[384,768]{1,0:T(8,128)(2,1)}, bf16[384,768]{1,0:T(8,128)(2,1)S(1)}, u32[]{:S(2)}, u32[]{:S(2)}) collective-permute-start(bf16[384,768]{1,0:T(8,128)(2,1)} %shard_map.30.own), channel_id=1, source_target_pairs={{0,1},{1,0},{2,3},{3,2},{4,5},{5,4},{6,7},{7,6},{8,9},{9,8},{10,11... | collective-permute-start | bytes 1769480 | tf_op jit(solution)/shard_map/ppermute | solution.py:235
  41.5 13.7 %collective-permute-start.1 = (bf16[384,768]{1,0:T(8,128)(2,1)}, bf16[384,768]{1,0:T(8,128)(2,1)S(1)}, u32[]{:S(2)}, u32[]{:S(2)}) collective-permute-start(bf16[384,768]{1,0:T(8,128)(2,1)} %shard_map.30.own), channel_id=1, source_target_pairs={{0,6},{1,3},{2,4},{3,1},{4,2},{5,7},{6,0},{7,5},{8,14},{9,11},{10,... | collective-permute-start | bytes 1769480 | tf_op jit(solution)/shard_map/ppermute | solution.py:230
  51.5 13.0 %collective-permute-start.3 = (bf16[384,768]{1,0:T(8,128)(2,1)S(1)}, bf16[384,768]{1,0:T(8,128)(2,1)S(1)}, u32[]{:S(2)}, u32[]{:S(2)}) collective-permute-start(bf16[384,768]{1,0:T(8,128)(2,1)S(1)} %collective-permute-done.first), channel_id=1, source_target_pairs={{0,6},{1,3},{2,4},{3,1},{4,2},{5,7},{6,0},{7,5},{8,14},{9,11},{10,... | collective-permute-start | bytes 1769480 | tf_op jit(solution)/shard_map/ppermute | solution.py:230
  55.2 1.1 copy-start
  58.3 8.9 %collective-permute-start.4 = (bf16[24,8,1344]{2,1,0:T(8,128)(2,1)S(1)}, bf16[24,8,1344]{2,1,0:T(8,128)(2,1)S(1)}, u32[]{:S(2)}, u32[]{:S(2)}) collective-permute-start(bf16[24,8,1344]{2,1,0:T(8,128)(2,1)S(1)} %get-tuple-element.11), channel_id=1, source_target_pairs={{0,1},{1,0},{2,3},{3,2},{4,5},{5,4},{6,7},{7,6},{8,9},{9,8},{10,11... | collective-permute-start | bytes 1548296 | tf_op jit(solution)/shard_map/ppermute | solution.py:249
  65.3 3.3 %collective-permute-start.5 = (bf16[8,8,1344]{2,1,0:T(8,128)(2,1)S(1)}, bf16[8,8,1344]{2,1,0:T(8,128)(2,1)S(1)}, u32[]{:S(2)}, u32[]{:S(2)}) collective-permute-start(bf16[8,8,1344]{2,1,0:T(8,128)(2,1)S(1)} %get-tuple-element.12), channel_id=1, source_target_pairs={{0,1},{1,0},{2,3},{3,2},{4,5},{5,4},{6,7},{7,6},{8,9},{9,8},{10,11... | collective-permute-start | bytes 516104 | tf_op jit(solution)/shard_map/ppermute | solution.py:251

commit v2 on v1

--- a/solution.py
+++ b/solution.py
@@ -72,7 +72,7 @@
         out[m] = part[m]
 
 
-def lower_kernel(received_hbm, coeffs_hbm, own_hbm, out, received, coeffs, own, sems):
+def lower_kernel(received_hbm, coeffs_hbm, own_hbm, out, out_a, out_b, received, coeffs, own, sems):
     size = received.shape[0] * received.shape[2]
     lanes = received.shape[3]
     half = lanes // 2
@@ -87,16 +87,16 @@
                 pltpu.make_async_copy(coeffs_hbm.at[rows], coeffs.at[rows], sems.at[1, a]),
             )
         )
-    own_load = pltpu.make_async_copy(own_hbm, own, sems.at[0, NB - 1])
-    order = list(range(NB - 1))
-    for a in order:
-        for load in loads[a]:
-            load.start()
-    own_load.start()
+    loads.append((pltpu.make_async_copy(own_hbm, own, sems.at[0, NB - 1]),))
+    for load in loads[0] + loads[1]:
+        load.start()
     sums = [None] * NB
-    for a in order:
+    for a in range(NB - 1):
         for load in loads[a]:
             load.wait()
+        if a + 2 < NB:
+            for load in loads[a + 2]:
+                load.start()
         lhs = jnp.concatenate(
             [received[:, OFF_AT[a, b]].reshape(size, lanes) for b in range(a + 1, NB)], axis=1
         )
@@ -107,12 +107,13 @@
             at = (b - a - 1) * lanes
             term = part[at : at + lanes]
             sums[b] = term if sums[b] is None else sums[b] + term
-    own_load.wait()
+    loads[NB - 1][0].wait()
     for b in range(NB):
         both = own[b] if sums[b] is None else sums[b] + own[b]
         both = both.astype(BF16)
-        out[b * half : (b + 1) * half, :occ] = both[:half]
-        out[b * half : (b + 1) * half, occ:] = both[half:]
+        for ref, at in ((out, b), (out_a if b < NB // 2 else out_b, b % (NB // 2))):
+            ref[at * half : (at + 1) * half, :occ] = both[:half]
+            ref[at * half : (at + 1) * half, occ:] = both[half:]
 
 
 def tiles_kernel(pieces, mine, sib, out_mine, out_sib):
@@ -122,23 +123,26 @@
     for cols, out in ((mine, out_mine), (sib, out_sib)):
         right = cols[...]
         for place, piece in enumerate(pieces):
-            full = lax.dot_general(
-                piece[...], right, (((1,), (1,)), ((), ())), preferred_element_type=F32
-            ).astype(BF16)
-            for a in range(NB):
-                part = full[a * width : (a + 1) * width, a * width :]
-                begin = tile_of(a, a) * width
-                out[place * groups : (place + 1) * groups, :, begin : begin + part.shape[1]] = part.reshape(
-                    groups, high, part.shape[1]
-                )
-
-
-def near_kernel(own, first, second, sib, out_mine, out_sib):
-    tiles_kernel((own, first, second), own, sib, out_mine, out_sib)
-
-
-def far_kernel(far, own, sib, out_mine, out_sib):
-    tiles_kernel((far,), own, sib, out_mine, out_sib)
+            a = 0
+            for part in piece:
+                full = lax.dot_general(
+                    part[...], right, (((1,), (1,)), ((), ())), preferred_element_type=F32
+                ).astype(BF16)
+                for k in range(part.shape[0] // width):
+                    strip = full[k * width : (k + 1) * width, a * width :]
+                    begin = tile_of(a, a) * width
+                    out[place * groups : (place + 1) * groups, :, begin : begin + strip.shape[1]] = strip.reshape(
+                        groups, high, strip.shape[1]
+                    )
+                    a += 1
+
+
+def near_kernel(own, first_a, first_b, second, sib, out_mine, out_sib):
+    tiles_kernel(((own,), (first_a, first_b), (second,)), own, sib, out_mine, out_sib)
+
+
+def far_kernel(far_a, far_b, own, sib, out_mine, out_sib):
+    tiles_kernel(((far_a, far_b),), own, sib, out_mine, out_sib)
 
 
 def gather_kernel(near, far, near_s, far_s, out):
@@ -209,13 +213,16 @@
         2 * integrals.size + 2 * orbitals.size,
         63,
     )
-    half = call(
+    whole = jax.ShapeDtypeStruct((NB * width, slabs * occ), BF16)
+    side = jax.ShapeDtypeStruct((NB // 2 * width, slabs * occ), BF16)
+    in_hbm = lambda array: pltpu.with_memory_space_constraint(array, pltpu.HBM)
+    half, half_a, half_b = call(
         lower_kernel,
-        jax.ShapeDtypeStruct((NB * width, slabs * occ), BF16),
-        (received, orbitals, own),
+        (whole, side, side),
+        (in_hbm(received), in_hbm(orbitals), in_hbm(own)),
         flops * len(OFF),
         2 * received.size + 2 * orbitals.size,
-        63,
+        20,
         in_specs=[ANY] * 3,
         scratch_shapes=[
             pltpu.VMEM(received.shape, BF16),
@@ -230,10 +237,12 @@
         return lax.ppermute(array, ("x", "core"), [(a * cores + c, b * cores + d) for (a, c), (b, d) in pairs])
 
     swap = [(i, (i + 1) % cores) for i in range(cores)]
-    first = exchange(half, 0)
+    first_a = exchange(half_a, 0)
+    first_b = exchange(half_b, 0)
     second = exchange(half, 1)
+    far_a = exchange(first_a, 1)
     sib = lax.ppermute(half, "core", swap)
-    far = exchange(first, 1)
+    far_b = exchange(first_b, 1)
 
     product = 2 * half.shape[0] ** 2 * half.shape[1]
     near_shape = jax.ShapeDtypeStruct((3 * ys, rows, tile_count * width), BF16)
@@ -241,13 +250,13 @@
     near, near_s = call(
         near_kernel,
         (near_shape, near_shape),
-        (half, first, second, sib),
+        (half, first_a, first_b, second, sib),
         6 * product,
         8 * half.size,
         16,
     )
     near_s = lax.ppermute(near_s, "core", swap)
-    far, far_s = call(far_kernel, (far_shape, far_shape), (far, half, sib), 2 * product, 6 * half.size, 12)
+    far, far_s = call(far_kernel, (far_shape, far_shape), (far_a, far_b, half, sib), 2 * product, 6 * half.size, 12)
     far_s = lax.ppermute(far_s, "core", swap)
     partial = call(
         gather_kernel,

time: 121 us -> 132 us (1.091)
  the two profiles are of different devices: /device:TPU:8 before, /device:TPU:6 now
where the time goes in v2:
time: 132 us
  blocking collectives  46.4 us (35%)
  waiting for transfers between devices  34.8 us (26%)
  starting transfers between devices  34 us (26%)
  Pallas kernels  16.4 us (12%)
    all_to_all x1, blocking collectives, body(): lax.all_to_all(partial.reshape(zs, ys * rows, tile_count * width), AXES,...  27.9 us
    all_to_all x1, waiting for transfers between devices, body(): received = lax.all_to_all(packed, ('x', 'core'), 0, 0)  18.7 us
    all_to_all x1, blocking collectives, body(): lax.all_to_all(summed.reshape(ys, rows, tile_count * width), AXES, 0, 0,...  18.4 us
    ppermute x5, starting transfers between devices, exchange(): lax.ppermute(array, ('x', 'core'), [(a * cores + c, b * cores + d) for (a...  16.9 us
    pallas_call x8, Pallas kernels, call(): pl.pallas_call(kernel, out_shape=out_shape, compiler_params=pltpu.Compile...  16.4 us
    ppermute x5, waiting for transfers between devices, exchange(): lax.ppermute(array, ('x', 'core'), [(a * cores + c, b * cores + d) for (a...  14.7 us
    all_to_all x1, starting transfers between devices, body(): received = lax.all_to_all(packed, ('x', 'core'), 0, 0)  10.1 us
    ppermute x1, starting transfers between devices, body(): near_s = lax.ppermute(near_s, 'core', swap)  3.19 us
  transfers between devices with their start and end apart: 9, of which 7 were waited for; matrix products, arithmetic and copies ran while one was open for 0% of the time, Pallas kernels for 5%

profile of v2, /device:TPU:6, one launch (start us, length us, event | category | flops | bytes accessed | tf_op | source)
XLA Modules:
  0.0 131.7 jit_solution(9731494599636539528)
XLA Ops:
  0.0 2.7 %shard_map.28 = bf16[8,15,64,128]{3,2,1,0:T(8,128)(2,1)} custom-call(bf16[2,21,64,512]{3,2,1,0:T(8,128)(2,1)} %tiles.1), custom_call_target="tpu_custom_call" | custom-call | bytes 5505024 | tf_op jit(solution)/shard_map/pallas_call | solution.py:30
  2.7 10.1 %all-to-all-start = ((bf16[8,15,64,128]{3,2,1,0:T(8,128)(2,1)}), bf16[8,15,64,128]{3,2,1,0:T(8,128)(2,1)}, u32[]{:S(2)}, u32[]{:S(2)}) async-start(bf16[8,15,64,128]{3,2,1,0:T(8,128)(2,1)} %shard_map.28), calls=%async_computation | async-start | bytes 3932160 | tf_op jit(solution)/shard_map/all_to_all | solution.py:207
  12.8 5.1 %shard_map.29.own_hbm = f32[6,128,384]{2,1,0:T(8,128)} custom-call(bf16[2,21,64,512]{3,2,1,0:T(8,128)(2,1)} %tiles.1, bf16[3072,384]{1,0:T(8,128)(2,1)} %coeffs_hbm.1), custom_call_target="tpu_custom_call" | custom-call | flops 1056964608 | bytes 5111808 | tf_op jit(solution)/shard_map/pallas_call | solution.py:30
  17.9 18.7 %all-to-all-done.received_hbm = bf16[8,15,64,128]{3,2,1,0:T(8,128)(2,1)} async-done(((bf16[8,15,64,128]{3,2,1,0:T(8,128)(2,1)}), bf16[8,15,64,128]{3,2,1,0:T(8,128)(2,1)}, u32[]{:S(2)}, u32[]{:S(2)}) %all-to-all-start) | async-done | bytes 1966112 | tf_op jit(solution)/shard_map/all_to_all | solution.py:207
  36.6 4.4 %shard_map.30 = (bf16[384,768]{1,0:T(8,128)(2,1)S(1)}, bf16[192,768]{1,0:T(8,128)(2,1)S(1)}, bf16[192,768]{1,0:T(8,128)(2,1)S(1)}) custom-call(bf16[8,15,64,128]{3,2,1,0:T(8,128)(2,1)} %all-to-all-done.received_hbm, bf16[3072,384]{1,0:T(8,128)(2,1)} %coeffs_hbm.1, f32[6,128,384]{2,1,0:T(8,128)} %shard_map.29.own_hbm), custom_call_target="tpu_custom_call" | custom-call | flops 754974720 | bytes 4325376 | tf_op jit(solution)/shard_map/pallas_call | solution.py:30
  41.0 1.9 %collective-permute-start.3 = (bf16[384,768]{1,0:T(8,128)(2,1)S(1)}, bf16[384,768]{1,0:T(8,128)(2,1)S(1)}, u32[]{:S(2)}, u32[]{:S(2)}) collective-permute-start(bf16[384,768]{1,0:T(8,128)(2,1)S(1)} %get-tuple-element.12.own), channel_id=1, source_target_pairs={{0,1},{1,0},{2,3},{3,2},{4,5},{5,4},{6,7},{7,6},{8,9},{9,8},{10,11... | collective-permute-start | bytes 1769480 | tf_op jit(solution)/shard_map/ppermute | solution.py:244
  42.9 4.0 %collective-permute-start.2 = (bf16[384,768]{1,0:T(8,128)(2,1)S(1)}, bf16[384,768]{1,0:T(8,128)(2,1)S(1)}, u32[]{:S(2)}, u32[]{:S(2)}) collective-permute-start(bf16[384,768]{1,0:T(8,128)(2,1)S(1)} %get-tuple-element.12.own), channel_id=1, source_target_pairs={{0,6},{1,3},{2,4},{3,1},{4,2},{5,7},{6,0},{7,5},{8,14},{9,11},{10,... | collective-permute-start | bytes 1769480 | tf_op jit(solution)/shard_map/ppermute | solution.py:237
  46.9 1.9 %collective-permute-start = (bf16[192,768]{1,0:T(8,128)(2,1)S(1)}, bf16[192,768]{1,0:T(8,128)(2,1)S(1)}, u32[]{:S(2)}, u32[]{:S(2)}) collective-permute-start(bf16[192,768]{1,0:T(8,128)(2,1)S(1)} %get-tuple-element.13), channel_id=1, source_target_pairs={{0,2},{1,7},{2,0},{3,5},{4,6},{5,3},{6,4},{7,1},{8,10},{9,15},{10,... | collective-permute-start | bytes 884744 | tf_op jit(solution)/shard_map/ppermute | solution.py:237
  48.8 3.9 %collective-permute-start.1 = (bf16[192,768]{1,0:T(8,128)(2,1)S(1)}, bf16[192,768]{1,0:T(8,128)(2,1)S(1)}, u32[]{:S(2)}, u32[]{:S(2)}) collective-permute-start(bf16[192,768]{1,0:T(8,128)(2,1)S(1)} %get-tuple-element.14), channel_id=1, source_target_pairs={{0,2},{1,7},{2,0},{3,5},{4,6},{5,3},{6,4},{7,1},{8,10},{9,15},{10,... | collective-permute-start | bytes 884744 | tf_op jit(solution)/shard_map/ppermute | solution.py:237
  52.8 4.6 %collective-permute-done.first_a = bf16[192,768]{1,0:T(8,128)(2,1)S(1)} collective-permute-done((bf16[192,768]{1,0:T(8,128)(2,1)S(1)}, bf16[192,768]{1,0:T(8,128)(2,1)S(1)}, u32[]{:S(2)}, u32[]{:S(2)}) %collective-permute-start) | collective-permute-done | bytes 294944 | tf_op jit(solution)/shard_map/ppermute | solution.py:237
  57.4 3.2 %collective-permute-done.1.first_b = bf16[192,768]{1,0:T(8,128)(2,1)S(1)} collective-permute-done((bf16[192,768]{1,0:T(8,128)(2,1)S(1)}, bf16[192,768]{1,0:T(8,128)(2,1)S(1)}, u32[]{:S(2)}, u32[]{:S(2)}) %collective-permute-start.1) | collective-permute-done | bytes 294944 | tf_op jit(solution)/shard_map/ppermute | solution.py:237
  60.5 0.0 collective-permute-done.3.sib
  60.5 0.2 collective-permute-done.2.second
  60.7 2.2 %shard_map.31 = (bf16[24,8,1344]{2,1,0:T(8,128)(2,1)S(1)}, bf16[24,8,1344]{2,1,0:T(8,128)(2,1)S(1)}) custom-call(bf16[384,768]{1,0:T(8,128)(2,1)S(1)} %get-tuple-element.12.own, bf16[192,768]{1,0:T(8,128)(2,1)S(1)} %collective-permute-done.first_a, bf16[192,768]{1,0:T(8,128)(2,1)S(1)} %collective-permute-done.1.first_b, ...), custom_call_target="tpu_custom_call" | custom-call | flops 1358954496 | bytes 2359296 | tf_op jit(solution)/shard_map/pallas_call | solution.py:30
  62.9 3.2 %collective-permute-start.6 = (bf16[24,8,1344]{2,1,0:T(8,128)(2,1)S(1)}, bf16[24,8,1344]{2,1,0:T(8,128)(2,1)S(1)}, u32[]{:S(2)}, u32[]{:S(2)}) collective-permute-start(bf16[24,8,1344]{2,1,0:T(8,128)(2,1)S(1)} %get-tuple-element.17), channel_id=1, source_target_pairs={{0,1},{1,0},{2,3},{3,2},{4,5},{5,4},{6,7},{7,6},{8,9},{9,8},{10,11... | collective-permute-start | bytes 1548296 | tf_op jit(solution)/shard_map/ppermute | solution.py:258
  66.1 4.0 %collective-permute-start.4 = (bf16[192,768]{1,0:T(8,128)(2,1)S(1)}, bf16[192,768]{1,0:T(8,128)(2,1)S(1)}, u32[]{:S(2)}, u32[]{:S(2)}) collective-permute-start(bf16[192,768]{1,0:T(8,128)(2,1)S(1)} %collective-permute-done.first_a), channel_id=1, source_target_pairs={{0,6},{1,3},{2,4},{3,1},{4,2},{5,7},{6,0},{7,5},{8,14},{9,11},{10,... | collective-permute-start | bytes 884744 | tf_op jit(solution)/shard_map/ppermute | solution.py:237
  70.1 3.1 %collective-permute-start.5 = (bf16[192,768]{1,0:T(8,128)(2,1)S(1)}, bf16[192,768]{1,0:T(8,128)(2,1)S(1)}, u32[]{:S(2)}, u32[]{:S(2)}) collective-permute-start(bf16[192,768]{1,0:T(8,128)(2,1)S(1)} %collective-permute-done.1.first_b), channel_id=1, source_target_pairs={{0,6},{1,3},{2,4},{3,1},{4,2},{5,7},{6,0},{7,5},{8,14},{9,11},{10,... | collective-permute-start | bytes 884744 | tf_op jit(solution)/shard_map/ppermute | solution.py:237
  73.2 2.8 %collective-permute-done.4.far_a = bf16[192,768]{1,0:T(8,128)(2,1)S(1)} collective-permute-done((bf16[192,768]{1,0:T(8,128)(2,1)S(1)}, bf16[192,768]{1,0:T(8,128)(2,1)S(1)}, u32[]{:S(2)}, u32[]{:S(2)}) %collective-permute-start.4) | collective-permute-done | bytes 294944 | tf_op jit(solution)/shard_map/ppermute | solution.py:237
  76.0 4.0 %collective-permute-done.5.far_b = bf16[192,768]{1,0:T(8,128)(2,1)S(1)} collective-permute-done((bf16[192,768]{1,0:T(8,128)(2,1)S(1)}, bf16[192,768]{1,0:T(8,128)(2,1)S(1)}, u32[]{:S(2)}, u32[]{:S(2)}) %collective-permute-start.5) | collective-permute-done | bytes 294944 | tf_op jit(solution)/shard_map/ppermute | solution.py:237
  80.0 1.0 shard_map.32
  80.9 1.9 %collective-permute-start.7 = (bf16[8,8,1344]{2,1,0:T(8,128)(2,1)S(1)}, bf16[8,8,1344]{2,1,0:T(8,128)(2,1)S(1)}, u32[]{:S(2)}, u32[]{:S(2)}) collective-permute-start(bf16[8,8,1344]{2,1,0:T(8,128)(2,1)S(1)} %get-tuple-element.18), channel_id=1, source_target_pairs={{0,1},{1,0},{2,3},{3,2},{4,5},{5,4},{6,7},{7,6},{8,9},{9,8},{10,11... | collective-permute-start | bytes 516104 | tf_op jit(solution)/shard_map/ppermute | solution.py:260
  82.9 1.4 %collective-permute-done.7.far_s = bf16[8,8,1344]{2,1,0:T(8,128)(2,1)S(1)} collective-permute-done((bf16[8,8,1344]{2,1,0:T(8,128)(2,1)S(1)}, bf16[8,8,1344]{2,1,0:T(8,128)(2,1)S(1)}, u32[]{:S(2)}, u32[]{:S(2)}) %collective-permute-start.7) | collective-permute-done | bytes 172064 | tf_op jit(solution)/shard_map/ppermute | solution.py:260
  84.2 0.0 collective-permute-done.6.near_s
  84.3 0.2 shard_map.33
  84.4 27.9 %all_to_all.15.received = bf16[8,64,1344]{2,1,0:T(8,128)(2,1)S(1)} all-to-all(bf16[8,64,1344]{2,1,0:T(8,128)(2,1)S(1)} %bitcast.3), channel_id=1, replica_groups={{0,64,128,192,256,320,384,448},{8,72,136,200,264,328,392,456},{16,80,14..., dimensions={0} | all-to-all | bytes 2752512 | tf_op jit(solution)/shard_map/all_to_all | solution.py:273
  112.4 0.2 shard_map.34
  112.6 18.4 %all_to_all.16.received = f32[8,8,1344]{2,1,0:T(8,128)S(1)} all-to-all(f32[8,8,1344]{2,1,0:T(8,128)S(1)} %bitcast.4), channel_id=1, replica_groups={{0,8,16,24,32,40,48,56},{64,72,80,88,96,104,112,120},{128,136,144,152,1..., dimensions={0} | all-to-all | bytes 688128 | tf_op jit(solution)/shard_map/all_to_all | solution.py:284
  131.0 0.7 shard_map.35
Async XLA Ops:
  2.7 33.9 %all-to-all-start = ((bf16[8,15,64,128]{3,2,1,0:T(8,128)(2,1)}), bf16[8,15,64,128]{3,2,1,0:T(8,128)(2,1)}, u32[]{:S(2)}, u32[]{:S(2)}) async-start(bf16[8,15,64,128]{3,2,1,0:T(8,128)(2,1)} %shard_map.28), calls=%async_computation | async-start | bytes 3932160 | tf_op jit(solution)/shard_map/all_to_all | solution.py:207
  41.0 19.6 %collective-permute-start.3 = (bf16[384,768]{1,0:T(8,128)(2,1)S(1)}, bf16[384,768]{1,0:T(8,128)(2,1)S(1)}, u32[]{:S(2)}, u32[]{:S(2)}) collective-permute-start(bf16[384,768]{1,0:T(8,128)(2,1)S(1)} %get-tuple-element.12.own), channel_id=1, source_target_pairs={{0,1},{1,0},{2,3},{3,2},{4,5},{5,4},{6,7},{7,6},{8,9},{9,8},{10,11... | collective-permute-start | bytes 1769480 | tf_op jit(solution)/shard_map/ppermute | solution.py:244
  42.9 17.8 %collective-permute-start.2 = (bf16[384,768]{1,0:T(8,128)(2,1)S(1)}, bf16[384,768]{1,0:T(8,128)(2,1)S(1)}, u32[]{:S(2)}, u32[]{:S(2)}) collective-permute-start(bf16[384,768]{1,0:T(8,128)(2,1)S(1)} %get-tuple-element.12.own), channel_id=1, source_target_pairs={{0,6},{1,3},{2,4},{3,1},{4,2},{5,7},{6,0},{7,5},{8,14},{9,11},{10,... | collective-permute-start | bytes 1769480 | tf_op jit(solution)/shard_map/ppermute | solution.py:237
  46.9 10.5 %collective-permute-start = (bf16[192,768]{1,0:T(8,128)(2,1)S(1)}, bf16[192,768]{1,0:T(8,128)(2,1)S(1)}, u32[]{:S(2)}, u32[]{:S(2)}) collective-permute-start(bf16[192,768]{1,0:T(8,128)(2,1)S(1)} %get-tuple-element.13), channel_id=1, source_target_pairs={{0,2},{1,7},{2,0},{3,5},{4,6},{5,3},{6,4},{7,1},{8,10},{9,15},{10,... | collective-permute-start | bytes 884744 | tf_op jit(solution)/shard_map/ppermute | solution.py:237
  48.8 11.7 %collective-permute-start.1 = (bf16[192,768]{1,0:T(8,128)(2,1)S(1)}, bf16[192,768]{1,0:T(8,128)(2,1)S(1)}, u32[]{:S(2)}, u32[]{:S(2)}) collective-permute-start(bf16[192,768]{1,0:T(8,128)(2,1)S(1)} %get-tuple-element.14), channel_id=1, source_target_pairs={{0,2},{1,7},{2,0},{3,5},{4,6},{5,3},{6,4},{7,1},{8,10},{9,15},{10,... | collective-permute-start | bytes 884744 | tf_op jit(solution)/shard_map/ppermute | solution.py:237
  62.9 21.3 %collective-permute-start.6 = (bf16[24,8,1344]{2,1,0:T(8,128)(2,1)S(1)}, bf16[24,8,1344]{2,1,0:T(8,128)(2,1)S(1)}, u32[]{:S(2)}, u32[]{:S(2)}) collective-permute-start(bf16[24,8,1344]{2,1,0:T(8,128)(2,1)S(1)} %get-tuple-element.17), channel_id=1, source_target_pairs={{0,1},{1,0},{2,3},{3,2},{4,5},{5,4},{6,7},{7,6},{8,9},{9,8},{10,11... | collective-permute-start | bytes 1548296 | tf_op jit(solution)/shard_map/ppermute | solution.py:258
  66.1 9.8 %collective-permute-start.4 = (bf16[192,768]{1,0:T(8,128)(2,1)S(1)}, bf16[192,768]{1,0:T(8,128)(2,1)S(1)}, u32[]{:S(2)}, u32[]{:S(2)}) collective-permute-start(bf16[192,768]{1,0:T(8,128)(2,1)S(1)} %collective-permute-done.first_a), channel_id=1, source_target_pairs={{0,6},{1,3},{2,4},{3,1},{4,2},{5,7},{6,0},{7,5},{8,14},{9,11},{10,... | collective-permute-start | bytes 884744 | tf_op jit(solution)/shard_map/ppermute | solution.py:237
  70.1 9.8 %collective-permute-start.5 = (bf16[192,768]{1,0:T(8,128)(2,1)S(1)}, bf16[192,768]{1,0:T(8,128)(2,1)S(1)}, u32[]{:S(2)}, u32[]{:S(2)}) collective-permute-start(bf16[192,768]{1,0:T(8,128)(2,1)S(1)} %collective-permute-done.1.first_b), channel_id=1, source_target_pairs={{0,6},{1,3},{2,4},{3,1},{4,2},{5,7},{6,0},{7,5},{8,14},{9,11},{10,... | collective-permute-start | bytes 884744 | tf_op jit(solution)/shard_map/ppermute | solution.py:237
  80.9 3.3 %collective-permute-start.7 = (bf16[8,8,1344]{2,1,0:T(8,128)(2,1)S(1)}, bf16[8,8,1344]{2,1,0:T(8,128)(2,1)S(1)}, u32[]{:S(2)}, u32[]{:S(2)}) collective-permute-start(bf16[8,8,1344]{2,1,0:T(8,128)(2,1)S(1)} %get-tuple-element.18), channel_id=1, source_target_pairs={{0,1},{1,0},{2,3},{3,2},{4,5},{5,4},{6,7},{7,6},{8,9},{9,8},{10,11... | collective-permute-start | bytes 516104 | tf_op jit(solution)/shard_map/ppermute | solution.py:260

commit v3 on v2

v3 whole, which is shorter than its diff:
```python
import jax
import jax.numpy as jnp
import numpy as np
from jax import lax
from jax.experimental import pallas as pl
from jax.experimental.pallas import tpu as pltpu
from jax.sharding import Mesh
from jax.sharding import PartitionSpec as P


NB = 6
AXES = ("z", "y", "x", "core")
F32 = jnp.float32
BF16 = jnp.bfloat16
VMEM = pl.BlockSpec(memory_space=pltpu.VMEM)
ANY = pl.BlockSpec(memory_space=pl.ANY)


def tile_of(a, b):
    return a * NB - a * (a - 1) // 2 + b - a


CUT = 4
OFF = [(a, b) for b in range(NB) for a in range(b)]
OFF_AT = {pair: at for at, pair in enumerate(OFF)}


def call(kernel, out_shape, args, flops, nbytes, vmem_mib, **options):
    options.setdefault("in_specs", [VMEM] * len(args))
    options.setdefault("out_specs", jax.tree.map(lambda _: VMEM, out_shape))
    return pl.pallas_call(
        kernel,
        out_shape=out_shape,
        compiler_params=pltpu.CompilerParams(vmem_limit_bytes=vmem_mib * 2**20),
        cost_estimate=pl.CostEstimate(flops=flops, bytes_accessed=nbytes, transcendentals=0),
        **options,
    )(*args)


def pack_kernel(tiles_hbm, out_hbm, tiles, out, sems):
    parts = out.shape[0]
    width = tiles.shape[3] // parts
    loads, stores = [], []
    for a in range(NB - 1):
        stored = pl.ds(tile_of(a, a + 1), NB - 1 - a)
        held = pl.ds(tile_of(a, a + 1) - a - 1, NB - 1 - a)
        loads.append(pltpu.make_async_copy(tiles_hbm.at[:, stored], tiles.at[:, held], sems.at[0, a]))
    for b in range(1, NB):
        ready = pl.ds(OFF_AT[0, b], b)
        stores.append(pltpu.make_async_copy(out.at[:, ready], out_hbm.at[:, ready], sems.at[1, b - 1]))
    for load in loads:
        load.start()
    for at, (a, b) in enumerate(OFF):
        if a == b - 1:
            loads[a].wait()
        first, second = (tiles[slab, tile_of(a, b) - a - 1] for slab in range(2))
        for d in range(parts):
            cols = slice(d * width, (d + 1) * width)
            out[d, at] = jnp.concatenate([first[:, cols], second[:, cols]], axis=1)
        if a == b - 1:
            stores[a].start()
    for store in stores:
        store.wait()


def own_kernel(tiles, coeffs, out):
    size = tiles.shape[3]
    rows = 2 * tiles.shape[2]
    for m in range(NB):
        lhs = jnp.concatenate([tiles[:, tile_of(a, m)].reshape(rows, size) for a in range(m + 1)], axis=0)
        part = jnp.dot(lhs, coeffs[m * size : (m + 1) * size], preferred_element_type=F32)
        part = part.reshape(m + 1, rows, part.shape[1])
        if m:
            out[:m] = out[:m] + part[:m]
        out[m] = part[m]


def lower_part(cols, received_hbm, coeffs_hbm, own_hbm, received, coeffs, own, sems):
    size = received.shape[0] * received.shape[2]
    lanes = received.shape[3]
    last = cols[-1]
    begin = OFF_AT[0, cols[0]] if cols[0] else 0
    count = OFF_AT[last - 1, last] + 1 - begin
    loads = [pltpu.make_async_copy(received_hbm.at[:, pl.ds(begin, count)], received, sems.at[0])]
    for a in range(last):
        rows = pl.ds(a * size, size)
        loads.append(pltpu.make_async_copy(coeffs_hbm.at[rows], coeffs.at[rows], sems.at[a + 1]))
    loads.append(pltpu.make_async_copy(own_hbm.at[pl.ds(cols[0], len(cols))], own, sems.at[last + 1]))
    for load in loads:
        load.start()
    loads[0].wait()
    sums = {b: None for b in cols}
    for a in range(last):
        loads[a + 1].wait()
        fed = [b for b in cols if b > a]
        lhs = jnp.concatenate(
            [received[:, OFF_AT[a, b] - begin].reshape(size, lanes) for b in fed], axis=1
        )
        part = lax.dot_general(
            lhs, coeffs[a * size : (a + 1) * size], (((0,), (0,)), ((), ())), preferred_element_type=F32
        )
        for at, b in enumerate(fed):
            term = part[at * lanes : (at + 1) * lanes]
            sums[b] = term if sums[b] is None else sums[b] + term
    loads[-1].wait()
    both = [own[at] if sums[b] is None else sums[b] + own[at] for at, b in enumerate(cols)]
    return [value.astype(BF16) for value in both]


def put_rows(values, out, begin):
    half, occ = values[0].shape[0] // 2, values[0].shape[1]
    for at, value in enumerate(values):
        rows = slice(begin + at * half, begin + (at + 1) * half)
        out[rows, :occ] = value[:half]
        out[rows, occ:] = value[half:]


def lower_a_kernel(received_hbm, coeffs_hbm, own_hbm, out_a, *scratch):
    put_rows(lower_part(range(CUT), received_hbm, coeffs_hbm, own_hbm, *scratch), out_a, 0)


def lower_b_kernel(received_hbm, coeffs_hbm, own_hbm, half_a, out, out_b, *scratch):
    values = lower_part(range(CUT, NB), received_hbm, coeffs_hbm, own_hbm, *scratch)
    put_rows(values, out_b, 0)
    out[: half_a.shape[0]] = half_a[...]
    put_rows(values, out, half_a.shape[0])


def tiles_kernel(pieces, mine, sib, out_mine, out_sib, base=0):
    width = mine.shape[0] // NB
    high = out_mine.shape[1]
    groups = width // high
    for cols, out in ((sib, out_sib), (mine, out_mine)):
        right = cols[...]
        for place, piece in enumerate(pieces):
            for first, part in piece:
                full = lax.dot_general(
                    part[...], right, (((1,), (1,)), ((), ())), preferred_element_type=F32
                ).astype(BF16)
                for k in range(part.shape[0] // width):
                    a = first + k
                    strip = full[k * width : (k + 1) * width, a * width :]
                    begin = tile_of(a, a) * width - base
                    out[place * groups : (place + 1) * groups, :, begin : begin + strip.shape[1]] = strip.reshape(
                        groups, high, strip.shape[1]
                    )


def near_kernel(own, first_a, first_b, second, sib, out_mine, out_sib):
    pieces = ([(0, own)], [(0, first_a), (CUT, first_b)], [(0, second)])
    tiles_kernel(pieces, own, sib, out_mine, out_sib)


def far_a_kernel(far_a, own, sib, out_mine, out_sib):
    tiles_kernel(([(0, far_a)],), own, sib, out_mine, out_sib)


def far_b_kernel(far_b, own, sib, out_mine, out_sib):
    base = tile_of(CUT, CUT) * own.shape[0] // NB
    tiles_kernel(([(CUT, far_b)],), own, sib, out_mine, out_sib, base)


def gather_kernel(near, far_a, far_b, near_s, far_as, far_bs, out):
    cores = lax.axis_size("core")
    zs, ys = lax.axis_size("z"), lax.axis_size("y")
    x, core = lax.axis_index("x"), lax.axis_index("core")
    even = core == 0
    first, second = jnp.where(even, x ^ 1, x ^ 3), jnp.where(even, x ^ 3, x ^ 1)
    cut = far_a.shape[2]
    for places, parity, close, low, high in (
        ((x, first, second, x ^ 2), core, near, far_a, far_b),
        ((x, second, first, x ^ 2), 1 - core, near_s, far_as, far_bs),
    ):
        for at, place in enumerate(places):
            z = place * cores + parity
            for y in range(ys):
                to = jnp.where(even, z * ys + y, y * zs + z)
                if at < 3:
                    out[to] = close[at * ys + y]
                else:
                    out[to, :, :cut] = low[y]
                    out[to, :, cut:] = high[y]


def sum_of(received):
    total = received[0].astype(F32)
    for k in range(1, received.shape[0]):
        total = total + received[k].astype(F32)
    return total


def sum_kernel(received, out):
    out[...] = sum_of(received).astype(out.dtype)


def last_kernel(received, out):
    total = sum_of(received)
    width = out.shape[2]
    for t in range(out.shape[0]):
        out[t] = total[:, t * width : (t + 1) * width]


def body(integrals, orbitals):
    slabs, tile_count, width, size = integrals.shape
    occ = orbitals.shape[1]
    xs, cores, zs, ys = (lax.axis_size(name) for name in ("x", "core", "z", "y"))
    parts = xs * cores
    rows = size // (zs * ys)
    flops = 2 * slabs * width * size * occ

    packed = call(
        pack_kernel,
        jax.ShapeDtypeStruct((parts, len(OFF), width, slabs * width), BF16),
        (integrals,),
        0,
        2 * integrals.size * 2,
        63,
        in_specs=[ANY],
        out_specs=ANY,
        scratch_shapes=[
            pltpu.VMEM((slabs, len(OFF), width, size), BF16),
            pltpu.VMEM((parts, len(OFF), width, slabs * width), BF16),
            pltpu.SemaphoreType.DMA((2, NB - 1)),
        ],
    )
    received = lax.all_to_all(packed, ("x", "core"), 0, 0)
    own = call(
        own_kernel,
        jax.ShapeDtypeStruct((NB, slabs * width, occ), F32),
        (integrals, orbitals),
        flops * tile_count,
        2 * integrals.size + 2 * orbitals.size,
        63,
    )
    low = jax.ShapeDtypeStruct((CUT * width, slabs * occ), BF16)
    high = jax.ShapeDtypeStruct(((NB - CUT) * width, slabs * occ), BF16)
    whole = jax.ShapeDtypeStruct((NB * width, slabs * occ), BF16)
    in_hbm = [pltpu.with_memory_space_constraint(array, pltpu.HBM) for array in (received, orbitals, own)]

    def lower(kernel, out_shape, args, cols):
        tiles = sum(cols)
        return call(
            kernel,
            out_shape,
            (*in_hbm, *args),
            flops * tiles,
            2 * tiles * parts * width * slabs * width + 2 * orbitals.size,
            20,
            in_specs=[ANY] * 3 + [VMEM] * len(args),
            scratch_shapes=[
                pltpu.VMEM((parts, tiles, width, slabs * width), BF16),
                pltpu.VMEM((cols[-1] * size, occ), BF16),
                pltpu.VMEM((len(cols), slabs * width, occ), F32),
                pltpu.SemaphoreType.DMA((cols[-1] + 2,)),
            ],
        )

    def exchange(array, turn):
        pairs = [((x, c), (x ^ (3 if (c + turn) % 2 else 1), c)) for x in range(xs) for c in range(cores)]
        return lax.ppermute(array, ("x", "core"), [(a * cores + c, b * cores + d) for (a, c), (b, d) in pairs])

    swap = [(i, (i + 1) % cores) for i in range(cores)]
    half_a = lower(lower_a_kernel, low, (), range(CUT))
    first_a = exchange(half_a, 0)
    half, half_b = lower(lower_b_kernel, (whole, high), (half_a,), range(CUT, NB))
    first_b = exchange(half_b, 0)
    second = exchange(half, 1)
    far_a = exchange(first_a, 1)
    sib = lax.ppermute(half, "core", swap)
    far_b = exchange(first_b, 1)

    product = 2 * half.shape[0] ** 2 * half.shape[1]
    cut = tile_of(CUT, CUT) * width
    near_shape = jax.ShapeDtypeStruct((3 * ys, rows, tile_count * width), BF16)
    low_shape = jax.ShapeDtypeStruct((ys, rows, cut), BF16)
    high_shape = jax.ShapeDtypeStruct((ys, rows, tile_count * width - cut), BF16)
    near, near_s = call(
        near_kernel,
        (near_shape, near_shape),
        (half, first_a, first_b, second, sib),
        6 * product,
        8 * half.size,
        16,
    )
    near_s = lax.ppermute(near_s, "core", swap)
    far_a, far_as = call(far_a_kernel, (low_shape, low_shape), (far_a, half, sib), 2 * product, 6 * half.size, 12)
    far_as = lax.ppermute(far_as, "core", swap)
    far_b, far_bs = call(
        far_b_kernel, (high_shape, high_shape), (far_b, half, sib), product, 6 * half.size, 12
    )
    far_bs = lax.ppermute(far_bs, "core", swap)
    partial = call(
        gather_kernel,
        jax.ShapeDtypeStruct((zs * ys, rows, tile_count * width), BF16),
        (near, far_a, far_b, near_s, far_as, far_bs),
        0,
        8 * near.size,
        12,
    )

    at = np.arange(zs * ys * parts).reshape(zs, ys, xs, cores)
    along_z = [[at[:, y, x, c].tolist() for x in range(xs) for y in range(ys)] for c in range(2)]
    along_y = [[at[z, :, x, c].tolist() for x in range(xs) for z in range(zs)] for c in range(2)]
    arrived = lax.all_to_all(
        partial.reshape(zs, ys * rows, tile_count * width), AXES, 0, 0, axis_index_groups=along_z[0] + along_y[1]
    )
    summed = call(
        sum_kernel,
        jax.ShapeDtypeStruct(arrived.shape[1:], BF16),
        (arrived,),
        arrived.size,
        2 * arrived.size,
        8,
    )
    arrived = lax.all_to_all(
        summed.reshape(ys, rows, tile_count * width), AXES, 0, 0, axis_index_groups=along_y[0] + along_z[1]
    )
    tiles = call(
        last_kernel,
        jax.ShapeDtypeStruct((tile_count, rows, width), F32),
        (arrived,),
        arrived.size,
        4 * arrived.size,
        8,
    )
    return jnp.transpose(tiles, (1, 0, 2))


def solution(mesh):
    grid = Mesh(mesh.devices.reshape(8, 8, 4, 2), AXES)
    return jax.shard_map(
        body,
        mesh=grid,
        in_specs=(P(("z", "y"), None, ("x", "core"), None), P()),
        out_specs=P(("z", "y"), None, ("x", "core")),
        check_vma=False,
    )
```

time: 132 us -> 126 us (0.955)
  the two profiles are of different devices: /device:TPU:6 before, /device:TPU:8 now
where the time goes in v3:
time: 126 us; the launch traced here: 125 us
  blocking collectives  48.7 us (39%)
  waiting for transfers between devices  31.2 us (25%)
  starting transfers between devices  28 us (22%)
  Pallas kernels  17.4 us (14%)
    all_to_all x1, blocking collectives, body(): lax.all_to_all(partial.reshape(zs, ys * rows, tile_count * width), AXES,...  33.2 us
    all_to_all x1, waiting for transfers between devices, body(): received = lax.all_to_all(packed, ('x', 'core'), 0, 0)  20.7 us
    pallas_call x10, Pallas kernels, call(): pl.pallas_call(kernel, out_shape=out_shape, compiler_params=pltpu.Compile...  17.4 us
    all_to_all x1, blocking collectives, body(): lax.all_to_all(summed.reshape(ys, rows, tile_count * width), AXES, 0, 0,...  15.5 us
    ppermute x5, starting transfers between devices, exchange(): lax.ppermute(array, ('x', 'core'), [(a * cores + c, b * cores + d) for (a...  15.5 us
    ppermute x5, waiting for transfers between devices, exchange(): lax.ppermute(array, ('x', 'core'), [(a * cores + c, b * cores + d) for (a...  9.31 us
    all_to_all x1, starting transfers between devices, body(): received = lax.all_to_all(packed, ('x', 'core'), 0, 0)  4.34 us
  transfers between devices with their start and end apart: 10, of which 4 were waited for; matrix products, arithmetic and copies ran while one was open for 0% of the time, Pallas kernels for 6%

profile of v3, /device:TPU:8, one launch (start us, length us, event | category | flops | bytes accessed | tf_op | source)
XLA Modules:
  0.0 125.5 jit_solution(14065223496977893824)
XLA Ops:
  0.0 2.9 %shard_map.28 = bf16[8,15,64,128]{3,2,1,0:T(8,128)(2,1)} custom-call(bf16[2,21,64,512]{3,2,1,0:T(8,128)(2,1)} %tiles.1), custom_call_target="tpu_custom_call" | custom-call | bytes 5505024 | tf_op jit(solution)/shard_map/pallas_call | solution.py:31
  2.9 4.3 %all-to-all-start = ((bf16[8,15,64,128]{3,2,1,0:T(8,128)(2,1)}), bf16[8,15,64,128]{3,2,1,0:T(8,128)(2,1)}, u32[]{:S(2)}, u32[]{:S(2)}) async-start(bf16[8,15,64,128]{3,2,1,0:T(8,128)(2,1)} %shard_map.28), calls=%async_computation | async-start | bytes 3932160 | tf_op jit(solution)/shard_map/all_to_all | solution.py:226
  7.3 5.1 %shard_map.29.own_hbm = f32[6,128,384]{2,1,0:T(8,128)} custom-call(bf16[2,21,64,512]{3,2,1,0:T(8,128)(2,1)} %tiles.1, bf16[3072,384]{1,0:T(8,128)(2,1)} %coeffs_hbm.3), custom_call_target="tpu_custom_call" | custom-call | flops 1056964608 | bytes 5111808 | tf_op jit(solution)/shard_map/pallas_call | solution.py:31
  12.3 20.7 %all-to-all-done.received_hbm = bf16[8,15,64,128]{3,2,1,0:T(8,128)(2,1)} async-done(((bf16[8,15,64,128]{3,2,1,0:T(8,128)(2,1)}), bf16[8,15,64,128]{3,2,1,0:T(8,128)(2,1)}, u32[]{:S(2)}, u32[]{:S(2)}) %all-to-all-start) | async-done | bytes 1966112 | tf_op jit(solution)/shard_map/all_to_all | solution.py:226
  33.1 2.3 %shard_map.30.half_a = bf16[256,768]{1,0:T(8,128)(2,1)S(1)} custom-call(bf16[8,15,64,128]{3,2,1,0:T(8,128)(2,1)} %all-to-all-done.received_hbm, bf16[3072,384]{1,0:T(8,128)(2,1)} %coeffs_hbm.3, f32[6,128,384]{2,1,0:T(8,128)} %shard_map.29.own_hbm), custom_call_target="tpu_custom_call" | custom-call | flops 301989888 | bytes 3145728 | tf_op jit(solution)/shard_map/pallas_call | solution.py:31
  35.4 3.0 %shard_map.31 = (bf16[384,768]{1,0:T(8,128)(2,1)S(1)}, bf16[128,768]{1,0:T(8,128)(2,1)S(1)}) custom-call(bf16[8,15,64,128]{3,2,1,0:T(8,128)(2,1)} %all-to-all-done.received_hbm, bf16[3072,384]{1,0:T(8,128)(2,1)} %coeffs_hbm.3, f32[6,128,384]{2,1,0:T(8,128)} %shard_map.29.own_hbm, bf16[256,768]{1,0:T(8,128)(2,1)S(1)} %shard_map.30.half_a), custom_call_target="tpu_custom_call" | custom-call | flops 452984832 | bytes 3538944 | tf_op jit(solution)/shard_map/pallas_call | solution.py:31
  38.5 1.9 %collective-permute-start.3 = (bf16[384,768]{1,0:T(8,128)(2,1)S(1)}, bf16[384,768]{1,0:T(8,128)(2,1)S(1)}, u32[]{:S(2)}, u32[]{:S(2)}) collective-permute-start(bf16[384,768]{1,0:T(8,128)(2,1)S(1)} %get-tuple-element.13.own), channel_id=1, source_target_pairs={{0,1},{1,0},{2,3},{3,2},{4,5},{5,4},{6,7},{7,6},{8,9},{9,8},{10,11... | collective-permute-start | bytes 1769480 | tf_op jit(solution)/shard_map/ppermute | solution.py:269
  40.4 3.1 %collective-permute-start.2 = (bf16[384,768]{1,0:T(8,128)(2,1)S(1)}, bf16[384,768]{1,0:T(8,128)(2,1)S(1)}, u32[]{:S(2)}, u32[]{:S(2)}) collective-permute-start(bf16[384,768]{1,0:T(8,128)(2,1)S(1)} %get-tuple-element.13.own), channel_id=1, source_target_pairs={{0,6},{1,3},{2,4},{3,1},{4,2},{5,7},{6,0},{7,5},{8,14},{9,11},{10,... | collective-permute-start | bytes 1769480 | tf_op jit(solution)/shard_map/ppermute | solution.py:260
  43.5 1.9 %collective-permute-start = (bf16[256,768]{1,0:T(8,128)(2,1)S(1)}, bf16[256,768]{1,0:T(8,128)(2,1)S(1)}, u32[]{:S(2)}, u32[]{:S(2)}) collective-permute-start(bf16[256,768]{1,0:T(8,128)(2,1)S(1)} %shard_map.30.half_a), channel_id=1, source_target_pairs={{0,2},{1,7},{2,0},{3,5},{4,6},{5,3},{6,4},{7,1},{8,10},{9,15},{10,... | collective-permute-start | bytes 1179656 | tf_op jit(solution)/shard_map/ppermute | solution.py:260
  45.4 3.9 %collective-permute-start.1 = (bf16[128,768]{1,0:T(8,128)(2,1)S(1)}, bf16[128,768]{1,0:T(8,128)(2,1)S(1)}, u32[]{:S(2)}, u32[]{:S(2)}) collective-permute-start(bf16[128,768]{1,0:T(8,128)(2,1)S(1)} %get-tuple-element.14), channel_id=1, source_target_pairs={{0,2},{1,7},{2,0},{3,5},{4,6},{5,3},{6,4},{7,1},{8,10},{9,15},{10,... | collective-permute-start | bytes 589832 | tf_op jit(solution)/shard_map/ppermute | solution.py:260
  49.3 6.6 %collective-permute-done.first_a = bf16[256,768]{1,0:T(8,128)(2,1)S(1)} collective-permute-done((bf16[256,768]{1,0:T(8,128)(2,1)S(1)}, bf16[256,768]{1,0:T(8,128)(2,1)S(1)}, u32[]{:S(2)}, u32[]{:S(2)}) %collective-permute-start) | collective-permute-done | bytes 393248 | tf_op jit(solution)/shard_map/ppermute | solution.py:260
  55.9 3.1 %collective-permute-start.4 = (bf16[256,768]{1,0:T(8,128)(2,1)S(1)}, bf16[256,768]{1,0:T(8,128)(2,1)S(1)}, u32[]{:S(2)}, u32[]{:S(2)}) collective-permute-start(bf16[256,768]{1,0:T(8,128)(2,1)S(1)} %collective-permute-done.first_a), channel_id=1, source_target_pairs={{0,6},{1,3},{2,4},{3,1},{4,2},{5,7},{6,0},{7,5},{8,14},{9,11},{10,... | collective-permute-start | bytes 1179656 | tf_op jit(solution)/shard_map/ppermute | solution.py:260
  59.0 0.0 collective-permute-done.1.first_b
  59.0 0.0 collective-permute-done.3.sib
  59.0 0.0 collective-permute-done.2.second
  59.0 2.0 %shard_map.32 = (bf16[24,8,1344]{2,1,0:T(8,128)(2,1)S(1)}, bf16[24,8,1344]{2,1,0:T(8,128)(2,1)S(1)}) custom-call(bf16[384,768]{1,0:T(8,128)(2,1)S(1)} %get-tuple-element.13.own, bf16[256,768]{1,0:T(8,128)(2,1)S(1)} %collective-permute-done.first_a, bf16[128,768]{1,0:T(8,128)(2,1)S(1)} %collective-permute-done.1.first_b, ...), custom_call_target="tpu_custom_call" | custom-call | flops 1358954496 | bytes 2359296 | tf_op jit(solution)/shard_map/pallas_call | solution.py:31
  61.0 2.4 %collective-permute-start.6 = (bf16[24,8,1344]{2,1,0:T(8,128)(2,1)S(1)}, bf16[24,8,1344]{2,1,0:T(8,128)(2,1)S(1)}, u32[]{:S(2)}, u32[]{:S(2)}) collective-permute-start(bf16[24,8,1344]{2,1,0:T(8,128)(2,1)S(1)} %get-tuple-element.18), channel_id=1, source_target_pairs={{0,1},{1,0},{2,3},{3,2},{4,5},{5,4},{6,7},{7,6},{8,9},{9,8},{10,11... | collective-permute-start | bytes 1548296 | tf_op jit(solution)/shard_map/ppermute | solution.py:285
  63.4 3.5 %collective-permute-start.5 = (bf16[128,768]{1,0:T(8,128)(2,1)S(1)}, bf16[128,768]{1,0:T(8,128)(2,1)S(1)}, u32[]{:S(2)}, u32[]{:S(2)}) collective-permute-start(bf16[128,768]{1,0:T(8,128)(2,1)S(1)} %collective-permute-done.1.first_b), channel_id=1, source_target_pairs={{0,6},{1,3},{2,4},{3,1},{4,2},{5,7},{6,0},{7,5},{8,14},{9,11},{10,... | collective-permute-start | bytes 589832 | tf_op jit(solution)/shard_map/ppermute | solution.py:260
  66.9 0.0 collective-permute-done.4.far_a
  66.9 0.6 shard_map.33
  67.5 1.9 %collective-permute-start.7 = (bf16[8,8,1152]{2,1,0:T(8,128)(2,1)S(1)}, bf16[8,8,1152]{2,1,0:T(8,128)(2,1)S(1)}, u32[]{:S(2)}, u32[]{:S(2)}) collective-permute-start(bf16[8,8,1152]{2,1,0:T(8,128)(2,1)S(1)} %get-tuple-element.19), channel_id=1, source_target_pairs={{0,1},{1,0},{2,3},{3,2},{4,5},{5,4},{6,7},{7,6},{8,9},{9,8},{10,11... | collective-permute-start | bytes 442376 | tf_op jit(solution)/shard_map/ppermute | solution.py:287
  69.5 2.7 %collective-permute-done.5.far_b = bf16[128,768]{1,0:T(8,128)(2,1)S(1)} collective-permute-done((bf16[128,768]{1,0:T(8,128)(2,1)S(1)}, bf16[128,768]{1,0:T(8,128)(2,1)S(1)}, u32[]{:S(2)}, u32[]{:S(2)}) %collective-permute-start.5) | collective-permute-done | bytes 196640 | tf_op jit(solution)/shard_map/ppermute | solution.py:260
  72.2 0.3 shard_map.34
  72.5 1.9 %collective-permute-start.8 = (bf16[8,8,192]{2,1,0:T(8,128)(2,1)S(1)}, bf16[8,8,192]{2,1,0:T(8,128)(2,1)S(1)}, u32[]{:S(2)}, u32[]{:S(2)}) collective-permute-start(bf16[8,8,192]{2,1,0:T(8,128)(2,1)S(1)} %get-tuple-element.20), channel_id=1, source_target_pairs={{0,1},{1,0},{2,3},{3,2},{4,5},{5,4},{6,7},{7,6},{8,9},{9,8},{10,11... | collective-permute-start | bytes 73736 | tf_op jit(solution)/shard_map/ppermute | solution.py:291
  74.5 1.2 collective-permute-done.8.far_bs
  75.6 0.0 collective-permute-done.7.far_as
  75.6 0.0 collective-permute-done.6.near_s
  75.6 0.2 shard_map.35
  75.8 33.2 %all_to_all.15.received = bf16[8,64,1344]{2,1,0:T(8,128)(2,1)S(1)} all-to-all(bf16[8,64,1344]{2,1,0:T(8,128)(2,1)S(1)} %bitcast.3), channel_id=1, replica_groups={{0,64,128,192,256,320,384,448},{8,72,136,200,264,328,392,456},{16,80,14..., dimensions={0} | all-to-all | bytes 2752512 | tf_op jit(solution)/shard_map/all_to_all | solution.py:304
  109.1 0.2 shard_map.36
  109.3 15.5 %all_to_all.16.received = bf16[8,8,1344]{2,1,0:T(8,128)(2,1)S(1)} all-to-all(bf16[8,8,1344]{2,1,0:T(8,128)(2,1)S(1)} %bitcast.4), channel_id=1, replica_groups={{0,8,16,24,32,40,48,56},{64,72,80,88,96,104,112,120},{128,136,144,152,1..., dimensions={0} | all-to-all | bytes 344064 | tf_op jit(solution)/shard_map/all_to_all | solution.py:315
  124.7 0.7 shard_map.37
Async XLA Ops:
  2.9 30.2 %all-to-all-start = ((bf16[8,15,64,128]{3,2,1,0:T(8,128)(2,1)}), bf16[8,15,64,128]{3,2,1,0:T(8,128)(2,1)}, u32[]{:S(2)}, u32[]{:S(2)}) async-start(bf16[8,15,64,128]{3,2,1,0:T(8,128)(2,1)} %shard_map.28), calls=%async_computation | async-start | bytes 3932160 | tf_op jit(solution)/shard_map/all_to_all | solution.py:226
  38.5 20.5 %collective-permute-start.3 = (bf16[384,768]{1,0:T(8,128)(2,1)S(1)}, bf16[384,768]{1,0:T(8,128)(2,1)S(1)}, u32[]{:S(2)}, u32[]{:S(2)}) collective-permute-start(bf16[384,768]{1,0:T(8,128)(2,1)S(1)} %get-tuple-element.13.own), channel_id=1, source_target_pairs={{0,1},{1,0},{2,3},{3,2},{4,5},{5,4},{6,7},{7,6},{8,9},{9,8},{10,11... | collective-permute-start | bytes 1769480 | tf_op jit(solution)/shard_map/ppermute | solution.py:269
  40.4 18.6 %collective-permute-start.2 = (bf16[384,768]{1,0:T(8,128)(2,1)S(1)}, bf16[384,768]{1,0:T(8,128)(2,1)S(1)}, u32[]{:S(2)}, u32[]{:S(2)}) collective-permute-start(bf16[384,768]{1,0:T(8,128)(2,1)S(1)} %get-tuple-element.13.own), channel_id=1, source_target_pairs={{0,6},{1,3},{2,4},{3,1},{4,2},{5,7},{6,0},{7,5},{8,14},{9,11},{10,... | collective-permute-start | bytes 1769480 | tf_op jit(solution)/shard_map/ppermute | solution.py:260
  43.5 12.4 %collective-permute-start = (bf16[256,768]{1,0:T(8,128)(2,1)S(1)}, bf16[256,768]{1,0:T(8,128)(2,1)S(1)}, u32[]{:S(2)}, u32[]{:S(2)}) collective-permute-start(bf16[256,768]{1,0:T(8,128)(2,1)S(1)} %shard_map.30.half_a), channel_id=1, source_target_pairs={{0,2},{1,7},{2,0},{3,5},{4,6},{5,3},{6,4},{7,1},{8,10},{9,15},{10,... | collective-permute-start | bytes 1179656 | tf_op jit(solution)/shard_map/ppermute | solution.py:260
  45.4 13.6 %collective-permute-start.1 = (bf16[128,768]{1,0:T(8,128)(2,1)S(1)}, bf16[128,768]{1,0:T(8,128)(2,1)S(1)}, u32[]{:S(2)}, u32[]{:S(2)}) collective-permute-start(bf16[128,768]{1,0:T(8,128)(2,1)S(1)} %get-tuple-element.14), channel_id=1, source_target_pairs={{0,2},{1,7},{2,0},{3,5},{4,6},{5,3},{6,4},{7,1},{8,10},{9,15},{10,... | collective-permute-start | bytes 589832 | tf_op jit(solution)/shard_map/ppermute | solution.py:260
  55.9 11.0 %collective-permute-start.4 = (bf16[256,768]{1,0:T(8,128)(2,1)S(1)}, bf16[256,768]{1,0:T(8,128)(2,1)S(1)}, u32[]{:S(2)}, u32[]{:S(2)}) collective-permute-start(bf16[256,768]{1,0:T(8,128)(2,1)S(1)} %collective-permute-done.first_a), channel_id=1, source_target_pairs={{0,6},{1,3},{2,4},{3,1},{4,2},{5,7},{6,0},{7,5},{8,14},{9,11},{10,... | collective-permute-start | bytes 1179656 | tf_op jit(solution)/shard_map/ppermute | solution.py:260
  61.0 14.6 %collective-permute-start.6 = (bf16[24,8,1344]{2,1,0:T(8,128)(2,1)S(1)}, bf16[24,8,1344]{2,1,0:T(8,128)(2,1)S(1)}, u32[]{:S(2)}, u32[]{:S(2)}) collective-permute-start(bf16[24,8,1344]{2,1,0:T(8,128)(2,1)S(1)} %get-tuple-element.18), channel_id=1, source_target_pairs={{0,1},{1,0},{2,3},{3,2},{4,5},{5,4},{6,7},{7,6},{8,9},{9,8},{10,11... | collective-permute-start | bytes 1548296 | tf_op jit(solution)/shard_map/ppermute | solution.py:285
  63.4 8.8 %collective-permute-start.5 = (bf16[128,768]{1,0:T(8,128)(2,1)S(1)}, bf16[128,768]{1,0:T(8,128)(2,1)S(1)}, u32[]{:S(2)}, u32[]{:S(2)}) collective-permute-start(bf16[128,768]{1,0:T(8,128)(2,1)S(1)} %collective-permute-done.1.first_b), channel_id=1, source_target_pairs={{0,6},{1,3},{2,4},{3,1},{4,2},{5,7},{6,0},{7,5},{8,14},{9,11},{10,... | collective-permute-start | bytes 589832 | tf_op jit(solution)/shard_map/ppermute | solution.py:260
  67.5 8.1 %collective-permute-start.7 = (bf16[8,8,1152]{2,1,0:T(8,128)(2,1)S(1)}, bf16[8,8,1152]{2,1,0:T(8,128)(2,1)S(1)}, u32[]{:S(2)}, u32[]{:S(2)}) collective-permute-start(bf16[8,8,1152]{2,1,0:T(8,128)(2,1)S(1)} %get-tuple-element.19), channel_id=1, source_target_pairs={{0,1},{1,0},{2,3},{3,2},{4,5},{5,4},{6,7},{7,6},{8,9},{9,8},{10,11... | collective-permute-start | bytes 442376 | tf_op jit(solution)/shard_map/ppermute | solution.py:287
  72.5 3.1 %collective-permute-start.8 = (bf16[8,8,192]{2,1,0:T(8,128)(2,1)S(1)}, bf16[8,8,192]{2,1,0:T(8,128)(2,1)S(1)}, u32[]{:S(2)}, u32[]{:S(2)}) collective-permute-start(bf16[8,8,192]{2,1,0:T(8,128)(2,1)S(1)} %get-tuple-element.20), channel_id=1, source_target_pairs={{0,1},{1,0},{2,3},{3,2},{4,5},{5,4},{6,7},{7,6},{8,9},{9,8},{10,11... | collective-permute-start | bytes 73736 | tf_op jit(solution)/shard_map/ppermute | solution.py:291

commit v4 on v2

--- a/solution.py
+++ b/solution.py
@@ -72,7 +72,7 @@
         out[m] = part[m]
 
 
-def lower_kernel(received_hbm, coeffs_hbm, own_hbm, out, out_a, out_b, received, coeffs, own, sems):
+def lower_kernel(received_hbm, coeffs_hbm, own_hbm, out, received, coeffs, own, sems):
     size = received.shape[0] * received.shape[2]
     lanes = received.shape[3]
     half = lanes // 2
@@ -111,56 +111,56 @@
     for b in range(NB):
         both = own[b] if sums[b] is None else sums[b] + own[b]
         both = both.astype(BF16)
-        for ref, at in ((out, b), (out_a if b < NB // 2 else out_b, b % (NB // 2))):
-            ref[at * half : (at + 1) * half, :occ] = both[:half]
-            ref[at * half : (at + 1) * half, occ:] = both[half:]
-
-
-def tiles_kernel(pieces, mine, sib, out_mine, out_sib):
-    width = mine.shape[0] // NB
-    high = out_mine.shape[1]
-    groups = width // high
-    for cols, out in ((mine, out_mine), (sib, out_sib)):
-        right = cols[...]
-        for place, piece in enumerate(pieces):
-            a = 0
-            for part in piece:
-                full = lax.dot_general(
-                    part[...], right, (((1,), (1,)), ((), ())), preferred_element_type=F32
-                ).astype(BF16)
-                for k in range(part.shape[0] // width):
-                    strip = full[k * width : (k + 1) * width, a * width :]
-                    begin = tile_of(a, a) * width
-                    out[place * groups : (place + 1) * groups, :, begin : begin + strip.shape[1]] = strip.reshape(
-                        groups, high, strip.shape[1]
-                    )
-                    a += 1
-
-
-def near_kernel(own, first_a, first_b, second, sib, out_mine, out_sib):
-    tiles_kernel(((own,), (first_a, first_b), (second,)), own, sib, out_mine, out_sib)
-
-
-def far_kernel(far_a, far_b, own, sib, out_mine, out_sib):
-    tiles_kernel(((far_a, far_b),), own, sib, out_mine, out_sib)
-
-
-def gather_kernel(near, far, near_s, far_s, out):
+        out[b * half : (b + 1) * half, :occ] = both[:half]
+        out[b * half : (b + 1) * half, occ:] = both[half:]
+
+
+def strips_of(piece, cols):
+    width = piece.shape[0] // NB
+    full = lax.dot_general(piece[...], cols[...], (((1,), (1,)), ((), ())), preferred_element_type=F32).astype(BF16)
+    for a in range(NB):
+        begin = tile_of(a, a) * width
+        yield begin, full[a * width : (a + 1) * width, a * width :]
+
+
+def tiles_kernel(pieces, cols, out, place=0):
+    high = out.shape[1]
+    for piece in pieces:
+        groups = piece.shape[0] // NB // high
+        for begin, strip in strips_of(piece, cols):
+            out[place : place + groups, :, begin : begin + strip.shape[1]] = strip.reshape(groups, high, strip.shape[1])
+        place += groups
+
+
+def near_kernel(own, sib, first, out):
+    tiles_kernel((own, sib, first), own, out)
+
+
+def cross_kernel(first, second, first_s, out_same, out_other):
+    tiles_kernel((first,), second, out_same)
+    tiles_kernel((first,), first_s, out_other)
+
+
+def gather_kernel(near, own, first_s, second, second_s, far, far_s, out, late):
     cores = lax.axis_size("core")
     zs, ys = lax.axis_size("z"), lax.axis_size("y")
     x, core = lax.axis_index("x"), lax.axis_index("core")
     even = core == 0
-    first, second = jnp.where(even, x ^ 1, x ^ 3), jnp.where(even, x ^ 3, x ^ 1)
-    for places, source, parity in (
-        ((x, first, second), near, core),
-        ((x ^ 2,), far, core),
-        ((x, second, first), near_s, 1 - core),
-        ((x ^ 2,), far_s, 1 - core),
+    one, two = jnp.where(even, x ^ 1, x ^ 3), jnp.where(even, x ^ 3, x ^ 1)
+    tiles_kernel((first_s, second, second_s), own, late)
+    for chip, parity, source, begin in (
+        (x, core, near, 0),
+        (x, 1 - core, near, ys),
+        (one, core, near, 2 * ys),
+        (two, 1 - core, late, 0),
+        (two, core, late, ys),
+        (one, 1 - core, late, 2 * ys),
+        (x ^ 2, core, far, 0),
+        (x ^ 2, 1 - core, far_s, 0),
     ):
-        for at, place in enumerate(places):
-            z = place * cores + parity
-            for y in range(ys):
-                out[jnp.where(even, z * ys + y, y * zs + z)] = source[at * ys + y]
+        z = chip * cores + parity
+        for y in range(ys):
+            out[jnp.where(even, z * ys + y, y * zs + z)] = source[begin + y]
 
 
 def sum_of(received):
@@ -171,7 +171,7 @@
 
 
 def sum_kernel(received, out):
-    out[...] = sum_of(received)
+    out[...] = sum_of(received).astype(out.dtype)
 
 
 def last_kernel(received, out):
@@ -214,11 +214,10 @@
         63,
     )
     whole = jax.ShapeDtypeStruct((NB * width, slabs * occ), BF16)
-    side = jax.ShapeDtypeStruct((NB // 2 * width, slabs * occ), BF16)
     in_hbm = lambda array: pltpu.with_memory_space_constraint(array, pltpu.HBM)
-    half, half_a, half_b = call(
+    half = call(
         lower_kernel,
-        (whole, side, side),
+        whole,
         (in_hbm(received), in_hbm(orbitals), in_hbm(own)),
         flops * len(OFF),
         2 * received.size + 2 * orbitals.size,
@@ -232,39 +231,43 @@
         ],
     )
 
-    def exchange(array, turn):
-        pairs = [((x, c), (x ^ (3 if (c + turn) % 2 else 1), c)) for x in range(xs) for c in range(cores)]
-        return lax.ppermute(array, ("x", "core"), [(a * cores + c, b * cores + d) for (a, c), (b, d) in pairs])
-
-    swap = [(i, (i + 1) % cores) for i in range(cores)]
-    first_a = exchange(half_a, 0)
-    first_b = exchange(half_b, 0)
+    def exchange(array, turn, flip=0):
+        pairs = [
+            (x * cores + c, (x ^ (3 if (c + turn) % 2 else 1)) * cores + (c + flip) % cores)
+            for x in range(xs)
+            for c in range(cores)
+        ]
+        return lax.ppermute(array, ("x", "core"), pairs)
+
+    def swapped(array):
+        return lax.ppermute(array, "core", [(c, (c + 1) % cores) for c in range(cores)])
+
+    product = 2 * half.shape[0] ** 2 * half.shape[1]
+    tiles_shape = lambda pieces: jax.ShapeDtypeStruct((pieces * ys, rows, tile_count * width), BF16)
+    first = exchange(half, 0)
     second = exchange(half, 1)
-    far_a = exchange(first_a, 1)
-    sib = lax.ppermute(half, "core", swap)
-    far_b = exchange(first_b, 1)
-
-    product = 2 * half.shape[0] ** 2 * half.shape[1]
-    near_shape = jax.ShapeDtypeStruct((3 * ys, rows, tile_count * width), BF16)
-    far_shape = jax.ShapeDtypeStruct((ys, rows, tile_count * width), BF16)
-    near, near_s = call(
-        near_kernel,
-        (near_shape, near_shape),
-        (half, first_a, first_b, second, sib),
-        6 * product,
-        8 * half.size,
-        16,
-    )
-    near_s = lax.ppermute(near_s, "core", swap)
-    far, far_s = call(far_kernel, (far_shape, far_shape), (far_a, far_b, half, sib), 2 * product, 6 * half.size, 12)
-    far_s = lax.ppermute(far_s, "core", swap)
+    sib = swapped(half)
+    first_s = swapped(first)
+    near = call(near_kernel, tiles_shape(3), (half, sib, first), 3 * product, 8 * half.size, 12)
+    same, other = call(
+        cross_kernel,
+        (tiles_shape(1), tiles_shape(1)),
+        (first, second, first_s),
+        2 * product,
+        7 * half.size,
+        12,
+    )
+    far = exchange(same, 1)
+    far_s = exchange(other, 1, 1)
+    second_s = swapped(second)
     partial = call(
         gather_kernel,
-        jax.ShapeDtypeStruct((zs * ys, rows, tile_count * width), BF16),
-        (near, far, near_s, far_s),
-        0,
-        8 * near.size,
-        12,
+        tiles_shape(zs),
+        (near, half, first_s, second, second_s, far, far_s),
+        3 * product,
+        16 * half.size,
+        16,
+        scratch_shapes=[pltpu.VMEM(tiles_shape(3).shape, BF16)],
     )
 
     at = np.arange(zs * ys * parts).reshape(zs, ys, xs, cores)
@@ -275,7 +278,7 @@
     )
     summed = call(
         sum_kernel,
-        jax.ShapeDtypeStruct(arrived.shape[1:], F32),
+        jax.ShapeDtypeStruct(arrived.shape[1:], BF16),
         (arrived,),
         arrived.size,
         2 * arrived.size,

time: 132 us -> 123 us (0.932)
  waiting for transfers between devices: 34.8 us -> 31 us
  starting transfers between devices: 34 us -> 30.3 us
  blocking collectives: 46.4 us -> 44.4 us
    ppermute x8 -> x7, waiting for transfers between devices: 16.1 us -> 12.4 us  [the longest x4 12.3 us: exchange(): return lax.ppermute(array, ('x', 'core'), pairs)]
    ppermute x8 -> x7, starting transfers between devices: 23.9 us -> 20.2 us  [the longest x4 14 us: exchange(): return lax.ppermute(array, ('x', 'core'), pairs)]
    all_to_all x1, blocking collectives: 18.4 us -> 16.5 us  [body(): lax.all_to_all(summed.reshape(ys, rows, tile_count * width), AXES, 0, 0,...]
  transfers between devices with their start and end apart: 9 -> 8, of which waited for: 7 -> 3; matrix products, arithmetic and copies ran while one was open for 0% -> 0% of each run, Pallas kernels for 5% -> 6%
where the time goes in v4:
time: 123 us; the launch traced here: 122 us
  blocking collectives  44.4 us (36%)
  waiting for transfers between devices  31 us (25%)
  starting transfers between devices  30.3 us (25%)
  Pallas kernels  16.3 us (13%)
    all_to_all x1, blocking collectives, body(): lax.all_to_all(partial.reshape(zs, ys * rows, tile_count * width), AXES,...  27.9 us
    all_to_all x1, waiting for transfers between devices, body(): received = lax.all_to_all(packed, ('x', 'core'), 0, 0)  18.7 us
    all_to_all x1, blocking collectives, body(): lax.all_to_all(summed.reshape(ys, rows, tile_count * width), AXES, 0, 0,...  16.5 us
    pallas_call x8, Pallas kernels, call(): pl.pallas_call(kernel, out_shape=out_shape, compiler_params=pltpu.Compile...  16.3 us
    ppermute x4, starting transfers between devices, exchange(): return lax.ppermute(array, ('x', 'core'), pairs)  14 us
    ppermute x4, waiting for transfers between devices, exchange(): return lax.ppermute(array, ('x', 'core'), pairs)  12.3 us
    all_to_all x1, starting transfers between devices, body(): received = lax.all_to_all(packed, ('x', 'core'), 0, 0)  10.1 us
    ppermute x3, starting transfers between devices, swapped(): lax.ppermute(array, 'core', [(c, (c + 1) % cores) for c in range(cores)])  6.24 us
  transfers between devices with their start and end apart: 8, of which 3 were waited for; matrix products, arithmetic and copies ran while one was open for 0% of the time, Pallas kernels for 6%

profile of v4, /device:TPU:6, one launch (start us, length us, event | category | flops | bytes accessed | tf_op | source)
XLA Modules:
  0.0 122.2 jit_solution(17230764875191318958)
XLA Ops:
  0.0 2.7 %shard_map.28 = bf16[8,15,64,128]{3,2,1,0:T(8,128)(2,1)} custom-call(bf16[2,21,64,512]{3,2,1,0:T(8,128)(2,1)} %tiles.1), custom_call_target="tpu_custom_call" | custom-call | bytes 5505024 | tf_op jit(solution)/shard_map/pallas_call | solution.py:30
  2.7 10.1 %all-to-all-start = ((bf16[8,15,64,128]{3,2,1,0:T(8,128)(2,1)}), bf16[8,15,64,128]{3,2,1,0:T(8,128)(2,1)}, u32[]{:S(2)}, u32[]{:S(2)}) async-start(bf16[8,15,64,128]{3,2,1,0:T(8,128)(2,1)} %shard_map.28), calls=%async_computation | async-start | bytes 3932160 | tf_op jit(solution)/shard_map/all_to_all | solution.py:207
  12.8 5.1 %shard_map.29.own_hbm = f32[6,128,384]{2,1,0:T(8,128)} custom-call(bf16[2,21,64,512]{3,2,1,0:T(8,128)(2,1)} %tiles.1, bf16[3072,384]{1,0:T(8,128)(2,1)} %coeffs_hbm.1), custom_call_target="tpu_custom_call" | custom-call | flops 1056964608 | bytes 5111808 | tf_op jit(solution)/shard_map/pallas_call | solution.py:30
  17.9 18.7 %all-to-all-done.received_hbm = bf16[8,15,64,128]{3,2,1,0:T(8,128)(2,1)} async-done(((bf16[8,15,64,128]{3,2,1,0:T(8,128)(2,1)}), bf16[8,15,64,128]{3,2,1,0:T(8,128)(2,1)}, u32[]{:S(2)}, u32[]{:S(2)}) %all-to-all-start) | async-done | bytes 1966112 | tf_op jit(solution)/shard_map/all_to_all | solution.py:207
  36.6 4.4 %shard_map.30.own = bf16[384,768]{1,0:T(8,128)(2,1)S(1)} custom-call(bf16[8,15,64,128]{3,2,1,0:T(8,128)(2,1)} %all-to-all-done.received_hbm, bf16[3072,384]{1,0:T(8,128)(2,1)} %coeffs_hbm.1, f32[6,128,384]{2,1,0:T(8,128)} %shard_map.29.own_hbm), custom_call_target="tpu_custom_call" | custom-call | flops 754974720 | bytes 4325376 | tf_op jit(solution)/shard_map/pallas_call | solution.py:30
  41.0 1.9 %collective-permute-start.1 = (bf16[384,768]{1,0:T(8,128)(2,1)S(1)}, bf16[384,768]{1,0:T(8,128)(2,1)S(1)}, u32[]{:S(2)}, u32[]{:S(2)}) collective-permute-start(bf16[384,768]{1,0:T(8,128)(2,1)S(1)} %shard_map.30.own), channel_id=1, source_target_pairs={{0,2},{1,7},{2,0},{3,5},{4,6},{5,3},{6,4},{7,1},{8,10},{9,15},{10,... | collective-permute-start | bytes 1769480 | tf_op jit(solution)/shard_map/ppermute | solution.py:240
  42.9 4.6 %collective-permute-start.3 = (bf16[384,768]{1,0:T(8,128)(2,1)S(1)}, bf16[384,768]{1,0:T(8,128)(2,1)S(1)}, u32[]{:S(2)}, u32[]{:S(2)}) collective-permute-start(bf16[384,768]{1,0:T(8,128)(2,1)S(1)} %shard_map.30.own), channel_id=1, source_target_pairs={{0,6},{1,3},{2,4},{3,1},{4,2},{5,7},{6,0},{7,5},{8,14},{9,11},{10,... | collective-permute-start | bytes 1769480 | tf_op jit(solution)/shard_map/ppermute | solution.py:240
  47.5 9.3 %collective-permute-done.1.first = bf16[384,768]{1,0:T(8,128)(2,1)S(1)} collective-permute-done((bf16[384,768]{1,0:T(8,128)(2,1)S(1)}, bf16[384,768]{1,0:T(8,128)(2,1)S(1)}, u32[]{:S(2)}, u32[]{:S(2)}) %collective-permute-start.1) | collective-permute-done | bytes 589856 | tf_op jit(solution)/shard_map/ppermute | solution.py:240
  56.8 1.9 %collective-permute-start.2 = (bf16[384,768]{1,0:T(8,128)(2,1)S(1)}, bf16[384,768]{1,0:T(8,128)(2,1)S(1)}, u32[]{:S(2)}, u32[]{:S(2)}) collective-permute-start(bf16[384,768]{1,0:T(8,128)(2,1)S(1)} %collective-permute-done.1.first), channel_id=1, source_target_pairs={{0,1},{1,0},{2,3},{3,2},{4,5},{5,4},{6,7},{7,6},{8,9},{9,8},{10,11... | collective-permute-start | bytes 1769480 | tf_op jit(solution)/shard_map/ppermute | solution.py:243
  58.7 2.4 %collective-permute-start = (bf16[384,768]{1,0:T(8,128)(2,1)S(1)}, bf16[384,768]{1,0:T(8,128)(2,1)S(1)}, u32[]{:S(2)}, u32[]{:S(2)}) collective-permute-start(bf16[384,768]{1,0:T(8,128)(2,1)S(1)} %shard_map.30.own), channel_id=1, source_target_pairs={{0,1},{1,0},{2,3},{3,2},{4,5},{5,4},{6,7},{7,6},{8,9},{9,8},{10,11... | collective-permute-start | bytes 1769480 | tf_op jit(solution)/shard_map/ppermute | solution.py:243
  61.1 0.0 collective-permute-done.3.second
  61.1 1.9 %collective-permute-start.4 = (bf16[384,768]{1,0:T(8,128)(2,1)S(1)}, bf16[384,768]{1,0:T(8,128)(2,1)S(1)}, u32[]{:S(2)}, u32[]{:S(2)}) collective-permute-start(bf16[384,768]{1,0:T(8,128)(2,1)S(1)} %collective-permute-done.3.second), channel_id=1, source_target_pairs={{0,1},{1,0},{2,3},{3,2},{4,5},{5,4},{6,7},{7,6},{8,9},{9,8},{10,11... | collective-permute-start | bytes 1769480 | tf_op jit(solution)/shard_map/ppermute | solution.py:243
  63.0 0.0 collective-permute-done.2.first_s
  63.0 0.8 shard_map.32
  63.9 4.9 %collective-permute-start.5 = (bf16[8,8,1344]{2,1,0:T(8,128)(2,1)S(1)}, bf16[8,8,1344]{2,1,0:T(8,128)(2,1)S(1)}, u32[]{:S(2)}, u32[]{:S(2)}) collective-permute-start(bf16[8,8,1344]{2,1,0:T(8,128)(2,1)S(1)} %get-tuple-element.7), channel_id=1, source_target_pairs={{0,6},{1,3},{2,4},{3,1},{4,2},{5,7},{6,0},{7,5},{8,14},{9,11},{10,... | collective-permute-start | bytes 516104 | tf_op jit(solution)/shard_map/ppermute | solution.py:240
  68.8 2.6 %collective-permute-start.6 = (bf16[8,8,1344]{2,1,0:T(8,128)(2,1)S(1)}, bf16[8,8,1344]{2,1,0:T(8,128)(2,1)S(1)}, u32[]{:S(2)}, u32[]{:S(2)}) collective-permute-start(bf16[8,8,1344]{2,1,0:T(8,128)(2,1)S(1)} %get-tuple-element.8), channel_id=1, source_target_pairs={{0,7},{1,2},{2,5},{3,0},{4,3},{5,6},{6,1},{7,4},{8,15},{9,10},{10,... | collective-permute-start | bytes 516104 | tf_op jit(solution)/shard_map/ppermute | solution.py:240
  71.4 0.0 collective-permute-done.sib
  71.4 1.2 shard_map.31.near
  72.6 0.0 collective-permute-done.4.second_s
  72.6 0.0 collective-permute-done.5.far
  72.6 3.0 %collective-permute-done.6.far_s = bf16[8,8,1344]{2,1,0:T(8,128)(2,1)S(1)} collective-permute-done((bf16[8,8,1344]{2,1,0:T(8,128)(2,1)S(1)}, bf16[8,8,1344]{2,1,0:T(8,128)(2,1)S(1)}, u32[]{:S(2)}, u32[]{:S(2)}) %collective-permute-start.6) | collective-permute-done | bytes 172064 | tf_op jit(solution)/shard_map/ppermute | solution.py:240
  75.6 1.2 shard_map.33
  76.8 27.9 %all_to_all.15.received = bf16[8,64,1344]{2,1,0:T(8,128)(2,1)S(1)} all-to-all(bf16[8,64,1344]{2,1,0:T(8,128)(2,1)S(1)} %bitcast.3), channel_id=1, replica_groups={{0,64,128,192,256,320,384,448},{8,72,136,200,264,328,392,456},{16,80,14..., dimensions={0} | all-to-all | bytes 2752512 | tf_op jit(solution)/shard_map/all_to_all | solution.py:276
  104.8 0.2 shard_map.34
  105.0 16.5 %all_to_all.16.received = bf16[8,8,1344]{2,1,0:T(8,128)(2,1)S(1)} all-to-all(bf16[8,8,1344]{2,1,0:T(8,128)(2,1)S(1)} %bitcast.4), channel_id=1, replica_groups={{0,8,16,24,32,40,48,56},{64,72,80,88,96,104,112,120},{128,136,144,152,1..., dimensions={0} | all-to-all | bytes 344064 | tf_op jit(solution)/shard_map/all_to_all | solution.py:287
  121.5 0.7 shard_map.35
Async XLA Ops:
  2.7 33.9 %all-to-all-start = ((bf16[8,15,64,128]{3,2,1,0:T(8,128)(2,1)}), bf16[8,15,64,128]{3,2,1,0:T(8,128)(2,1)}, u32[]{:S(2)}, u32[]{:S(2)}) async-start(bf16[8,15,64,128]{3,2,1,0:T(8,128)(2,1)} %shard_map.28), calls=%async_computation | async-start | bytes 3932160 | tf_op jit(solution)/shard_map/all_to_all | solution.py:207
  41.0 15.8 %collective-permute-start.1 = (bf16[384,768]{1,0:T(8,128)(2,1)S(1)}, bf16[384,768]{1,0:T(8,128)(2,1)S(1)}, u32[]{:S(2)}, u32[]{:S(2)}) collective-permute-start(bf16[384,768]{1,0:T(8,128)(2,1)S(1)} %shard_map.30.own), channel_id=1, source_target_pairs={{0,2},{1,7},{2,0},{3,5},{4,6},{5,3},{6,4},{7,1},{8,10},{9,15},{10,... | collective-permute-start | bytes 1769480 | tf_op jit(solution)/shard_map/ppermute | solution.py:240
  42.9 18.2 %collective-permute-start.3 = (bf16[384,768]{1,0:T(8,128)(2,1)S(1)}, bf16[384,768]{1,0:T(8,128)(2,1)S(1)}, u32[]{:S(2)}, u32[]{:S(2)}) collective-permute-start(bf16[384,768]{1,0:T(8,128)(2,1)S(1)} %shard_map.30.own), channel_id=1, source_target_pairs={{0,6},{1,3},{2,4},{3,1},{4,2},{5,7},{6,0},{7,5},{8,14},{9,11},{10,... | collective-permute-start | bytes 1769480 | tf_op jit(solution)/shard_map/ppermute | solution.py:240
  56.8 6.3 %collective-permute-start.2 = (bf16[384,768]{1,0:T(8,128)(2,1)S(1)}, bf16[384,768]{1,0:T(8,128)(2,1)S(1)}, u32[]{:S(2)}, u32[]{:S(2)}) collective-permute-start(bf16[384,768]{1,0:T(8,128)(2,1)S(1)} %collective-permute-done.1.first), channel_id=1, source_target_pairs={{0,1},{1,0},{2,3},{3,2},{4,5},{5,4},{6,7},{7,6},{8,9},{9,8},{10,11... | collective-permute-start | bytes 1769480 | tf_op jit(solution)/shard_map/ppermute | solution.py:243
  58.7 12.7 %collective-permute-start = (bf16[384,768]{1,0:T(8,128)(2,1)S(1)}, bf16[384,768]{1,0:T(8,128)(2,1)S(1)}, u32[]{:S(2)}, u32[]{:S(2)}) collective-permute-start(bf16[384,768]{1,0:T(8,128)(2,1)S(1)} %shard_map.30.own), channel_id=1, source_target_pairs={{0,1},{1,0},{2,3},{3,2},{4,5},{5,4},{6,7},{7,6},{8,9},{9,8},{10,11... | collective-permute-start | bytes 1769480 | tf_op jit(solution)/shard_map/ppermute | solution.py:243
  61.1 11.5 %collective-permute-start.4 = (bf16[384,768]{1,0:T(8,128)(2,1)S(1)}, bf16[384,768]{1,0:T(8,128)(2,1)S(1)}, u32[]{:S(2)}, u32[]{:S(2)}) collective-permute-start(bf16[384,768]{1,0:T(8,128)(2,1)S(1)} %collective-permute-done.3.second), channel_id=1, source_target_pairs={{0,1},{1,0},{2,3},{3,2},{4,5},{5,4},{6,7},{7,6},{8,9},{9,8},{10,11... | collective-permute-start | bytes 1769480 | tf_op jit(solution)/shard_map/ppermute | solution.py:243
  63.9 8.7 %collective-permute-start.5 = (bf16[8,8,1344]{2,1,0:T(8,128)(2,1)S(1)}, bf16[8,8,1344]{2,1,0:T(8,128)(2,1)S(1)}, u32[]{:S(2)}, u32[]{:S(2)}) collective-permute-start(bf16[8,8,1344]{2,1,0:T(8,128)(2,1)S(1)} %get-tuple-element.7), channel_id=1, source_target_pairs={{0,6},{1,3},{2,4},{3,1},{4,2},{5,7},{6,0},{7,5},{8,14},{9,11},{10,... | collective-permute-start | bytes 516104 | tf_op jit(solution)/shard_map/ppermute | solution.py:240
  68.8 6.8 %collective-permute-start.6 = (bf16[8,8,1344]{2,1,0:T(8,128)(2,1)S(1)}, bf16[8,8,1344]{2,1,0:T(8,128)(2,1)S(1)}, u32[]{:S(2)}, u32[]{:S(2)}) collective-permute-start(bf16[8,8,1344]{2,1,0:T(8,128)(2,1)S(1)} %get-tuple-element.8), channel_id=1, source_target_pairs={{0,7},{1,2},{2,5},{3,0},{4,3},{5,6},{6,1},{7,4},{8,15},{9,10},{10,... | collective-permute-start | bytes 516104 | tf_op jit(solution)/shard_map/ppermute | solution.py:240

commit v5 on v4

--- a/solution.py
+++ b/solution.py
@@ -141,20 +141,24 @@
     tiles_kernel((first,), first_s, out_other)
 
 
-def gather_kernel(near, own, first_s, second, second_s, far, far_s, out, late):
+def late_kernel(own, first_s, second, out):
+    tiles_kernel((first_s, second), own, out)
+
+
+def gather_kernel(near, late, own, second_s, far, far_s, out, last):
     cores = lax.axis_size("core")
     zs, ys = lax.axis_size("z"), lax.axis_size("y")
     x, core = lax.axis_index("x"), lax.axis_index("core")
     even = core == 0
     one, two = jnp.where(even, x ^ 1, x ^ 3), jnp.where(even, x ^ 3, x ^ 1)
-    tiles_kernel((first_s, second, second_s), own, late)
+    tiles_kernel((second_s,), own, last)
     for chip, parity, source, begin in (
         (x, core, near, 0),
         (x, 1 - core, near, ys),
         (one, core, near, 2 * ys),
         (two, 1 - core, late, 0),
         (two, core, late, ys),
-        (one, 1 - core, late, 2 * ys),
+        (one, 1 - core, last, 0),
         (x ^ 2, core, far, 0),
         (x ^ 2, 1 - core, far_s, 0),
     ):
@@ -260,14 +264,15 @@
     far = exchange(same, 1)
     far_s = exchange(other, 1, 1)
     second_s = swapped(second)
+    late = call(late_kernel, tiles_shape(2), (half, first_s, second), 2 * product, 7 * half.size, 12)
     partial = call(
         gather_kernel,
         tiles_shape(zs),
-        (near, half, first_s, second, second_s, far, far_s),
-        3 * product,
+        (near, late, half, second_s, far, far_s),
+        product,
         16 * half.size,
         16,
-        scratch_shapes=[pltpu.VMEM(tiles_shape(3).shape, BF16)],
+        scratch_shapes=[pltpu.VMEM(tiles_shape(1).shape, BF16)],
     )
 
     at = np.arange(zs * ys * parts).reshape(zs, ys, xs, cores)

time: 123 us -> 122 us (level)
    pallas_call x8 -> x9, Pallas kernels: 16.3 us -> 16.5 us  [call(): pl.pallas_call(kernel, out_shape=out_shape, compiler_params=pltpu.Compile...]
  transfers between devices with their start and end apart: 8 -> 8, of which waited for: 3 -> 3; matrix products, arithmetic and copies ran while one was open for 0% -> 0% of each run, Pallas kernels for 6% -> 7%
where the time goes in v5:
time: 122 us
  blocking collectives  44.4 us (36%)
  starting transfers between devices  30.3 us (25%)
  waiting for transfers between devices  30.2 us (25%)
  Pallas kernels  16.5 us (14%)
    all_to_all x1, blocking collectives, body(): lax.all_to_all(partial.reshape(zs, ys * rows, tile_count * width), AXES,...  27.9 us
    all_to_all x1, waiting for transfers between devices, body(): received = lax.all_to_all(packed, ('x', 'core'), 0, 0)  18.7 us
    pallas_call x9, Pallas kernels, call(): pl.pallas_call(kernel, out_shape=out_shape, compiler_params=pltpu.Compile...  16.5 us
    all_to_all x1, blocking collectives, body(): lax.all_to_all(summed.reshape(ys, rows, tile_count * width), AXES, 0, 0,...  16.5 us
    ppermute x4, starting transfers between devices, exchange(): return lax.ppermute(array, ('x', 'core'), pairs)  14 us
    ppermute x4, waiting for transfers between devices, exchange(): return lax.ppermute(array, ('x', 'core'), pairs)  11.5 us
    all_to_all x1, starting transfers between devices, body(): received = lax.all_to_all(packed, ('x', 'core'), 0, 0)  10.1 us
    ppermute x3, starting transfers between devices, swapped(): lax.ppermute(array, 'core', [(c, (c + 1) % cores) for c in range(cores)])  6.24 us
  transfers between devices with their start and end apart: 8, of which 3 were waited for; matrix products, arithmetic and copies ran while one was open for 0% of the time, Pallas kernels for 7%

profile of v5, /device:TPU:6, one launch (start us, length us, event | category | flops | bytes accessed | tf_op | source)
XLA Modules:
  0.0 121.6 jit_solution(11165057347535473644)
XLA Ops:
  0.0 2.7 %shard_map.28 = bf16[8,15,64,128]{3,2,1,0:T(8,128)(2,1)} custom-call(bf16[2,21,64,512]{3,2,1,0:T(8,128)(2,1)} %tiles.1), custom_call_target="tpu_custom_call" | custom-call | bytes 5505024 | tf_op jit(solution)/shard_map/pallas_call | solution.py:30
  2.7 10.1 %all-to-all-start = ((bf16[8,15,64,128]{3,2,1,0:T(8,128)(2,1)}), bf16[8,15,64,128]{3,2,1,0:T(8,128)(2,1)}, u32[]{:S(2)}, u32[]{:S(2)}) async-start(bf16[8,15,64,128]{3,2,1,0:T(8,128)(2,1)} %shard_map.28), calls=%async_computation | async-start | bytes 3932160 | tf_op jit(solution)/shard_map/all_to_all | solution.py:211
  12.8 5.1 %shard_map.29.own_hbm = f32[6,128,384]{2,1,0:T(8,128)} custom-call(bf16[2,21,64,512]{3,2,1,0:T(8,128)(2,1)} %tiles.1, bf16[3072,384]{1,0:T(8,128)(2,1)} %coeffs_hbm.1), custom_call_target="tpu_custom_call" | custom-call | flops 1056964608 | bytes 5111808 | tf_op jit(solution)/shard_map/pallas_call | solution.py:30
  17.9 18.7 %all-to-all-done.received_hbm = bf16[8,15,64,128]{3,2,1,0:T(8,128)(2,1)} async-done(((bf16[8,15,64,128]{3,2,1,0:T(8,128)(2,1)}), bf16[8,15,64,128]{3,2,1,0:T(8,128)(2,1)}, u32[]{:S(2)}, u32[]{:S(2)}) %all-to-all-start) | async-done | bytes 1966112 | tf_op jit(solution)/shard_map/all_to_all | solution.py:211
  36.6 4.4 %shard_map.30.own = bf16[384,768]{1,0:T(8,128)(2,1)S(1)} custom-call(bf16[8,15,64,128]{3,2,1,0:T(8,128)(2,1)} %all-to-all-done.received_hbm, bf16[3072,384]{1,0:T(8,128)(2,1)} %coeffs_hbm.1, f32[6,128,384]{2,1,0:T(8,128)} %shard_map.29.own_hbm), custom_call_target="tpu_custom_call" | custom-call | flops 754974720 | bytes 4325376 | tf_op jit(solution)/shard_map/pallas_call | solution.py:30
  41.0 1.9 %collective-permute-start.1 = (bf16[384,768]{1,0:T(8,128)(2,1)S(1)}, bf16[384,768]{1,0:T(8,128)(2,1)S(1)}, u32[]{:S(2)}, u32[]{:S(2)}) collective-permute-start(bf16[384,768]{1,0:T(8,128)(2,1)S(1)} %shard_map.30.own), channel_id=1, source_target_pairs={{0,2},{1,7},{2,0},{3,5},{4,6},{5,3},{6,4},{7,1},{8,10},{9,15},{10,... | collective-permute-start | bytes 1769480 | tf_op jit(solution)/shard_map/ppermute | solution.py:244
  42.9 4.6 %collective-permute-start.3 = (bf16[384,768]{1,0:T(8,128)(2,1)S(1)}, bf16[384,768]{1,0:T(8,128)(2,1)S(1)}, u32[]{:S(2)}, u32[]{:S(2)}) collective-permute-start(bf16[384,768]{1,0:T(8,128)(2,1)S(1)} %shard_map.30.own), channel_id=1, source_target_pairs={{0,6},{1,3},{2,4},{3,1},{4,2},{5,7},{6,0},{7,5},{8,14},{9,11},{10,... | collective-permute-start | bytes 1769480 | tf_op jit(solution)/shard_map/ppermute | solution.py:244
  47.5 9.3 %collective-permute-done.1.first = bf16[384,768]{1,0:T(8,128)(2,1)S(1)} collective-permute-done((bf16[384,768]{1,0:T(8,128)(2,1)S(1)}, bf16[384,768]{1,0:T(8,128)(2,1)S(1)}, u32[]{:S(2)}, u32[]{:S(2)}) %collective-permute-start.1) | collective-permute-done | bytes 589856 | tf_op jit(solution)/shard_map/ppermute | solution.py:244
  56.8 1.9 %collective-permute-start.2 = (bf16[384,768]{1,0:T(8,128)(2,1)S(1)}, bf16[384,768]{1,0:T(8,128)(2,1)S(1)}, u32[]{:S(2)}, u32[]{:S(2)}) collective-permute-start(bf16[384,768]{1,0:T(8,128)(2,1)S(1)} %collective-permute-done.1.first), channel_id=1, source_target_pairs={{0,1},{1,0},{2,3},{3,2},{4,5},{5,4},{6,7},{7,6},{8,9},{9,8},{10,11... | collective-permute-start | bytes 1769480 | tf_op jit(solution)/shard_map/ppermute | solution.py:247
  58.7 2.4 %collective-permute-start = (bf16[384,768]{1,0:T(8,128)(2,1)S(1)}, bf16[384,768]{1,0:T(8,128)(2,1)S(1)}, u32[]{:S(2)}, u32[]{:S(2)}) collective-permute-start(bf16[384,768]{1,0:T(8,128)(2,1)S(1)} %shard_map.30.own), channel_id=1, source_target_pairs={{0,1},{1,0},{2,3},{3,2},{4,5},{5,4},{6,7},{7,6},{8,9},{9,8},{10,11... | collective-permute-start | bytes 1769480 | tf_op jit(solution)/shard_map/ppermute | solution.py:247
  61.1 0.0 collective-permute-done.3.second
  61.1 1.9 %collective-permute-start.4 = (bf16[384,768]{1,0:T(8,128)(2,1)S(1)}, bf16[384,768]{1,0:T(8,128)(2,1)S(1)}, u32[]{:S(2)}, u32[]{:S(2)}) collective-permute-start(bf16[384,768]{1,0:T(8,128)(2,1)S(1)} %collective-permute-done.3.second), channel_id=1, source_target_pairs={{0,1},{1,0},{2,3},{3,2},{4,5},{5,4},{6,7},{7,6},{8,9},{9,8},{10,11... | collective-permute-start | bytes 1769480 | tf_op jit(solution)/shard_map/ppermute | solution.py:247
  63.0 0.0 collective-permute-done.2.first_s
  63.0 0.8 shard_map.33
  63.9 4.9 %collective-permute-start.5 = (bf16[8,8,1344]{2,1,0:T(8,128)(2,1)S(1)}, bf16[8,8,1344]{2,1,0:T(8,128)(2,1)S(1)}, u32[]{:S(2)}, u32[]{:S(2)}) collective-permute-start(bf16[8,8,1344]{2,1,0:T(8,128)(2,1)S(1)} %get-tuple-element.7), channel_id=1, source_target_pairs={{0,6},{1,3},{2,4},{3,1},{4,2},{5,7},{6,0},{7,5},{8,14},{9,11},{10,... | collective-permute-start | bytes 516104 | tf_op jit(solution)/shard_map/ppermute | solution.py:244
  68.8 2.6 %collective-permute-start.6 = (bf16[8,8,1344]{2,1,0:T(8,128)(2,1)S(1)}, bf16[8,8,1344]{2,1,0:T(8,128)(2,1)S(1)}, u32[]{:S(2)}, u32[]{:S(2)}) collective-permute-start(bf16[8,8,1344]{2,1,0:T(8,128)(2,1)S(1)} %get-tuple-element.8), channel_id=1, source_target_pairs={{0,7},{1,2},{2,5},{3,0},{4,3},{5,6},{6,1},{7,4},{8,15},{9,10},{10,... | collective-permute-start | bytes 516104 | tf_op jit(solution)/shard_map/ppermute | solution.py:244
  71.4 0.0 collective-permute-done.sib
  71.4 1.2 shard_map.31.near
  72.6 0.9 shard_map.32.late
  73.4 0.0 collective-permute-done.4.second_s
  73.4 0.0 collective-permute-done.5.far
  73.5 2.2 %collective-permute-done.6.far_s = bf16[8,8,1344]{2,1,0:T(8,128)(2,1)S(1)} collective-permute-done((bf16[8,8,1344]{2,1,0:T(8,128)(2,1)S(1)}, bf16[8,8,1344]{2,1,0:T(8,128)(2,1)S(1)}, u32[]{:S(2)}, u32[]{:S(2)}) %collective-permute-start.6) | collective-permute-done | bytes 172064 | tf_op jit(solution)/shard_map/ppermute | solution.py:244
  75.6 0.6 shard_map.34
  76.2 27.9 %all_to_all.15.received = bf16[8,64,1344]{2,1,0:T(8,128)(2,1)S(1)} all-to-all(bf16[8,64,1344]{2,1,0:T(8,128)(2,1)S(1)} %bitcast.3), channel_id=1, replica_groups={{0,64,128,192,256,320,384,448},{8,72,136,200,264,328,392,456},{16,80,14..., dimensions={0} | all-to-all | bytes 2752512 | tf_op jit(solution)/shard_map/all_to_all | solution.py:281
  104.2 0.2 shard_map.35
  104.3 16.5 %all_to_all.16.received = bf16[8,8,1344]{2,1,0:T(8,128)(2,1)S(1)} all-to-all(bf16[8,8,1344]{2,1,0:T(8,128)(2,1)S(1)} %bitcast.4), channel_id=1, replica_groups={{0,8,16,24,32,40,48,56},{64,72,80,88,96,104,112,120},{128,136,144,152,1..., dimensions={0} | all-to-all | bytes 344064 | tf_op jit(solution)/shard_map/all_to_all | solution.py:292
  120.8 0.7 shard_map.36
Async XLA Ops:
  2.7 33.9 %all-to-all-start = ((bf16[8,15,64,128]{3,2,1,0:T(8,128)(2,1)}), bf16[8,15,64,128]{3,2,1,0:T(8,128)(2,1)}, u32[]{:S(2)}, u32[]{:S(2)}) async-start(bf16[8,15,64,128]{3,2,1,0:T(8,128)(2,1)} %shard_map.28), calls=%async_computation | async-start | bytes 3932160 | tf_op jit(solution)/shard_map/all_to_all | solution.py:211
  41.0 15.8 %collective-permute-start.1 = (bf16[384,768]{1,0:T(8,128)(2,1)S(1)}, bf16[384,768]{1,0:T(8,128)(2,1)S(1)}, u32[]{:S(2)}, u32[]{:S(2)}) collective-permute-start(bf16[384,768]{1,0:T(8,128)(2,1)S(1)} %shard_map.30.own), channel_id=1, source_target_pairs={{0,2},{1,7},{2,0},{3,5},{4,6},{5,3},{6,4},{7,1},{8,10},{9,15},{10,... | collective-permute-start | bytes 1769480 | tf_op jit(solution)/shard_map/ppermute | solution.py:244
  42.9 18.2 %collective-permute-start.3 = (bf16[384,768]{1,0:T(8,128)(2,1)S(1)}, bf16[384,768]{1,0:T(8,128)(2,1)S(1)}, u32[]{:S(2)}, u32[]{:S(2)}) collective-permute-start(bf16[384,768]{1,0:T(8,128)(2,1)S(1)} %shard_map.30.own), channel_id=1, source_target_pairs={{0,6},{1,3},{2,4},{3,1},{4,2},{5,7},{6,0},{7,5},{8,14},{9,11},{10,... | collective-permute-start | bytes 1769480 | tf_op jit(solution)/shard_map/ppermute | solution.py:244
  56.8 6.3 %collective-permute-start.2 = (bf16[384,768]{1,0:T(8,128)(2,1)S(1)}, bf16[384,768]{1,0:T(8,128)(2,1)S(1)}, u32[]{:S(2)}, u32[]{:S(2)}) collective-permute-start(bf16[384,768]{1,0:T(8,128)(2,1)S(1)} %collective-permute-done.1.first), channel_id=1, source_target_pairs={{0,1},{1,0},{2,3},{3,2},{4,5},{5,4},{6,7},{7,6},{8,9},{9,8},{10,11... | collective-permute-start | bytes 1769480 | tf_op jit(solution)/shard_map/ppermute | solution.py:247
  58.7 12.7 %collective-permute-start = (bf16[384,768]{1,0:T(8,128)(2,1)S(1)}, bf16[384,768]{1,0:T(8,128)(2,1)S(1)}, u32[]{:S(2)}, u32[]{:S(2)}) collective-permute-start(bf16[384,768]{1,0:T(8,128)(2,1)S(1)} %shard_map.30.own), channel_id=1, source_target_pairs={{0,1},{1,0},{2,3},{3,2},{4,5},{5,4},{6,7},{7,6},{8,9},{9,8},{10,11... | collective-permute-start | bytes 1769480 | tf_op jit(solution)/shard_map/ppermute | solution.py:247
  61.1 12.3 %collective-permute-start.4 = (bf16[384,768]{1,0:T(8,128)(2,1)S(1)}, bf16[384,768]{1,0:T(8,128)(2,1)S(1)}, u32[]{:S(2)}, u32[]{:S(2)}) collective-permute-start(bf16[384,768]{1,0:T(8,128)(2,1)S(1)} %collective-permute-done.3.second), channel_id=1, source_target_pairs={{0,1},{1,0},{2,3},{3,2},{4,5},{5,4},{6,7},{7,6},{8,9},{9,8},{10,11... | collective-permute-start | bytes 1769480 | tf_op jit(solution)/shard_map/ppermute | solution.py:247
  63.9 9.5 %collective-permute-start.5 = (bf16[8,8,1344]{2,1,0:T(8,128)(2,1)S(1)}, bf16[8,8,1344]{2,1,0:T(8,128)(2,1)S(1)}, u32[]{:S(2)}, u32[]{:S(2)}) collective-permute-start(bf16[8,8,1344]{2,1,0:T(8,128)(2,1)S(1)} %get-tuple-element.7), channel_id=1, source_target_pairs={{0,6},{1,3},{2,4},{3,1},{4,2},{5,7},{6,0},{7,5},{8,14},{9,11},{10,... | collective-permute-start | bytes 516104 | tf_op jit(solution)/shard_map/ppermute | solution.py:244
  68.8 6.8 %collective-permute-start.6 = (bf16[8,8,1344]{2,1,0:T(8,128)(2,1)S(1)}, bf16[8,8,1344]{2,1,0:T(8,128)(2,1)S(1)}, u32[]{:S(2)}, u32[]{:S(2)}) collective-permute-start(bf16[8,8,1344]{2,1,0:T(8,128)(2,1)S(1)} %get-tuple-element.8), channel_id=1, source_target_pairs={{0,7},{1,2},{2,5},{3,0},{4,3},{5,6},{6,1},{7,4},{8,15},{9,10},{10,... | collective-permute-start | bytes 516104 | tf_op jit(solution)/shard_map/ppermute | solution.py:244

commit v6 on v3

--- a/solution.py
+++ b/solution.py
@@ -126,60 +126,62 @@
     put_rows(values, out, half_a.shape[0])
 
 
-def tiles_kernel(pieces, mine, sib, out_mine, out_sib, base=0):
-    width = mine.shape[0] // NB
-    high = out_mine.shape[1]
-    groups = width // high
-    for cols, out in ((sib, out_sib), (mine, out_mine)):
-        right = cols[...]
-        for place, piece in enumerate(pieces):
-            for first, part in piece:
-                full = lax.dot_general(
-                    part[...], right, (((1,), (1,)), ((), ())), preferred_element_type=F32
-                ).astype(BF16)
-                for k in range(part.shape[0] // width):
-                    a = first + k
-                    strip = full[k * width : (k + 1) * width, a * width :]
-                    begin = tile_of(a, a) * width - base
-                    out[place * groups : (place + 1) * groups, :, begin : begin + strip.shape[1]] = strip.reshape(
-                        groups, high, strip.shape[1]
-                    )
-
-
-def near_kernel(own, first_a, first_b, second, sib, out_mine, out_sib):
-    pieces = ([(0, own)], [(0, first_a), (CUT, first_b)], [(0, second)])
-    tiles_kernel(pieces, own, sib, out_mine, out_sib)
-
-
-def far_a_kernel(far_a, own, sib, out_mine, out_sib):
-    tiles_kernel(([(0, far_a)],), own, sib, out_mine, out_sib)
-
-
-def far_b_kernel(far_b, own, sib, out_mine, out_sib):
-    base = tile_of(CUT, CUT) * own.shape[0] // NB
-    tiles_kernel(([(CUT, far_b)],), own, sib, out_mine, out_sib, base)
-
-
-def gather_kernel(near, far_a, far_b, near_s, far_as, far_bs, out):
+def rows_in(piece):
+    return jnp.concatenate([part[...] for part in piece], axis=0) if isinstance(piece, tuple) else piece[...]
+
+
+def strips_of(piece, cols):
+    piece, cols = rows_in(piece), rows_in(cols)
+    width = piece.shape[0] // NB
+    full = lax.dot_general(piece, cols, (((1,), (1,)), ((), ())), preferred_element_type=F32).astype(BF16)
+    for a in range(NB):
+        begin = tile_of(a, a) * width
+        yield begin, full[a * width : (a + 1) * width, a * width :]
+
+
+def tiles_kernel(pieces, cols, out):
+    place = 0
+    high = out.shape[1]
+    groups = out.shape[0] // len(pieces)
+    for piece in pieces:
+        for begin, strip in strips_of(piece, cols):
+            out[place : place + groups, :, begin : begin + strip.shape[1]] = strip.reshape(groups, high, strip.shape[1])
+        place += groups
+
+
+def near_kernel(own, sib, first_a, first_b, out):
+    tiles_kernel((own, sib, (first_a, first_b)), own, out)
+
+
+def cross_kernel(first_a, first_b, second, first_as, first_bs, out_same, out_other):
+    tiles_kernel(((first_a, first_b),), second, out_same)
+    tiles_kernel(((first_a, first_b),), (first_as, first_bs), out_other)
+
+
+def late_kernel(own, first_as, first_bs, second, out):
+    tiles_kernel(((first_as, first_bs), second), own, out)
+
+
+def gather_kernel(near, late, own, second_s, far, far_s, out, last):
     cores = lax.axis_size("core")
     zs, ys = lax.axis_size("z"), lax.axis_size("y")
     x, core = lax.axis_index("x"), lax.axis_index("core")
     even = core == 0
-    first, second = jnp.where(even, x ^ 1, x ^ 3), jnp.where(even, x ^ 3, x ^ 1)
-    cut = far_a.shape[2]
-    for places, parity, close, low, high in (
-        ((x, first, second, x ^ 2), core, near, far_a, far_b),
-        ((x, second, first, x ^ 2), 1 - core, near_s, far_as, far_bs),
+    one, two = jnp.where(even, x ^ 1, x ^ 3), jnp.where(even, x ^ 3, x ^ 1)
+    tiles_kernel((second_s,), own, last)
+    for chip, parity, source, begin in (
+        (x, core, near, 0),
+        (x, 1 - core, near, ys),
+        (one, core, near, 2 * ys),
+        (two, 1 - core, late, 0),
+        (two, core, late, ys),
+        (one, 1 - core, last, 0),
+        (x ^ 2, core, far, 0),
+        (x ^ 2, 1 - core, far_s, 0),
     ):
-        for at, place in enumerate(places):
-            z = place * cores + parity
-            for y in range(ys):
-                to = jnp.where(even, z * ys + y, y * zs + z)
-                if at < 3:
-                    out[to] = close[at * ys + y]
-                else:
-                    out[to, :, :cut] = low[y]
-                    out[to, :, cut:] = high[y]
+        z = chip * cores + parity
+        for y in range(ys):
+            out[jnp.where(even, z * ys + y, y * zs + z)] = source[begin + y]
 
 
 def sum_of(received):
@@ -255,47 +257,50 @@
             ],
         )
 
-    def exchange(array, turn):
-        pairs = [((x, c), (x ^ (3 if (c + turn) % 2 else 1), c)) for x in range(xs) for c in range(cores)]
-        return lax.ppermute(array, ("x", "core"), [(a * cores + c, b * cores + d) for (a, c), (b, d) in pairs])
-
-    swap = [(i, (i + 1) % cores) for i in range(cores)]
+    def exchange(array, turn, flip=0):
+        pairs = [
+            (x * cores + c, (x ^ (3 if (c + turn) % 2 else 1)) * cores + (c + flip) % cores)
+            for x in range(xs)
+            for c in range(cores)
+        ]
+        return lax.ppermute(array, ("x", "core"), pairs)
+
+    def swapped(array):
+        return lax.ppermute(array, "core", [(c, (c + 1) % cores) for c in range(cores)])
+
+    product = 2 * whole.shape[0] ** 2 * whole.shape[1]
+    tiles_shape = lambda pieces: jax.ShapeDtypeStruct((pieces * ys, rows, tile_count * width), BF16)
     half_a = lower(lower_a_kernel, low, (), range(CUT))
     first_a = exchange(half_a, 0)
     half, half_b = lower(lower_b_kernel, (whole, high), (half_a,), range(CUT, NB))
     first_b = exchange(half_b, 0)
     second = exchange(half, 1)
-    far_a = exchange(first_a, 1)
-    sib = lax.ppermute(half, "core", swap)
-    far_b = exchange(first_b, 1)
-
-    product = 2 * half.shape[0] ** 2 * half.shape[1]
-    cut = tile_of(CUT, CUT) * width
-    near_shape = jax.ShapeDtypeStruct((3 * ys, rows, tile_count * width), BF16)
-    low_shape = jax.ShapeDtypeStruct((ys, rows, cut), BF16)
-    high_shape = jax.ShapeDtypeStruct((ys, rows, tile_count * width - cut), BF16)
-    near, near_s = call(
-        near_kernel,
-        (near_shape, near_shape),
-        (half, first_a, first_b, second, sib),
-        6 * product,
-        8 * half.size,
-        16,
-    )
-    near_s = lax.ppermute(near_s, "core", swap)
-    far_a, far_as = call(far_a_kernel, (low_shape, low_shape), (far_a, half, sib), 2 * product, 6 * half.size, 12)
-    far_as = lax.ppermute(far_as, "core", swap)
-    far_b, far_bs = call(
-        far_b_kernel, (high_shape, high_shape), (far_b, half, sib), product, 6 * half.size, 12
-    )
-    far_bs = lax.ppermute(far_bs, "core", swap)
+    sib = swapped(half)
+    first_as = swapped(first_a)
+    first_bs = swapped(first_b)
+    same, other = call(
+        cross_kernel,
+        (tiles_shape(1), tiles_shape(1)),
+        (first_a, first_b, second, first_as, first_bs),
+        2 * product,
+        7 * half.size,
+        12,
+    )
+    far = exchange(same, 1)
+    far_s = exchange(other, 1, 1)
+    second_s = swapped(second)
+    near = call(near_kernel, tiles_shape(3), (half, sib, first_a, first_b), 3 * product, 8 * half.size, 12)
+    late = call(
+        late_kernel, tiles_shape(2), (half, first_as, first_bs, second), 2 * product, 7 * half.size, 12
+    )
     partial = call(
         gather_kernel,
-        jax.ShapeDtypeStruct((zs * ys, rows, tile_count * width), BF16),
-        (near, far_a, far_b, near_s, far_as, far_bs),
-        0,
-        8 * near.size,
-        12,
+        tiles_shape(zs),
+        (near, late, half, second_s, far, far_s),
+        product,
+        16 * half.size,
+        16,
+        scratch_shapes=[pltpu.VMEM(tiles_shape(1).shape, BF16)],
     )
 
     at = np.arange(zs * ys * parts).reshape(zs, ys, xs, cores)

time: 126 us -> 124 us (0.984)
  the two profiles are of different devices: /device:TPU:8 before, /device:TPU:6 now
where the time goes in v6:
time: 124 us
  blocking collectives  44.5 us (36%)
  starting transfers between devices  34.8 us (28%)
  waiting for transfers between devices  26.6 us (21%)
  Pallas kernels  17.7 us (14%)
    all_to_all x1, blocking collectives, body(): lax.all_to_all(partial.reshape(zs, ys * rows, tile_count * width), AXES,...  28 us
    all_to_all x1, waiting for transfers between devices, body(): received = lax.all_to_all(packed, ('x', 'core'), 0, 0)  18.7 us
    pallas_call x10, Pallas kernels, call(): pl.pallas_call(kernel, out_shape=out_shape, compiler_params=pltpu.Compile...  17.7 us
    all_to_all x1, blocking collectives, body(): lax.all_to_all(summed.reshape(ys, rows, tile_count * width), AXES, 0, 0,...  16.5 us
    ppermute x5, starting transfers between devices, exchange(): return lax.ppermute(array, ('x', 'core'), pairs)  15.4 us
    all_to_all x1, starting transfers between devices, body(): received = lax.all_to_all(packed, ('x', 'core'), 0, 0)  10.1 us
    ppermute x4, starting transfers between devices, swapped(): lax.ppermute(array, 'core', [(c, (c + 1) % cores) for c in range(cores)])  9.28 us
    ppermute x5, waiting for transfers between devices, exchange(): return lax.ppermute(array, ('x', 'core'), pairs)  6.84 us
  transfers between devices with their start and end apart: 10, of which 6 were waited for; matrix products, arithmetic and copies ran while one was open for 0% of the time, Pallas kernels for 6%

profile of v6, /device:TPU:6, one launch (start us, length us, event | category | flops | bytes accessed | tf_op | source)
XLA Modules:
  0.0 123.7 jit_solution(10773884960036464513)
XLA Ops:
  0.0 2.9 %shard_map.28 = bf16[8,15,64,128]{3,2,1,0:T(8,128)(2,1)} custom-call(bf16[2,21,64,512]{3,2,1,0:T(8,128)(2,1)} %tiles.1), custom_call_target="tpu_custom_call" | custom-call | bytes 5505024 | tf_op jit(solution)/shard_map/pallas_call | solution.py:31
  2.9 10.1 %all-to-all-start = ((bf16[8,15,64,128]{3,2,1,0:T(8,128)(2,1)}), bf16[8,15,64,128]{3,2,1,0:T(8,128)(2,1)}, u32[]{:S(2)}, u32[]{:S(2)}) async-start(bf16[8,15,64,128]{3,2,1,0:T(8,128)(2,1)} %shard_map.28), calls=%async_computation | async-start | bytes 3932160 | tf_op jit(solution)/shard_map/all_to_all | solution.py:228
  13.0 5.1 %shard_map.29.own_hbm = f32[6,128,384]{2,1,0:T(8,128)} custom-call(bf16[2,21,64,512]{3,2,1,0:T(8,128)(2,1)} %tiles.1, bf16[3072,384]{1,0:T(8,128)(2,1)} %coeffs_hbm.3), custom_call_target="tpu_custom_call" | custom-call | flops 1056964608 | bytes 5111808 | tf_op jit(solution)/shard_map/pallas_call | solution.py:31
  18.1 18.7 %all-to-all-done.received_hbm = bf16[8,15,64,128]{3,2,1,0:T(8,128)(2,1)} async-done(((bf16[8,15,64,128]{3,2,1,0:T(8,128)(2,1)}), bf16[8,15,64,128]{3,2,1,0:T(8,128)(2,1)}, u32[]{:S(2)}, u32[]{:S(2)}) %all-to-all-start) | async-done | bytes 1966112 | tf_op jit(solution)/shard_map/all_to_all | solution.py:228
  36.8 2.3 %shard_map.30.half_a = bf16[256,768]{1,0:T(8,128)(2,1)S(1)} custom-call(bf16[8,15,64,128]{3,2,1,0:T(8,128)(2,1)} %all-to-all-done.received_hbm, bf16[3072,384]{1,0:T(8,128)(2,1)} %coeffs_hbm.3, f32[6,128,384]{2,1,0:T(8,128)} %shard_map.29.own_hbm), custom_call_target="tpu_custom_call" | custom-call | flops 301989888 | bytes 3145728 | tf_op jit(solution)/shard_map/pallas_call | solution.py:31
  39.1 3.0 %shard_map.31 = (bf16[384,768]{1,0:T(8,128)(2,1)S(1)}, bf16[128,768]{1,0:T(8,128)(2,1)S(1)}) custom-call(bf16[8,15,64,128]{3,2,1,0:T(8,128)(2,1)} %all-to-all-done.received_hbm, bf16[3072,384]{1,0:T(8,128)(2,1)} %coeffs_hbm.3, f32[6,128,384]{2,1,0:T(8,128)} %shard_map.29.own_hbm, bf16[256,768]{1,0:T(8,128)(2,1)S(1)} %shard_map.30.half_a), custom_call_target="tpu_custom_call" | custom-call | flops 452984832 | bytes 3538944 | tf_op jit(solution)/shard_map/pallas_call | solution.py:31
  42.1 4.0 %collective-permute-start.5 = (bf16[384,768]{1,0:T(8,128)(2,1)S(1)}, bf16[384,768]{1,0:T(8,128)(2,1)S(1)}, u32[]{:S(2)}, u32[]{:S(2)}) collective-permute-start(bf16[384,768]{1,0:T(8,128)(2,1)S(1)} %get-tuple-element.9.own), channel_id=1, source_target_pairs={{0,6},{1,3},{2,4},{3,1},{4,2},{5,7},{6,0},{7,5},{8,14},{9,11},{10,... | collective-permute-start | bytes 1769480 | tf_op jit(solution)/shard_map/ppermute | solution.py:266
  46.1 1.9 %collective-permute-start.1 = (bf16[256,768]{1,0:T(8,128)(2,1)S(1)}, bf16[256,768]{1,0:T(8,128)(2,1)S(1)}, u32[]{:S(2)}, u32[]{:S(2)}) collective-permute-start(bf16[256,768]{1,0:T(8,128)(2,1)S(1)} %shard_map.30.half_a), channel_id=1, source_target_pairs={{0,2},{1,7},{2,0},{3,5},{4,6},{5,3},{6,4},{7,1},{8,10},{9,15},{10,... | collective-permute-start | bytes 1179656 | tf_op jit(solution)/shard_map/ppermute | solution.py:266
  48.1 1.9 %collective-permute-start = (bf16[384,768]{1,0:T(8,128)(2,1)S(1)}, bf16[384,768]{1,0:T(8,128)(2,1)S(1)}, u32[]{:S(2)}, u32[]{:S(2)}) collective-permute-start(bf16[384,768]{1,0:T(8,128)(2,1)S(1)} %get-tuple-element.9.own), channel_id=1, source_target_pairs={{0,1},{1,0},{2,3},{3,2},{4,5},{5,4},{6,7},{7,6},{8,9},{9,8},{10,11... | collective-permute-start | bytes 1769480 | tf_op jit(solution)/shard_map/ppermute | solution.py:269
  50.0 3.9 %collective-permute-start.2 = (bf16[128,768]{1,0:T(8,128)(2,1)S(1)}, bf16[128,768]{1,0:T(8,128)(2,1)S(1)}, u32[]{:S(2)}, u32[]{:S(2)}) collective-permute-start(bf16[128,768]{1,0:T(8,128)(2,1)S(1)} %get-tuple-element.10), channel_id=1, source_target_pairs={{0,2},{1,7},{2,0},{3,5},{4,6},{5,3},{6,4},{7,1},{8,10},{9,15},{10,... | collective-permute-start | bytes 589832 | tf_op jit(solution)/shard_map/ppermute | solution.py:266
  53.9 2.8 %collective-permute-done.1.first_a = bf16[256,768]{1,0:T(8,128)(2,1)S(1)} collective-permute-done((bf16[256,768]{1,0:T(8,128)(2,1)S(1)}, bf16[256,768]{1,0:T(8,128)(2,1)S(1)}, u32[]{:S(2)}, u32[]{:S(2)}) %collective-permute-start.1) | collective-permute-done | bytes 393248 | tf_op jit(solution)/shard_map/ppermute | solution.py:266
  56.7 3.0 %collective-permute-start.3 = (bf16[256,768]{1,0:T(8,128)(2,1)S(1)}, bf16[256,768]{1,0:T(8,128)(2,1)S(1)}, u32[]{:S(2)}, u32[]{:S(2)}) collective-permute-start(bf16[256,768]{1,0:T(8,128)(2,1)S(1)} %collective-permute-done.1.first_a), channel_id=1, source_target_pairs={{0,1},{1,0},{2,3},{3,2},{4,5},{5,4},{6,7},{7,6},{8,9},{9,8},{10,11... | collective-permute-start | bytes 1179656 | tf_op jit(solution)/shard_map/ppermute | solution.py:269
  59.8 1.2 collective-permute-done.5.second
  60.9 1.9 %collective-permute-start.6 = (bf16[384,768]{1,0:T(8,128)(2,1)S(1)}, bf16[384,768]{1,0:T(8,128)(2,1)S(1)}, u32[]{:S(2)}, u32[]{:S(2)}) collective-permute-start(bf16[384,768]{1,0:T(8,128)(2,1)S(1)} %collective-permute-done.5.second), channel_id=1, source_target_pairs={{0,1},{1,0},{2,3},{3,2},{4,5},{5,4},{6,7},{7,6},{8,9},{9,8},{10,11... | collective-permute-start | bytes 1769480 | tf_op jit(solution)/shard_map/ppermute | solution.py:269
  62.9 0.0 collective-permute-done.2.first_b
  62.9 2.4 %collective-permute-start.4 = (bf16[128,768]{1,0:T(8,128)(2,1)S(1)}, bf16[128,768]{1,0:T(8,128)(2,1)S(1)}, u32[]{:S(2)}, u32[]{:S(2)}) collective-permute-start(bf16[128,768]{1,0:T(8,128)(2,1)S(1)} %collective-permute-done.2.first_b), channel_id=1, source_target_pairs={{0,1},{1,0},{2,3},{3,2},{4,5},{5,4},{6,7},{7,6},{8,9},{9,8},{10,11... | collective-permute-start | bytes 589832 | tf_op jit(solution)/shard_map/ppermute | solution.py:269
  65.3 1.0 collective-permute-done.4.first_bs
  66.3 0.0 collective-permute-done.3.first_as
  66.3 0.8 shard_map.34
  67.2 3.7 %collective-permute-start.7 = (bf16[8,8,1344]{2,1,0:T(8,128)(2,1)S(1)}, bf16[8,8,1344]{2,1,0:T(8,128)(2,1)S(1)}, u32[]{:S(2)}, u32[]{:S(2)}) collective-permute-start(bf16[8,8,1344]{2,1,0:T(8,128)(2,1)S(1)} %get-tuple-element.11), channel_id=1, source_target_pairs={{0,6},{1,3},{2,4},{3,1},{4,2},{5,7},{6,0},{7,5},{8,14},{9,11},{10,... | collective-permute-start | bytes 516104 | tf_op jit(solution)/shard_map/ppermute | solution.py:266
  70.9 1.9 %collective-permute-start.8 = (bf16[8,8,1344]{2,1,0:T(8,128)(2,1)S(1)}, bf16[8,8,1344]{2,1,0:T(8,128)(2,1)S(1)}, u32[]{:S(2)}, u32[]{:S(2)}) collective-permute-start(bf16[8,8,1344]{2,1,0:T(8,128)(2,1)S(1)} %get-tuple-element.12), channel_id=1, source_target_pairs={{0,7},{1,2},{2,5},{3,0},{4,3},{5,6},{6,1},{7,4},{8,15},{9,10},{10,... | collective-permute-start | bytes 516104 | tf_op jit(solution)/shard_map/ppermute | solution.py:266
  72.8 0.0 collective-permute-done.sib
  72.8 1.2 shard_map.32.near
  74.0 0.9 shard_map.33.late
  74.8 0.9 collective-permute-done.7.far
  75.8 1.9 %collective-permute-done.8.far_s = bf16[8,8,1344]{2,1,0:T(8,128)(2,1)S(1)} collective-permute-done((bf16[8,8,1344]{2,1,0:T(8,128)(2,1)S(1)}, bf16[8,8,1344]{2,1,0:T(8,128)(2,1)S(1)}, u32[]{:S(2)}, u32[]{:S(2)}) %collective-permute-start.8) | collective-permute-done | bytes 172064 | tf_op jit(solution)/shard_map/ppermute | solution.py:266
  77.7 0.0 collective-permute-done.6.second_s
  77.7 0.6 shard_map.35
  78.3 28.0 %all_to_all.15.received = bf16[8,64,1344]{2,1,0:T(8,128)(2,1)S(1)} all-to-all(bf16[8,64,1344]{2,1,0:T(8,128)(2,1)S(1)} %bitcast.3), channel_id=1, replica_groups={{0,64,128,192,256,320,384,448},{8,72,136,200,264,328,392,456},{16,80,14..., dimensions={0} | all-to-all | bytes 2752512 | tf_op jit(solution)/shard_map/all_to_all | solution.py:309
  106.2 0.2 shard_map.36
  106.4 16.5 %all_to_all.16.received = bf16[8,8,1344]{2,1,0:T(8,128)(2,1)S(1)} all-to-all(bf16[8,8,1344]{2,1,0:T(8,128)(2,1)S(1)} %bitcast.4), channel_id=1, replica_groups={{0,8,16,24,32,40,48,56},{64,72,80,88,96,104,112,120},{128,136,144,152,1..., dimensions={0} | all-to-all | bytes 344064 | tf_op jit(solution)/shard_map/all_to_all | solution.py:320
  122.9 0.7 shard_map.37
Async XLA Ops:
  2.9 33.9 %all-to-all-start = ((bf16[8,15,64,128]{3,2,1,0:T(8,128)(2,1)}), bf16[8,15,64,128]{3,2,1,0:T(8,128)(2,1)}, u32[]{:S(2)}, u32[]{:S(2)}) async-start(bf16[8,15,64,128]{3,2,1,0:T(8,128)(2,1)} %shard_map.28), calls=%async_computation | async-start | bytes 3932160 | tf_op jit(solution)/shard_map/all_to_all | solution.py:228
  42.1 18.8 %collective-permute-start.5 = (bf16[384,768]{1,0:T(8,128)(2,1)S(1)}, bf16[384,768]{1,0:T(8,128)(2,1)S(1)}, u32[]{:S(2)}, u32[]{:S(2)}) collective-permute-start(bf16[384,768]{1,0:T(8,128)(2,1)S(1)} %get-tuple-element.9.own), channel_id=1, source_target_pairs={{0,6},{1,3},{2,4},{3,1},{4,2},{5,7},{6,0},{7,5},{8,14},{9,11},{10,... | collective-permute-start | bytes 1769480 | tf_op jit(solution)/shard_map/ppermute | solution.py:266
  46.1 10.6 %collective-permute-start.1 = (bf16[256,768]{1,0:T(8,128)(2,1)S(1)}, bf16[256,768]{1,0:T(8,128)(2,1)S(1)}, u32[]{:S(2)}, u32[]{:S(2)}) collective-permute-start(bf16[256,768]{1,0:T(8,128)(2,1)S(1)} %shard_map.30.half_a), channel_id=1, source_target_pairs={{0,2},{1,7},{2,0},{3,5},{4,6},{5,3},{6,4},{7,1},{8,10},{9,15},{10,... | collective-permute-start | bytes 1179656 | tf_op jit(solution)/shard_map/ppermute | solution.py:266
  48.1 24.8 %collective-permute-start = (bf16[384,768]{1,0:T(8,128)(2,1)S(1)}, bf16[384,768]{1,0:T(8,128)(2,1)S(1)}, u32[]{:S(2)}, u32[]{:S(2)}) collective-permute-start(bf16[384,768]{1,0:T(8,128)(2,1)S(1)} %get-tuple-element.9.own), channel_id=1, source_target_pairs={{0,1},{1,0},{2,3},{3,2},{4,5},{5,4},{6,7},{7,6},{8,9},{9,8},{10,11... | collective-permute-start | bytes 1769480 | tf_op jit(solution)/shard_map/ppermute | solution.py:269
  50.0 12.9 %collective-permute-start.2 = (bf16[128,768]{1,0:T(8,128)(2,1)S(1)}, bf16[128,768]{1,0:T(8,128)(2,1)S(1)}, u32[]{:S(2)}, u32[]{:S(2)}) collective-permute-start(bf16[128,768]{1,0:T(8,128)(2,1)S(1)} %get-tuple-element.10), channel_id=1, source_target_pairs={{0,2},{1,7},{2,0},{3,5},{4,6},{5,3},{6,4},{7,1},{8,10},{9,15},{10,... | collective-permute-start | bytes 589832 | tf_op jit(solution)/shard_map/ppermute | solution.py:266
  56.7 9.6 %collective-permute-start.3 = (bf16[256,768]{1,0:T(8,128)(2,1)S(1)}, bf16[256,768]{1,0:T(8,128)(2,1)S(1)}, u32[]{:S(2)}, u32[]{:S(2)}) collective-permute-start(bf16[256,768]{1,0:T(8,128)(2,1)S(1)} %collective-permute-done.1.first_a), channel_id=1, source_target_pairs={{0,1},{1,0},{2,3},{3,2},{4,5},{5,4},{6,7},{7,6},{8,9},{9,8},{10,11... | collective-permute-start | bytes 1179656 | tf_op jit(solution)/shard_map/ppermute | solution.py:269
  60.9 16.8 %collective-permute-start.6 = (bf16[384,768]{1,0:T(8,128)(2,1)S(1)}, bf16[384,768]{1,0:T(8,128)(2,1)S(1)}, u32[]{:S(2)}, u32[]{:S(2)}) collective-permute-start(bf16[384,768]{1,0:T(8,128)(2,1)S(1)} %collective-permute-done.5.second), channel_id=1, source_target_pairs={{0,1},{1,0},{2,3},{3,2},{4,5},{5,4},{6,7},{7,6},{8,9},{9,8},{10,11... | collective-permute-start | bytes 1769480 | tf_op jit(solution)/shard_map/ppermute | solution.py:269
  62.9 3.5 %collective-permute-start.4 = (bf16[128,768]{1,0:T(8,128)(2,1)S(1)}, bf16[128,768]{1,0:T(8,128)(2,1)S(1)}, u32[]{:S(2)}, u32[]{:S(2)}) collective-permute-start(bf16[128,768]{1,0:T(8,128)(2,1)S(1)} %collective-permute-done.2.first_b), channel_id=1, source_target_pairs={{0,1},{1,0},{2,3},{3,2},{4,5},{5,4},{6,7},{7,6},{8,9},{9,8},{10,11... | collective-permute-start | bytes 589832 | tf_op jit(solution)/shard_map/ppermute | solution.py:269
  67.2 8.6 %collective-permute-start.7 = (bf16[8,8,1344]{2,1,0:T(8,128)(2,1)S(1)}, bf16[8,8,1344]{2,1,0:T(8,128)(2,1)S(1)}, u32[]{:S(2)}, u32[]{:S(2)}) collective-permute-start(bf16[8,8,1344]{2,1,0:T(8,128)(2,1)S(1)} %get-tuple-element.11), channel_id=1, source_target_pairs={{0,6},{1,3},{2,4},{3,1},{4,2},{5,7},{6,0},{7,5},{8,14},{9,11},{10,... | collective-permute-start | bytes 516104 | tf_op jit(solution)/shard_map/ppermute | solution.py:266
  70.9 6.8 %collective-permute-start.8 = (bf16[8,8,1344]{2,1,0:T(8,128)(2,1)S(1)}, bf16[8,8,1344]{2,1,0:T(8,128)(2,1)S(1)}, u32[]{:S(2)}, u32[]{:S(2)}) collective-permute-start(bf16[8,8,1344]{2,1,0:T(8,128)(2,1)S(1)} %get-tuple-element.12), channel_id=1, source_target_pairs={{0,7},{1,2},{2,5},{3,0},{4,3},{5,6},{6,1},{7,4},{8,15},{9,10},{10,... | collective-permute-start | bytes 516104 | tf_op jit(solution)/shard_map/ppermute | solution.py:266

commit v7 on v3

--- a/solution.py
+++ b/solution.py
@@ -126,60 +126,51 @@
     put_rows(values, out, half_a.shape[0])
 
 
-def tiles_kernel(pieces, mine, sib, out_mine, out_sib, base=0):
-    width = mine.shape[0] // NB
-    high = out_mine.shape[1]
+def tiles_kernel(pieces, cols, out):
+    width = cols.shape[0] // NB
+    high = out.shape[1]
     groups = width // high
-    for cols, out in ((sib, out_sib), (mine, out_mine)):
-        right = cols[...]
-        for place, piece in enumerate(pieces):
-            for first, part in piece:
-                full = lax.dot_general(
-                    part[...], right, (((1,), (1,)), ((), ())), preferred_element_type=F32
-                ).astype(BF16)
-                for k in range(part.shape[0] // width):
-                    a = first + k
-                    strip = full[k * width : (k + 1) * width, a * width :]
-                    begin = tile_of(a, a) * width - base
-                    out[place * groups : (place + 1) * groups, :, begin : begin + strip.shape[1]] = strip.reshape(
-                        groups, high, strip.shape[1]
-                    )
+    right = cols[...]
+    for place, piece in enumerate(pieces):
+        for first, part in piece:
+            full = lax.dot_general(
+                part[...], right, (((1,), (1,)), ((), ())), preferred_element_type=F32
+            ).astype(BF16)
+            for k in range(part.shape[0] // width):
+                a = first + k
+                strip = full[k * width : (k + 1) * width, a * width :]
+                begin = tile_of(a, a) * width
+                out[place * groups : (place + 1) * groups, :, begin : begin + strip.shape[1]] = strip.reshape(
+                    groups, high, strip.shape[1]
+                )
 
 
 def near_kernel(own, first_a, first_b, second, sib, out_mine, out_sib):
     pieces = ([(0, own)], [(0, first_a), (CUT, first_b)], [(0, second)])
-    tiles_kernel(pieces, own, sib, out_mine, out_sib)
-
-
-def far_a_kernel(far_a, own, sib, out_mine, out_sib):
-    tiles_kernel(([(0, far_a)],), own, sib, out_mine, out_sib)
-
-
-def far_b_kernel(far_b, own, sib, out_mine, out_sib):
-    base = tile_of(CUT, CUT) * own.shape[0] // NB
-    tiles_kernel(([(CUT, far_b)],), own, sib, out_mine, out_sib, base)
-
-
-def gather_kernel(near, far_a, far_b, near_s, far_as, far_bs, out):
+    tiles_kernel(pieces, sib, out_sib)
+    tiles_kernel(pieces, own, out_mine)
+
+
+def far_kernel(far_a, far_b, cols, out):
+    tiles_kernel(([(0, far_a), (CUT, far_b)],), cols, out)
+
+
+def gather_kernel(near, far, near_s, far_s, out):
     cores = lax.axis_size("core")
     zs, ys = lax.axis_size("z"), lax.axis_size("y")
     x, core = lax.axis_index("x"), lax.axis_index("core")
     even = core == 0
     first, second = jnp.where(even, x ^ 1, x ^ 3), jnp.where(even, x ^ 3, x ^ 1)
-    cut = far_a.shape[2]
-    for places, parity, close, low, high in (
-        ((x, first, second, x ^ 2), core, near, far_a, far_b),
-        ((x, second, first, x ^ 2), 1 - core, near_s, far_as, far_bs),
+    for places, source, parity in (
+        ((x, first, second), near, core),
+        ((x ^ 2,), far, core),
+        ((x, second, first), near_s, 1 - core),
+        ((x ^ 2,), far_s, 1 - core),
     ):
         for at, place in enumerate(places):
             z = place * cores + parity
             for y in range(ys):
-                to = jnp.where(even, z * ys + y, y * zs + z)
-                if at < 3:
-                    out[to] = close[at * ys + y]
-                else:
-                    out[to, :, :cut] = low[y]
-                    out[to, :, cut:] = high[y]
+                out[jnp.where(even, z * ys + y, y * zs + z)] = source[at * ys + y]
 
 
 def sum_of(received):
@@ -270,10 +261,8 @@
     far_b = exchange(first_b, 1)
 
     product = 2 * half.shape[0] ** 2 * half.shape[1]
-    cut = tile_of(CUT, CUT) * width
     near_shape = jax.ShapeDtypeStruct((3 * ys, rows, tile_count * width), BF16)
-    low_shape = jax.ShapeDtypeStruct((ys, rows, cut), BF16)
-    high_shape = jax.ShapeDtypeStruct((ys, rows, tile_count * width - cut), BF16)
+    far_shape = jax.ShapeDtypeStruct((ys, rows, tile_count * width), BF16)
     near, near_s = call(
         near_kernel,
         (near_shape, near_shape),
@@ -283,16 +272,13 @@
         16,
     )
     near_s = lax.ppermute(near_s, "core", swap)
-    far_a, far_as = call(far_a_kernel, (low_shape, low_shape), (far_a, half, sib), 2 * product, 6 * half.size, 12)
-    far_as = lax.ppermute(far_as, "core", swap)
-    far_b, far_bs = call(
-        far_b_kernel, (high_shape, high_shape), (far_b, half, sib), product, 6 * half.size, 12
-    )
-    far_bs = lax.ppermute(far_bs, "core", swap)
+    far_s = call(far_kernel, far_shape, (far_a, far_b, sib), product, 4 * half.size, 12)
+    far_s = lax.ppermute(far_s, "core", swap)
+    far = call(far_kernel, far_shape, (far_a, far_b, half), product, 4 * half.size, 12)
     partial = call(
         gather_kernel,
         jax.ShapeDtypeStruct((zs * ys, rows, tile_count * width), BF16),
-        (near, far_a, far_b, near_s, far_as, far_bs),
+        (near, far, near_s, far_s),
         0,
         8 * near.size,
         12,

time: 126 us -> 126 us (level)
  waiting for transfers between devices: 31.2 us -> 33.5 us
  starting transfers between devices: 28 us -> 26.1 us
    ppermute x5, waiting for transfers between devices: 9.31 us -> 11.9 us  [exchange(): lax.ppermute(array, ('x', 'core'), [(a * cores + c, b * cores + d) for (a...]
    ppermute x2 -> x1, starting transfers between devices: 3.84 us -> 1.92 us  [body(): far_s = lax.ppermute(far_s, 'core', swap)]
  transfers between devices with their start and end apart: 10 -> 9, of which waited for: 4 -> 4; matrix products, arithmetic and copies ran while one was open for 0% -> 0% of each run, Pallas kernels for 6% -> 6%
where the time goes in v7:
time: 126 us
  blocking collectives  48.7 us (39%)
  waiting for transfers between devices  33.5 us (27%)
  starting transfers between devices  26.1 us (21%)
  Pallas kernels  17.4 us (14%)
    all_to_all x1, blocking collectives, body(): lax.all_to_all(partial.reshape(zs, ys * rows, tile_count * width), AXES,...  33.2 us
    all_to_all x1, waiting for transfers between devices, body(): received = lax.all_to_all(packed, ('x', 'core'), 0, 0)  20.7 us
    pallas_call x10, Pallas kernels, call(): pl.pallas_call(kernel, out_shape=out_shape, compiler_params=pltpu.Compile...  17.4 us
    all_to_all x1, blocking collectives, body(): lax.all_to_all(summed.reshape(ys, rows, tile_count * width), AXES, 0, 0,...  15.5 us
    ppermute x5, starting transfers between devices, exchange(): lax.ppermute(array, ('x', 'core'), [(a * cores + c, b * cores + d) for (a...  15.5 us
    ppermute x5, waiting for transfers between devices, exchange(): lax.ppermute(array, ('x', 'core'), [(a * cores + c, b * cores + d) for (a...  11.9 us
    all_to_all x1, starting transfers between devices, body(): received = lax.all_to_all(packed, ('x', 'core'), 0, 0)  4.36 us
  transfers between devices with their start and end apart: 9, of which 4 were waited for; matrix products, arithmetic and copies ran while one was open for 0% of the time, Pallas kernels for 6%

profile of v7, /device:TPU:8, one launch (start us, length us, event | category | flops | bytes accessed | tf_op | source)
XLA Modules:
  0.0 125.9 jit_solution(337537522326908807)
XLA Ops:
  0.0 2.9 %shard_map.28 = bf16[8,15,64,128]{3,2,1,0:T(8,128)(2,1)} custom-call(bf16[2,21,64,512]{3,2,1,0:T(8,128)(2,1)} %tiles.1), custom_call_target="tpu_custom_call" | custom-call | bytes 5505024 | tf_op jit(solution)/shard_map/pallas_call | solution.py:31
  2.9 4.4 %all-to-all-start = ((bf16[8,15,64,128]{3,2,1,0:T(8,128)(2,1)}), bf16[8,15,64,128]{3,2,1,0:T(8,128)(2,1)}, u32[]{:S(2)}, u32[]{:S(2)}) async-start(bf16[8,15,64,128]{3,2,1,0:T(8,128)(2,1)} %shard_map.28), calls=%async_computation | async-start | bytes 3932160 | tf_op jit(solution)/shard_map/all_to_all | solution.py:217
  7.3 5.1 %shard_map.29.own_hbm = f32[6,128,384]{2,1,0:T(8,128)} custom-call(bf16[2,21,64,512]{3,2,1,0:T(8,128)(2,1)} %tiles.1, bf16[3072,384]{1,0:T(8,128)(2,1)} %coeffs_hbm.3), custom_call_target="tpu_custom_call" | custom-call | flops 1056964608 | bytes 5111808 | tf_op jit(solution)/shard_map/pallas_call | solution.py:31
  12.4 20.7 %all-to-all-done.received_hbm = bf16[8,15,64,128]{3,2,1,0:T(8,128)(2,1)} async-done(((bf16[8,15,64,128]{3,2,1,0:T(8,128)(2,1)}), bf16[8,15,64,128]{3,2,1,0:T(8,128)(2,1)}, u32[]{:S(2)}, u32[]{:S(2)}) %all-to-all-start) | async-done | bytes 1966112 | tf_op jit(solution)/shard_map/all_to_all | solution.py:217
  33.1 2.3 %shard_map.30.half_a = bf16[256,768]{1,0:T(8,128)(2,1)S(1)} custom-call(bf16[8,15,64,128]{3,2,1,0:T(8,128)(2,1)} %all-to-all-done.received_hbm, bf16[3072,384]{1,0:T(8,128)(2,1)} %coeffs_hbm.3, f32[6,128,384]{2,1,0:T(8,128)} %shard_map.29.own_hbm), custom_call_target="tpu_custom_call" | custom-call | flops 301989888 | bytes 3145728 | tf_op jit(solution)/shard_map/pallas_call | solution.py:31
  35.4 3.0 %shard_map.31 = (bf16[384,768]{1,0:T(8,128)(2,1)S(1)}, bf16[128,768]{1,0:T(8,128)(2,1)S(1)}) custom-call(bf16[8,15,64,128]{3,2,1,0:T(8,128)(2,1)} %all-to-all-done.received_hbm, bf16[3072,384]{1,0:T(8,128)(2,1)} %coeffs_hbm.3, f32[6,128,384]{2,1,0:T(8,128)} %shard_map.29.own_hbm, bf16[256,768]{1,0:T(8,128)(2,1)S(1)} %shard_map.30.half_a), custom_call_target="tpu_custom_call" | custom-call | flops 452984832 | bytes 3538944 | tf_op jit(solution)/shard_map/pallas_call | solution.py:31
  38.5 1.9 %collective-permute-start.3 = (bf16[384,768]{1,0:T(8,128)(2,1)S(1)}, bf16[384,768]{1,0:T(8,128)(2,1)S(1)}, u32[]{:S(2)}, u32[]{:S(2)}) collective-permute-start(bf16[384,768]{1,0:T(8,128)(2,1)S(1)} %get-tuple-element.9.own.cols), channel_id=1, source_target_pairs={{0,1},{1,0},{2,3},{3,2},{4,5},{5,4},{6,7},{7,6},{8,9},{9,8},{10,11... | collective-permute-start | bytes 1769480 | tf_op jit(solution)/shard_map/ppermute | solution.py:260
  40.4 3.1 %collective-permute-start.2 = (bf16[384,768]{1,0:T(8,128)(2,1)S(1)}, bf16[384,768]{1,0:T(8,128)(2,1)S(1)}, u32[]{:S(2)}, u32[]{:S(2)}) collective-permute-start(bf16[384,768]{1,0:T(8,128)(2,1)S(1)} %get-tuple-element.9.own.cols), channel_id=1, source_target_pairs={{0,6},{1,3},{2,4},{3,1},{4,2},{5,7},{6,0},{7,5},{8,14},{9,11},{10,... | collective-permute-start | bytes 1769480 | tf_op jit(solution)/shard_map/ppermute | solution.py:251
  43.5 1.9 %collective-permute-start = (bf16[256,768]{1,0:T(8,128)(2,1)S(1)}, bf16[256,768]{1,0:T(8,128)(2,1)S(1)}, u32[]{:S(2)}, u32[]{:S(2)}) collective-permute-start(bf16[256,768]{1,0:T(8,128)(2,1)S(1)} %shard_map.30.half_a), channel_id=1, source_target_pairs={{0,2},{1,7},{2,0},{3,5},{4,6},{5,3},{6,4},{7,1},{8,10},{9,15},{10,... | collective-permute-start | bytes 1179656 | tf_op jit(solution)/shard_map/ppermute | solution.py:251
  45.4 3.9 %collective-permute-start.1 = (bf16[128,768]{1,0:T(8,128)(2,1)S(1)}, bf16[128,768]{1,0:T(8,128)(2,1)S(1)}, u32[]{:S(2)}, u32[]{:S(2)}) collective-permute-start(bf16[128,768]{1,0:T(8,128)(2,1)S(1)} %get-tuple-element.10), channel_id=1, source_target_pairs={{0,2},{1,7},{2,0},{3,5},{4,6},{5,3},{6,4},{7,1},{8,10},{9,15},{10,... | collective-permute-start | bytes 589832 | tf_op jit(solution)/shard_map/ppermute | solution.py:251
  49.3 6.6 %collective-permute-done.first_a = bf16[256,768]{1,0:T(8,128)(2,1)S(1)} collective-permute-done((bf16[256,768]{1,0:T(8,128)(2,1)S(1)}, bf16[256,768]{1,0:T(8,128)(2,1)S(1)}, u32[]{:S(2)}, u32[]{:S(2)}) %collective-permute-start) | collective-permute-done | bytes 393248 | tf_op jit(solution)/shard_map/ppermute | solution.py:251
  55.9 3.1 %collective-permute-start.4 = (bf16[256,768]{1,0:T(8,128)(2,1)S(1)}, bf16[256,768]{1,0:T(8,128)(2,1)S(1)}, u32[]{:S(2)}, u32[]{:S(2)}) collective-permute-start(bf16[256,768]{1,0:T(8,128)(2,1)S(1)} %collective-permute-done.first_a), channel_id=1, source_target_pairs={{0,6},{1,3},{2,4},{3,1},{4,2},{5,7},{6,0},{7,5},{8,14},{9,11},{10,... | collective-permute-start | bytes 1179656 | tf_op jit(solution)/shard_map/ppermute | solution.py:251
  59.0 0.0 collective-permute-done.1.first_b
  59.0 0.0 collective-permute-done.3.sib.cols
  59.0 0.0 collective-permute-done.2.second
  59.0 2.0 %shard_map.32 = (bf16[24,8,1344]{2,1,0:T(8,128)(2,1)S(1)}, bf16[24,8,1344]{2,1,0:T(8,128)(2,1)S(1)}) custom-call(bf16[384,768]{1,0:T(8,128)(2,1)S(1)} %get-tuple-element.9.own.cols, bf16[256,768]{1,0:T(8,128)(2,1)S(1)} %collective-permute-done.first_a, bf16[128,768]{1,0:T(8,128)(2,1)S(1)} %collective-permute-done.1.first_b, ...), custom_call_target="tpu_custom_call" | custom-call | flops 1358954496 | bytes 2359296 | tf_op jit(solution)/shard_map/pallas_call | solution.py:31
  61.0 2.4 %collective-permute-start.6 = (bf16[24,8,1344]{2,1,0:T(8,128)(2,1)S(1)}, bf16[24,8,1344]{2,1,0:T(8,128)(2,1)S(1)}, u32[]{:S(2)}, u32[]{:S(2)}) collective-permute-start(bf16[24,8,1344]{2,1,0:T(8,128)(2,1)S(1)} %get-tuple-element.12), channel_id=1, source_target_pairs={{0,1},{1,0},{2,3},{3,2},{4,5},{5,4},{6,7},{7,6},{8,9},{9,8},{10,11... | collective-permute-start | bytes 1548296 | tf_op jit(solution)/shard_map/ppermute | solution.py:274
  63.4 3.5 %collective-permute-start.5 = (bf16[128,768]{1,0:T(8,128)(2,1)S(1)}, bf16[128,768]{1,0:T(8,128)(2,1)S(1)}, u32[]{:S(2)}, u32[]{:S(2)}) collective-permute-start(bf16[128,768]{1,0:T(8,128)(2,1)S(1)} %collective-permute-done.1.first_b), channel_id=1, source_target_pairs={{0,6},{1,3},{2,4},{3,1},{4,2},{5,7},{6,0},{7,5},{8,14},{9,11},{10,... | collective-permute-start | bytes 589832 | tf_op jit(solution)/shard_map/ppermute | solution.py:251
  66.9 5.3 %collective-permute-done.5.far_b = bf16[128,768]{1,0:T(8,128)(2,1)S(1)} collective-permute-done((bf16[128,768]{1,0:T(8,128)(2,1)S(1)}, bf16[128,768]{1,0:T(8,128)(2,1)S(1)}, u32[]{:S(2)}, u32[]{:S(2)}) %collective-permute-start.5) | collective-permute-done | bytes 196640 | tf_op jit(solution)/shard_map/ppermute | solution.py:251
  72.2 0.0 collective-permute-done.4.far_a
  72.2 0.5 shard_map.34
  72.7 1.9 %collective-permute-start.7 = (bf16[8,8,1344]{2,1,0:T(8,128)(2,1)S(1)}, bf16[8,8,1344]{2,1,0:T(8,128)(2,1)S(1)}, u32[]{:S(2)}, u32[]{:S(2)}) collective-permute-start(bf16[8,8,1344]{2,1,0:T(8,128)(2,1)S(1)} %shard_map.34), channel_id=1, source_target_pairs={{0,1},{1,0},{2,3},{3,2},{4,5},{5,4},{6,7},{7,6},{8,9},{9,8},{10,11... | collective-permute-start | bytes 516104 | tf_op jit(solution)/shard_map/ppermute | solution.py:276
  74.6 0.5 shard_map.33.far
  75.1 0.9 collective-permute-done.7.far_s
  76.0 0.0 collective-permute-done.6.near_s
  76.0 0.2 shard_map.35
  76.2 33.2 %all_to_all.15.received = bf16[8,64,1344]{2,1,0:T(8,128)(2,1)S(1)} all-to-all(bf16[8,64,1344]{2,1,0:T(8,128)(2,1)S(1)} %bitcast.3), channel_id=1, replica_groups={{0,64,128,192,256,320,384,448},{8,72,136,200,264,328,392,456},{16,80,14..., dimensions={0} | all-to-all | bytes 2752512 | tf_op jit(solution)/shard_map/all_to_all | solution.py:290
  109.4 0.2 shard_map.36
  109.6 15.5 %all_to_all.16.received = bf16[8,8,1344]{2,1,0:T(8,128)(2,1)S(1)} all-to-all(bf16[8,8,1344]{2,1,0:T(8,128)(2,1)S(1)} %bitcast.4), channel_id=1, replica_groups={{0,8,16,24,32,40,48,56},{64,72,80,88,96,104,112,120},{128,136,144,152,1..., dimensions={0} | all-to-all | bytes 344064 | tf_op jit(solution)/shard_map/all_to_all | solution.py:301
  125.1 0.7 shard_map.37
Async XLA Ops:
  2.9 30.2 %all-to-all-start = ((bf16[8,15,64,128]{3,2,1,0:T(8,128)(2,1)}), bf16[8,15,64,128]{3,2,1,0:T(8,128)(2,1)}, u32[]{:S(2)}, u32[]{:S(2)}) async-start(bf16[8,15,64,128]{3,2,1,0:T(8,128)(2,1)} %shard_map.28), calls=%async_computation | async-start | bytes 3932160 | tf_op jit(solution)/shard_map/all_to_all | solution.py:217
  38.5 20.5 %collective-permute-start.3 = (bf16[384,768]{1,0:T(8,128)(2,1)S(1)}, bf16[384,768]{1,0:T(8,128)(2,1)S(1)}, u32[]{:S(2)}, u32[]{:S(2)}) collective-permute-start(bf16[384,768]{1,0:T(8,128)(2,1)S(1)} %get-tuple-element.9.own.cols), channel_id=1, source_target_pairs={{0,1},{1,0},{2,3},{3,2},{4,5},{5,4},{6,7},{7,6},{8,9},{9,8},{10,11... | collective-permute-start | bytes 1769480 | tf_op jit(solution)/shard_map/ppermute | solution.py:260
  40.4 18.6 %collective-permute-start.2 = (bf16[384,768]{1,0:T(8,128)(2,1)S(1)}, bf16[384,768]{1,0:T(8,128)(2,1)S(1)}, u32[]{:S(2)}, u32[]{:S(2)}) collective-permute-start(bf16[384,768]{1,0:T(8,128)(2,1)S(1)} %get-tuple-element.9.own.cols), channel_id=1, source_target_pairs={{0,6},{1,3},{2,4},{3,1},{4,2},{5,7},{6,0},{7,5},{8,14},{9,11},{10,... | collective-permute-start | bytes 1769480 | tf_op jit(solution)/shard_map/ppermute | solution.py:251
  43.5 12.4 %collective-permute-start = (bf16[256,768]{1,0:T(8,128)(2,1)S(1)}, bf16[256,768]{1,0:T(8,128)(2,1)S(1)}, u32[]{:S(2)}, u32[]{:S(2)}) collective-permute-start(bf16[256,768]{1,0:T(8,128)(2,1)S(1)} %shard_map.30.half_a), channel_id=1, source_target_pairs={{0,2},{1,7},{2,0},{3,5},{4,6},{5,3},{6,4},{7,1},{8,10},{9,15},{10,... | collective-permute-start | bytes 1179656 | tf_op jit(solution)/shard_map/ppermute | solution.py:251
  45.4 13.6 %collective-permute-start.1 = (bf16[128,768]{1,0:T(8,128)(2,1)S(1)}, bf16[128,768]{1,0:T(8,128)(2,1)S(1)}, u32[]{:S(2)}, u32[]{:S(2)}) collective-permute-start(bf16[128,768]{1,0:T(8,128)(2,1)S(1)} %get-tuple-element.10), channel_id=1, source_target_pairs={{0,2},{1,7},{2,0},{3,5},{4,6},{5,3},{6,4},{7,1},{8,10},{9,15},{10,... | collective-permute-start | bytes 589832 | tf_op jit(solution)/shard_map/ppermute | solution.py:251
  55.9 16.3 %collective-permute-start.4 = (bf16[256,768]{1,0:T(8,128)(2,1)S(1)}, bf16[256,768]{1,0:T(8,128)(2,1)S(1)}, u32[]{:S(2)}, u32[]{:S(2)}) collective-permute-start(bf16[256,768]{1,0:T(8,128)(2,1)S(1)} %collective-permute-done.first_a), channel_id=1, source_target_pairs={{0,6},{1,3},{2,4},{3,1},{4,2},{5,7},{6,0},{7,5},{8,14},{9,11},{10,... | collective-permute-start | bytes 1179656 | tf_op jit(solution)/shard_map/ppermute | solution.py:251
  61.0 15.0 %collective-permute-start.6 = (bf16[24,8,1344]{2,1,0:T(8,128)(2,1)S(1)}, bf16[24,8,1344]{2,1,0:T(8,128)(2,1)S(1)}, u32[]{:S(2)}, u32[]{:S(2)}) collective-permute-start(bf16[24,8,1344]{2,1,0:T(8,128)(2,1)S(1)} %get-tuple-element.12), channel_id=1, source_target_pairs={{0,1},{1,0},{2,3},{3,2},{4,5},{5,4},{6,7},{7,6},{8,9},{9,8},{10,11... | collective-permute-start | bytes 1548296 | tf_op jit(solution)/shard_map/ppermute | solution.py:274
  63.4 8.8 %collective-permute-start.5 = (bf16[128,768]{1,0:T(8,128)(2,1)S(1)}, bf16[128,768]{1,0:T(8,128)(2,1)S(1)}, u32[]{:S(2)}, u32[]{:S(2)}) collective-permute-start(bf16[128,768]{1,0:T(8,128)(2,1)S(1)} %collective-permute-done.1.first_b), channel_id=1, source_target_pairs={{0,6},{1,3},{2,4},{3,1},{4,2},{5,7},{6,0},{7,5},{8,14},{9,11},{10,... | collective-permute-start | bytes 589832 | tf_op jit(solution)/shard_map/ppermute | solution.py:251
  72.7 3.3 %collective-permute-start.7 = (bf16[8,8,1344]{2,1,0:T(8,128)(2,1)S(1)}, bf16[8,8,1344]{2,1,0:T(8,128)(2,1)S(1)}, u32[]{:S(2)}, u32[]{:S(2)}) collective-permute-start(bf16[8,8,1344]{2,1,0:T(8,128)(2,1)S(1)} %shard_map.34), channel_id=1, source_target_pairs={{0,1},{1,0},{2,3},{3,2},{4,5},{5,4},{6,7},{7,6},{8,9},{9,8},{10,11... | collective-permute-start | bytes 516104 | tf_op jit(solution)/shard_map/ppermute | solution.py:276

commit v8 on v2

--- a/solution.py
+++ b/solution.py
@@ -72,7 +72,7 @@
         out[m] = part[m]
 
 
-def lower_kernel(received_hbm, coeffs_hbm, own_hbm, out, out_a, out_b, received, coeffs, own, sems):
+def lower_kernel(received_hbm, coeffs, own_hbm, out, out_a, out_b, received, own, sems):
     size = received.shape[0] * received.shape[2]
     lanes = received.shape[3]
     half = lanes // 2
@@ -80,23 +80,13 @@
     loads = []
     for a in range(NB - 1):
         tiles = pl.ds(OFF_AT[a, a + 1], NB - 1 - a)
-        rows = pl.ds(a * size, size)
-        loads.append(
-            (
-                pltpu.make_async_copy(received_hbm.at[:, tiles], received.at[:, tiles], sems.at[0, a]),
-                pltpu.make_async_copy(coeffs_hbm.at[rows], coeffs.at[rows], sems.at[1, a]),
-            )
-        )
-    loads.append((pltpu.make_async_copy(own_hbm, own, sems.at[0, NB - 1]),))
-    for load in loads[0] + loads[1]:
+        loads.append(pltpu.make_async_copy(received_hbm.at[:, tiles], received.at[:, tiles], sems.at[a]))
+    loads.append(pltpu.make_async_copy(own_hbm, own, sems.at[NB - 1]))
+    for load in loads:
         load.start()
     sums = [None] * NB
     for a in range(NB - 1):
-        for load in loads[a]:
-            load.wait()
-        if a + 2 < NB:
-            for load in loads[a + 2]:
-                load.start()
+        loads[a].wait()
         lhs = jnp.concatenate(
             [received[:, OFF_AT[a, b]].reshape(size, lanes) for b in range(a + 1, NB)], axis=1
         )
@@ -107,7 +97,7 @@
             at = (b - a - 1) * lanes
             term = part[at : at + lanes]
             sums[b] = term if sums[b] is None else sums[b] + term
-    loads[NB - 1][0].wait()
+    loads[NB - 1].wait()
     for b in range(NB):
         both = own[b] if sums[b] is None else sums[b] + own[b]
         both = both.astype(BF16)
@@ -116,33 +106,34 @@
             ref[at * half : (at + 1) * half, occ:] = both[half:]
 
 
-def tiles_kernel(pieces, mine, sib, out_mine, out_sib):
-    width = mine.shape[0] // NB
-    high = out_mine.shape[1]
+def products(pieces, cols, out):
+    width = cols.shape[0] // NB
+    high = out.shape[1]
     groups = width // high
-    for cols, out in ((mine, out_mine), (sib, out_sib)):
-        right = cols[...]
-        for place, piece in enumerate(pieces):
-            a = 0
-            for part in piece:
-                full = lax.dot_general(
-                    part[...], right, (((1,), (1,)), ((), ())), preferred_element_type=F32
-                ).astype(BF16)
-                for k in range(part.shape[0] // width):
-                    strip = full[k * width : (k + 1) * width, a * width :]
-                    begin = tile_of(a, a) * width
-                    out[place * groups : (place + 1) * groups, :, begin : begin + strip.shape[1]] = strip.reshape(
-                        groups, high, strip.shape[1]
-                    )
-                    a += 1
+    right = cols[...]
+    for place, piece in enumerate(pieces):
+        a = 0
+        for part in piece:
+            full = lax.dot_general(
+                part[...], right, (((1,), (1,)), ((), ())), preferred_element_type=F32
+            ).astype(BF16)
+            for k in range(part.shape[0] // width):
+                strip = full[k * width : (k + 1) * width, a * width :]
+                begin = tile_of(a, a) * width
+                out[place * groups : (place + 1) * groups, :, begin : begin + strip.shape[1]] = strip.reshape(
+                    groups, high, strip.shape[1]
+                )
+                a += 1
 
 
 def near_kernel(own, first_a, first_b, second, sib, out_mine, out_sib):
-    tiles_kernel(((own,), (first_a, first_b), (second,)), own, sib, out_mine, out_sib)
-
-
-def far_kernel(far_a, far_b, own, sib, out_mine, out_sib):
-    tiles_kernel(((far_a, far_b),), own, sib, out_mine, out_sib)
+    pieces = ((own,), (first_a, first_b), (second,))
+    products(pieces, sib, out_sib)
+    products(pieces, own, out_mine)
+
+
+def far_kernel(far_a, far_b, cols, out):
+    products(((far_a, far_b),), cols, out)
 
 
 def gather_kernel(near, far, near_s, far_s, out):
@@ -171,7 +162,7 @@
 
 
 def sum_kernel(received, out):
-    out[...] = sum_of(received)
+    out[...] = sum_of(received).astype(out.dtype)
 
 
 def last_kernel(received, out):
@@ -211,7 +202,7 @@
         (integrals, orbitals),
         flops * tile_count,
         2 * integrals.size + 2 * orbitals.size,
-        63,
+        52,
     )
     whole = jax.ShapeDtypeStruct((NB * width, slabs * occ), BF16)
     side = jax.ShapeDtypeStruct((NB // 2 * width, slabs * occ), BF16)
@@ -219,16 +210,15 @@
     half, half_a, half_b = call(
         lower_kernel,
         (whole, side, side),
-        (in_hbm(received), in_hbm(orbitals), in_hbm(own)),
+        (in_hbm(received), orbitals, in_hbm(own)),
         flops * len(OFF),
         2 * received.size + 2 * orbitals.size,
-        20,
-        in_specs=[ANY] * 3,
+        16,
+        in_specs=[ANY, VMEM, ANY],
         scratch_shapes=[
             pltpu.VMEM(received.shape, BF16),
-            pltpu.VMEM(orbitals.shape, BF16),
             pltpu.VMEM(own.shape, F32),
-            pltpu.SemaphoreType.DMA((2, NB)),
+            pltpu.SemaphoreType.DMA((NB,)),
         ],
     )
 
@@ -256,8 +246,9 @@
         16,
     )
     near_s = lax.ppermute(near_s, "core", swap)
-    far, far_s = call(far_kernel, (far_shape, far_shape), (far_a, far_b, half, sib), 2 * product, 6 * half.size, 12)
+    far_s = call(far_kernel, far_shape, (far_a, far_b, sib), product, 4 * half.size, 12)
     far_s = lax.ppermute(far_s, "core", swap)
+    far = call(far_kernel, far_shape, (far_a, far_b, half), product, 4 * half.size, 12)
     partial = call(
         gather_kernel,
         jax.ShapeDtypeStruct((zs * ys, rows, tile_count * width), BF16),
@@ -275,7 +266,7 @@
     )
     summed = call(
         sum_kernel,
-        jax.ShapeDtypeStruct(arrived.shape[1:], F32),
+        jax.ShapeDtypeStruct(arrived.shape[1:], BF16),
         (arrived,),
         arrived.size,
         2 * arrived.size,

time: 132 us -> 129 us (0.977)
  blocking collectives: 46.4 us -> 44.5 us
  Pallas kernels: 16.4 us -> 14.7 us
    all_to_all x1, blocking collectives: 18.4 us -> 16.5 us  [body(): lax.all_to_all(summed.reshape(ys, rows, tile_count * width), AXES, 0, 0,...]
    pallas_call x8 -> x9, Pallas kernels: 16.4 us -> 14.7 us  [call(): pl.pallas_call(kernel, out_shape=out_shape, compiler_params=pltpu.Compile...]
  transfers between devices with their start and end apart: 9 -> 9, of which waited for: 7 -> 7; matrix products, arithmetic and copies ran while one was open for 0% -> 0% of each run, Pallas kernels for 5% -> 4%
where the time goes in v8:
time: 129 us; the launch traced here: 128 us
  blocking collectives  44.5 us (34%)
  waiting for transfers between devices  34.1 us (26%)
  starting transfers between devices  34 us (26%)
  Pallas kernels  14.7 us (11%)
    all_to_all x1, blocking collectives, body(): lax.all_to_all(partial.reshape(zs, ys * rows, tile_count * width), AXES,...  27.9 us
    all_to_all x1, waiting for transfers between devices, body(): received = lax.all_to_all(packed, ('x', 'core'), 0, 0)  18.5 us
    ppermute x5, starting transfers between devices, exchange(): lax.ppermute(array, ('x', 'core'), [(a * cores + c, b * cores + d) for (a...  16.9 us
    all_to_all x1, blocking collectives, body(): lax.all_to_all(summed.reshape(ys, rows, tile_count * width), AXES, 0, 0,...  16.5 us
    ppermute x5, waiting for transfers between devices, exchange(): lax.ppermute(array, ('x', 'core'), [(a * cores + c, b * cores + d) for (a...  14.7 us
    pallas_call x9, Pallas kernels, call(): pl.pallas_call(kernel, out_shape=out_shape, compiler_params=pltpu.Compile...  14.7 us
    all_to_all x1, starting transfers between devices, body(): received = lax.all_to_all(packed, ('x', 'core'), 0, 0)  10.1 us
    ppermute x1, starting transfers between devices, body(): near_s = lax.ppermute(near_s, 'core', swap)  3.19 us
  transfers between devices with their start and end apart: 9, of which 7 were waited for; matrix products, arithmetic and copies ran while one was open for 0% of the time, Pallas kernels for 4%

profile of v8, /device:TPU:6, one launch (start us, length us, event | category | flops | bytes accessed | tf_op | source)
XLA Modules:
  0.0 128.3 jit_solution(18195331292381828567)
XLA Ops:
  0.0 2.7 %shard_map.28 = bf16[8,15,64,128]{3,2,1,0:T(8,128)(2,1)} custom-call(bf16[2,21,64,512]{3,2,1,0:T(8,128)(2,1)} %tiles.1), custom_call_target="tpu_custom_call" | custom-call | bytes 5505024 | tf_op jit(solution)/shard_map/pallas_call | solution.py:30
  2.7 10.1 %all-to-all-start = ((bf16[8,15,64,128]{3,2,1,0:T(8,128)(2,1)}), bf16[8,15,64,128]{3,2,1,0:T(8,128)(2,1)}, u32[]{:S(2)}, u32[]{:S(2)}) async-start(bf16[8,15,64,128]{3,2,1,0:T(8,128)(2,1)} %shard_map.28), calls=%async_computation | async-start | bytes 3932160 | tf_op jit(solution)/shard_map/all_to_all | solution.py:198
  12.8 0.0 copy-start
  12.8 4.2 %shard_map.29.own_hbm = f32[6,128,384]{2,1,0:T(8,128)S(1)} custom-call(bf16[2,21,64,512]{3,2,1,0:T(8,128)(2,1)} %tiles.1, bf16[3072,384]{1,0:T(8,128)(2,1)} %coeffs.3), custom_call_target="tpu_custom_call" | custom-call | flops 1056964608 | bytes 5111808 | tf_op jit(solution)/shard_map/pallas_call | solution.py:30
  17.0 0.0 copy-start.1
  17.0 1.0 copy-done.1
  18.0 18.5 %all-to-all-done.received_hbm = bf16[8,15,64,128]{3,2,1,0:T(8,128)(2,1)} async-done(((bf16[8,15,64,128]{3,2,1,0:T(8,128)(2,1)}), bf16[8,15,64,128]{3,2,1,0:T(8,128)(2,1)}, u32[]{:S(2)}, u32[]{:S(2)}) %all-to-all-start) | async-done | bytes 1966112 | tf_op jit(solution)/shard_map/all_to_all | solution.py:198
  36.6 0.0 copy-done
  36.6 3.2 %shard_map.30 = (bf16[384,768]{1,0:T(8,128)(2,1)S(1)}, bf16[192,768]{1,0:T(8,128)(2,1)S(1)}, bf16[192,768]{1,0:T(8,128)(2,1)S(1)}) custom-call(bf16[8,15,64,128]{3,2,1,0:T(8,128)(2,1)} %all-to-all-done.received_hbm, bf16[3072,384]{1,0:T(8,128)(2,1)S(1)} %copy-done, f32[6,128,384]{2,1,0:T(8,128)} %copy-done.1), custom_call_target="tpu_custom_call" | custom-call | flops 754974720 | bytes 4325376 | tf_op jit(solution)/shard_map/pallas_call | solution.py:30
  39.8 1.9 %collective-permute-start.3 = (bf16[384,768]{1,0:T(8,128)(2,1)S(1)}, bf16[384,768]{1,0:T(8,128)(2,1)S(1)}, u32[]{:S(2)}, u32[]{:S(2)}) collective-permute-start(bf16[384,768]{1,0:T(8,128)(2,1)S(1)} %get-tuple-element.10.own.cols), channel_id=1, source_target_pairs={{0,1},{1,0},{2,3},{3,2},{4,5},{5,4},{6,7},{7,6},{8,9},{9,8},{10,11... | collective-permute-start | bytes 1769480 | tf_op jit(solution)/shard_map/ppermute | solution.py:234
  41.8 4.0 %collective-permute-start.2 = (bf16[384,768]{1,0:T(8,128)(2,1)S(1)}, bf16[384,768]{1,0:T(8,128)(2,1)S(1)}, u32[]{:S(2)}, u32[]{:S(2)}) collective-permute-start(bf16[384,768]{1,0:T(8,128)(2,1)S(1)} %get-tuple-element.10.own.cols), channel_id=1, source_target_pairs={{0,6},{1,3},{2,4},{3,1},{4,2},{5,7},{6,0},{7,5},{8,14},{9,11},{10,... | collective-permute-start | bytes 1769480 | tf_op jit(solution)/shard_map/ppermute | solution.py:227
  45.8 1.9 %collective-permute-start = (bf16[192,768]{1,0:T(8,128)(2,1)S(1)}, bf16[192,768]{1,0:T(8,128)(2,1)S(1)}, u32[]{:S(2)}, u32[]{:S(2)}) collective-permute-start(bf16[192,768]{1,0:T(8,128)(2,1)S(1)} %get-tuple-element.11), channel_id=1, source_target_pairs={{0,2},{1,7},{2,0},{3,5},{4,6},{5,3},{6,4},{7,1},{8,10},{9,15},{10,... | collective-permute-start | bytes 884744 | tf_op jit(solution)/shard_map/ppermute | solution.py:227
  47.7 3.9 %collective-permute-start.1 = (bf16[192,768]{1,0:T(8,128)(2,1)S(1)}, bf16[192,768]{1,0:T(8,128)(2,1)S(1)}, u32[]{:S(2)}, u32[]{:S(2)}) collective-permute-start(bf16[192,768]{1,0:T(8,128)(2,1)S(1)} %get-tuple-element.12), channel_id=1, source_target_pairs={{0,2},{1,7},{2,0},{3,5},{4,6},{5,3},{6,4},{7,1},{8,10},{9,15},{10,... | collective-permute-start | bytes 884744 | tf_op jit(solution)/shard_map/ppermute | solution.py:227
  51.6 4.6 %collective-permute-done.first_a = bf16[192,768]{1,0:T(8,128)(2,1)S(1)} collective-permute-done((bf16[192,768]{1,0:T(8,128)(2,1)S(1)}, bf16[192,768]{1,0:T(8,128)(2,1)S(1)}, u32[]{:S(2)}, u32[]{:S(2)}) %collective-permute-start) | collective-permute-done | bytes 294944 | tf_op jit(solution)/shard_map/ppermute | solution.py:227
  56.2 3.2 %collective-permute-done.1.first_b = bf16[192,768]{1,0:T(8,128)(2,1)S(1)} collective-permute-done((bf16[192,768]{1,0:T(8,128)(2,1)S(1)}, bf16[192,768]{1,0:T(8,128)(2,1)S(1)}, u32[]{:S(2)}, u32[]{:S(2)}) %collective-permute-start.1) | collective-permute-done | bytes 294944 | tf_op jit(solution)/shard_map/ppermute | solution.py:227
  59.4 0.0 collective-permute-done.3.sib.cols
  59.4 0.2 collective-permute-done.2.second
  59.6 2.2 %shard_map.31 = (bf16[24,8,1344]{2,1,0:T(8,128)(2,1)S(1)}, bf16[24,8,1344]{2,1,0:T(8,128)(2,1)S(1)}) custom-call(bf16[384,768]{1,0:T(8,128)(2,1)S(1)} %get-tuple-element.10.own.cols, bf16[192,768]{1,0:T(8,128)(2,1)S(1)} %collective-permute-done.first_a, bf16[192,768]{1,0:T(8,128)(2,1)S(1)} %collective-permute-done.1.first_b, ...), custom_call_target="tpu_custom_call" | custom-call | flops 1358954496 | bytes 2359296 | tf_op jit(solution)/shard_map/pallas_call | solution.py:30
  61.8 3.2 %collective-permute-start.6 = (bf16[24,8,1344]{2,1,0:T(8,128)(2,1)S(1)}, bf16[24,8,1344]{2,1,0:T(8,128)(2,1)S(1)}, u32[]{:S(2)}, u32[]{:S(2)}) collective-permute-start(bf16[24,8,1344]{2,1,0:T(8,128)(2,1)S(1)} %get-tuple-element.14), channel_id=1, source_target_pairs={{0,1},{1,0},{2,3},{3,2},{4,5},{5,4},{6,7},{7,6},{8,9},{9,8},{10,11... | collective-permute-start | bytes 1548296 | tf_op jit(solution)/shard_map/ppermute | solution.py:248
  65.0 4.0 %collective-permute-start.4 = (bf16[192,768]{1,0:T(8,128)(2,1)S(1)}, bf16[192,768]{1,0:T(8,128)(2,1)S(1)}, u32[]{:S(2)}, u32[]{:S(2)}) collective-permute-start(bf16[192,768]{1,0:T(8,128)(2,1)S(1)} %collective-permute-done.first_a), channel_id=1, source_target_pairs={{0,6},{1,3},{2,4},{3,1},{4,2},{5,7},{6,0},{7,5},{8,14},{9,11},{10,... | collective-permute-start | bytes 884744 | tf_op jit(solution)/shard_map/ppermute | solution.py:227
  69.0 3.1 %collective-permute-start.5 = (bf16[192,768]{1,0:T(8,128)(2,1)S(1)}, bf16[192,768]{1,0:T(8,128)(2,1)S(1)}, u32[]{:S(2)}, u32[]{:S(2)}) collective-permute-start(bf16[192,768]{1,0:T(8,128)(2,1)S(1)} %collective-permute-done.1.first_b), channel_id=1, source_target_pairs={{0,6},{1,3},{2,4},{3,1},{4,2},{5,7},{6,0},{7,5},{8,14},{9,11},{10,... | collective-permute-start | bytes 884744 | tf_op jit(solution)/shard_map/ppermute | solution.py:227
  72.1 2.8 %collective-permute-done.4.far_a = bf16[192,768]{1,0:T(8,128)(2,1)S(1)} collective-permute-done((bf16[192,768]{1,0:T(8,128)(2,1)S(1)}, bf16[192,768]{1,0:T(8,128)(2,1)S(1)}, u32[]{:S(2)}, u32[]{:S(2)}) %collective-permute-start.4) | collective-permute-done | bytes 294944 | tf_op jit(solution)/shard_map/ppermute | solution.py:227
  74.8 4.0 %collective-permute-done.5.far_b = bf16[192,768]{1,0:T(8,128)(2,1)S(1)} collective-permute-done((bf16[192,768]{1,0:T(8,128)(2,1)S(1)}, bf16[192,768]{1,0:T(8,128)(2,1)S(1)}, u32[]{:S(2)}, u32[]{:S(2)}) %collective-permute-start.5) | collective-permute-done | bytes 294944 | tf_op jit(solution)/shard_map/ppermute | solution.py:227
  78.8 0.6 shard_map.33
  79.4 1.9 %collective-permute-start.7 = (bf16[8,8,1344]{2,1,0:T(8,128)(2,1)S(1)}, bf16[8,8,1344]{2,1,0:T(8,128)(2,1)S(1)}, u32[]{:S(2)}, u32[]{:S(2)}) collective-permute-start(bf16[8,8,1344]{2,1,0:T(8,128)(2,1)S(1)} %shard_map.33), channel_id=1, source_target_pairs={{0,1},{1,0},{2,3},{3,2},{4,5},{5,4},{6,7},{7,6},{8,9},{9,8},{10,11... | collective-permute-start | bytes 516104 | tf_op jit(solution)/shard_map/ppermute | solution.py:250
  81.4 0.6 shard_map.32.far
  82.0 0.8 collective-permute-done.7.far_s
  82.7 0.0 collective-permute-done.6.near_s
  82.7 0.2 shard_map.34
  82.9 27.9 %all_to_all.15.received = bf16[8,64,1344]{2,1,0:T(8,128)(2,1)S(1)} all-to-all(bf16[8,64,1344]{2,1,0:T(8,128)(2,1)S(1)} %bitcast.3), channel_id=1, replica_groups={{0,64,128,192,256,320,384,448},{8,72,136,200,264,328,392,456},{16,80,14..., dimensions={0} | all-to-all | bytes 2752512 | tf_op jit(solution)/shard_map/all_to_all | solution.py:264
  110.9 0.2 shard_map.35
  111.1 16.5 %all_to_all.16.received = bf16[8,8,1344]{2,1,0:T(8,128)(2,1)S(1)} all-to-all(bf16[8,8,1344]{2,1,0:T(8,128)(2,1)S(1)} %bitcast.4), channel_id=1, replica_groups={{0,8,16,24,32,40,48,56},{64,72,80,88,96,104,112,120},{128,136,144,152,1..., dimensions={0} | all-to-all | bytes 344064 | tf_op jit(solution)/shard_map/all_to_all | solution.py:275
  127.6 0.7 shard_map.36
Async XLA Ops:
  2.7 33.9 %all-to-all-start = ((bf16[8,15,64,128]{3,2,1,0:T(8,128)(2,1)}), bf16[8,15,64,128]{3,2,1,0:T(8,128)(2,1)}, u32[]{:S(2)}, u32[]{:S(2)}) async-start(bf16[8,15,64,128]{3,2,1,0:T(8,128)(2,1)} %shard_map.28), calls=%async_computation | async-start | bytes 3932160 | tf_op jit(solution)/shard_map/all_to_all | solution.py:198
  12.8 23.8 %copy-start = (bf16[3072,384]{1,0:T(8,128)(2,1)S(1)}, bf16[3072,384]{1,0:T(8,128)(2,1)}, u32[]{:S(2)}) copy-start(bf16[3072,384]{1,0:T(8,128)(2,1)} %coeffs.3) | copy-start | bytes 7077892
  17.0 1.0 copy-start.1
  39.8 19.6 %collective-permute-start.3 = (bf16[384,768]{1,0:T(8,128)(2,1)S(1)}, bf16[384,768]{1,0:T(8,128)(2,1)S(1)}, u32[]{:S(2)}, u32[]{:S(2)}) collective-permute-start(bf16[384,768]{1,0:T(8,128)(2,1)S(1)} %get-tuple-element.10.own.cols), channel_id=1, source_target_pairs={{0,1},{1,0},{2,3},{3,2},{4,5},{5,4},{6,7},{7,6},{8,9},{9,8},{10,11... | collective-permute-start | bytes 1769480 | tf_op jit(solution)/shard_map/ppermute | solution.py:234
  41.8 17.8 %collective-permute-start.2 = (bf16[384,768]{1,0:T(8,128)(2,1)S(1)}, bf16[384,768]{1,0:T(8,128)(2,1)S(1)}, u32[]{:S(2)}, u32[]{:S(2)}) collective-permute-start(bf16[384,768]{1,0:T(8,128)(2,1)S(1)} %get-tuple-element.10.own.cols), channel_id=1, source_target_pairs={{0,6},{1,3},{2,4},{3,1},{4,2},{5,7},{6,0},{7,5},{8,14},{9,11},{10,... | collective-permute-start | bytes 1769480 | tf_op jit(solution)/shard_map/ppermute | solution.py:227
  45.8 10.5 %collective-permute-start = (bf16[192,768]{1,0:T(8,128)(2,1)S(1)}, bf16[192,768]{1,0:T(8,128)(2,1)S(1)}, u32[]{:S(2)}, u32[]{:S(2)}) collective-permute-start(bf16[192,768]{1,0:T(8,128)(2,1)S(1)} %get-tuple-element.11), channel_id=1, source_target_pairs={{0,2},{1,7},{2,0},{3,5},{4,6},{5,3},{6,4},{7,1},{8,10},{9,15},{10,... | collective-permute-start | bytes 884744 | tf_op jit(solution)/shard_map/ppermute | solution.py:227
  47.7 11.7 %collective-permute-start.1 = (bf16[192,768]{1,0:T(8,128)(2,1)S(1)}, bf16[192,768]{1,0:T(8,128)(2,1)S(1)}, u32[]{:S(2)}, u32[]{:S(2)}) collective-permute-start(bf16[192,768]{1,0:T(8,128)(2,1)S(1)} %get-tuple-element.12), channel_id=1, source_target_pairs={{0,2},{1,7},{2,0},{3,5},{4,6},{5,3},{6,4},{7,1},{8,10},{9,15},{10,... | collective-permute-start | bytes 884744 | tf_op jit(solution)/shard_map/ppermute | solution.py:227
  61.8 20.9 %collective-permute-start.6 = (bf16[24,8,1344]{2,1,0:T(8,128)(2,1)S(1)}, bf16[24,8,1344]{2,1,0:T(8,128)(2,1)S(1)}, u32[]{:S(2)}, u32[]{:S(2)}) collective-permute-start(bf16[24,8,1344]{2,1,0:T(8,128)(2,1)S(1)} %get-tuple-element.14), channel_id=1, source_target_pairs={{0,1},{1,0},{2,3},{3,2},{4,5},{5,4},{6,7},{7,6},{8,9},{9,8},{10,11... | collective-permute-start | bytes 1548296 | tf_op jit(solution)/shard_map/ppermute | solution.py:248
  65.0 9.8 %collective-permute-start.4 = (bf16[192,768]{1,0:T(8,128)(2,1)S(1)}, bf16[192,768]{1,0:T(8,128)(2,1)S(1)}, u32[]{:S(2)}, u32[]{:S(2)}) collective-permute-start(bf16[192,768]{1,0:T(8,128)(2,1)S(1)} %collective-permute-done.first_a), channel_id=1, source_target_pairs={{0,6},{1,3},{2,4},{3,1},{4,2},{5,7},{6,0},{7,5},{8,14},{9,11},{10,... | collective-permute-start | bytes 884744 | tf_op jit(solution)/shard_map/ppermute | solution.py:227
  69.0 9.8 %collective-permute-start.5 = (bf16[192,768]{1,0:T(8,128)(2,1)S(1)}, bf16[192,768]{1,0:T(8,128)(2,1)S(1)}, u32[]{:S(2)}, u32[]{:S(2)}) collective-permute-start(bf16[192,768]{1,0:T(8,128)(2,1)S(1)} %collective-permute-done.1.first_b), channel_id=1, source_target_pairs={{0,6},{1,3},{2,4},{3,1},{4,2},{5,7},{6,0},{7,5},{8,14},{9,11},{10,... | collective-permute-start | bytes 884744 | tf_op jit(solution)/shard_map/ppermute | solution.py:227
  79.4 3.3 %collective-permute-start.7 = (bf16[8,8,1344]{2,1,0:T(8,128)(2,1)S(1)}, bf16[8,8,1344]{2,1,0:T(8,128)(2,1)S(1)}, u32[]{:S(2)}, u32[]{:S(2)}) collective-permute-start(bf16[8,8,1344]{2,1,0:T(8,128)(2,1)S(1)} %shard_map.33), channel_id=1, source_target_pairs={{0,1},{1,0},{2,3},{3,2},{4,5},{5,4},{6,7},{7,6},{8,9},{9,8},{10,11... | collective-permute-start | bytes 516104 | tf_op jit(solution)/shard_map/ppermute | solution.py:250

commit v9 on v8

--- a/solution.py
+++ b/solution.py
@@ -72,7 +72,7 @@
         out[m] = part[m]
 
 
-def lower_kernel(received_hbm, coeffs, own_hbm, out, out_a, out_b, received, own, sems):
+def lower_kernel(received_hbm, coeffs, own, out, out_a, out_b, received, sems):
     size = received.shape[0] * received.shape[2]
     lanes = received.shape[3]
     half = lanes // 2
@@ -81,7 +81,6 @@
     for a in range(NB - 1):
         tiles = pl.ds(OFF_AT[a, a + 1], NB - 1 - a)
         loads.append(pltpu.make_async_copy(received_hbm.at[:, tiles], received.at[:, tiles], sems.at[a]))
-    loads.append(pltpu.make_async_copy(own_hbm, own, sems.at[NB - 1]))
     for load in loads:
         load.start()
     sums = [None] * NB
@@ -97,7 +96,6 @@
             at = (b - a - 1) * lanes
             term = part[at : at + lanes]
             sums[b] = term if sums[b] is None else sums[b] + term
-    loads[NB - 1].wait()
     for b in range(NB):
         both = own[b] if sums[b] is None else sums[b] + own[b]
         both = both.astype(BF16)
@@ -210,15 +208,14 @@
     half, half_a, half_b = call(
         lower_kernel,
         (whole, side, side),
-        (in_hbm(received), orbitals, in_hbm(own)),
+        (in_hbm(received), orbitals, own),
         flops * len(OFF),
         2 * received.size + 2 * orbitals.size,
         16,
-        in_specs=[ANY, VMEM, ANY],
+        in_specs=[ANY, VMEM, VMEM],
         scratch_shapes=[
             pltpu.VMEM(received.shape, BF16),
-            pltpu.VMEM(own.shape, F32),
-            pltpu.SemaphoreType.DMA((NB,)),
+            pltpu.SemaphoreType.DMA((NB - 1,)),
         ],
     )
 

time: 129 us -> 129 us (level)
  no operation moved by 1% of the time
where the time goes in v9:
time: 129 us; the launch traced here: 128 us
  blocking collectives  44.4 us (34%)
  waiting for transfers between devices  35.1 us (27%)
  starting transfers between devices  34 us (26%)
  Pallas kernels  14.6 us (11%)
    all_to_all x1, blocking collectives, body(): lax.all_to_all(partial.reshape(zs, ys * rows, tile_count * width), AXES,...  28 us
    all_to_all x1, waiting for transfers between devices, body(): received = lax.all_to_all(packed, ('x', 'core'), 0, 0)  19.6 us
    ppermute x5, starting transfers between devices, exchange(): lax.ppermute(array, ('x', 'core'), [(a * cores + c, b * cores + d) for (a...  16.9 us
    all_to_all x1, blocking collectives, body(): lax.all_to_all(summed.reshape(ys, rows, tile_count * width), AXES, 0, 0,...  16.5 us
    ppermute x5, waiting for transfers between devices, exchange(): lax.ppermute(array, ('x', 'core'), [(a * cores + c, b * cores + d) for (a...  14.7 us
    pallas_call x9, Pallas kernels, call(): pl.pallas_call(kernel, out_shape=out_shape, compiler_params=pltpu.Compile...  14.6 us
    all_to_all x1, starting transfers between devices, body(): received = lax.all_to_all(packed, ('x', 'core'), 0, 0)  10.1 us
    ppermute x1, starting transfers between devices, body(): near_s = lax.ppermute(near_s, 'core', swap)  3.2 us
  transfers between devices with their start and end apart: 9, of which 7 were waited for; matrix products, arithmetic and copies ran while one was open for 0% of the time, Pallas kernels for 4%

profile of v9, /device:TPU:6, one launch (start us, length us, event | category | flops | bytes accessed | tf_op | source)
XLA Modules:
  0.0 128.3 jit_solution(14390727609019159594)
XLA Ops:
  0.0 2.7 %shard_map.28 = bf16[8,15,64,128]{3,2,1,0:T(8,128)(2,1)} custom-call(bf16[2,21,64,512]{3,2,1,0:T(8,128)(2,1)} %tiles.1), custom_call_target="tpu_custom_call" | custom-call | bytes 5505024 | tf_op jit(solution)/shard_map/pallas_call | solution.py:30
  2.7 10.1 %all-to-all-start = ((bf16[8,15,64,128]{3,2,1,0:T(8,128)(2,1)}), bf16[8,15,64,128]{3,2,1,0:T(8,128)(2,1)}, u32[]{:S(2)}, u32[]{:S(2)}) async-start(bf16[8,15,64,128]{3,2,1,0:T(8,128)(2,1)} %shard_map.28), calls=%async_computation | async-start | bytes 3932160 | tf_op jit(solution)/shard_map/all_to_all | solution.py:196
  12.8 0.0 copy-start
  12.8 4.2 %shard_map.29.own = f32[6,128,384]{2,1,0:T(8,128)S(1)} custom-call(bf16[2,21,64,512]{3,2,1,0:T(8,128)(2,1)} %tiles.1, bf16[3072,384]{1,0:T(8,128)(2,1)} %coeffs.3), custom_call_target="tpu_custom_call" | custom-call | flops 1056964608 | bytes 5111808 | tf_op jit(solution)/shard_map/pallas_call | solution.py:30
  17.0 19.6 %all-to-all-done.received_hbm = bf16[8,15,64,128]{3,2,1,0:T(8,128)(2,1)} async-done(((bf16[8,15,64,128]{3,2,1,0:T(8,128)(2,1)}), bf16[8,15,64,128]{3,2,1,0:T(8,128)(2,1)}, u32[]{:S(2)}, u32[]{:S(2)}) %all-to-all-start) | async-done | bytes 1966112 | tf_op jit(solution)/shard_map/all_to_all | solution.py:196
  36.6 0.0 copy-done
  36.6 3.2 %shard_map.30 = (bf16[384,768]{1,0:T(8,128)(2,1)S(1)}, bf16[192,768]{1,0:T(8,128)(2,1)S(1)}, bf16[192,768]{1,0:T(8,128)(2,1)S(1)}) custom-call(bf16[8,15,64,128]{3,2,1,0:T(8,128)(2,1)} %all-to-all-done.received_hbm, bf16[3072,384]{1,0:T(8,128)(2,1)S(1)} %copy-done, f32[6,128,384]{2,1,0:T(8,128)S(1)} %shard_map.29.own), custom_call_target="tpu_custom_call" | custom-call | flops 754974720 | bytes 4325376 | tf_op jit(solution)/shard_map/pallas_call | solution.py:30
  39.8 1.9 %collective-permute-start.3 = (bf16[384,768]{1,0:T(8,128)(2,1)S(1)}, bf16[384,768]{1,0:T(8,128)(2,1)S(1)}, u32[]{:S(2)}, u32[]{:S(2)}) collective-permute-start(bf16[384,768]{1,0:T(8,128)(2,1)S(1)} %get-tuple-element.10.own.cols), channel_id=1, source_target_pairs={{0,1},{1,0},{2,3},{3,2},{4,5},{5,4},{6,7},{7,6},{8,9},{9,8},{10,11... | collective-permute-start | bytes 1769480 | tf_op jit(solution)/shard_map/ppermute | solution.py:231
  41.7 4.0 %collective-permute-start.2 = (bf16[384,768]{1,0:T(8,128)(2,1)S(1)}, bf16[384,768]{1,0:T(8,128)(2,1)S(1)}, u32[]{:S(2)}, u32[]{:S(2)}) collective-permute-start(bf16[384,768]{1,0:T(8,128)(2,1)S(1)} %get-tuple-element.10.own.cols), channel_id=1, source_target_pairs={{0,6},{1,3},{2,4},{3,1},{4,2},{5,7},{6,0},{7,5},{8,14},{9,11},{10,... | collective-permute-start | bytes 1769480 | tf_op jit(solution)/shard_map/ppermute | solution.py:224
  45.7 1.9 %collective-permute-start = (bf16[192,768]{1,0:T(8,128)(2,1)S(1)}, bf16[192,768]{1,0:T(8,128)(2,1)S(1)}, u32[]{:S(2)}, u32[]{:S(2)}) collective-permute-start(bf16[192,768]{1,0:T(8,128)(2,1)S(1)} %get-tuple-element.11), channel_id=1, source_target_pairs={{0,2},{1,7},{2,0},{3,5},{4,6},{5,3},{6,4},{7,1},{8,10},{9,15},{10,... | collective-permute-start | bytes 884744 | tf_op jit(solution)/shard_map/ppermute | solution.py:224
  47.6 3.9 %collective-permute-start.1 = (bf16[192,768]{1,0:T(8,128)(2,1)S(1)}, bf16[192,768]{1,0:T(8,128)(2,1)S(1)}, u32[]{:S(2)}, u32[]{:S(2)}) collective-permute-start(bf16[192,768]{1,0:T(8,128)(2,1)S(1)} %get-tuple-element.12), channel_id=1, source_target_pairs={{0,2},{1,7},{2,0},{3,5},{4,6},{5,3},{6,4},{7,1},{8,10},{9,15},{10,... | collective-permute-start | bytes 884744 | tf_op jit(solution)/shard_map/ppermute | solution.py:224
  51.6 4.6 %collective-permute-done.first_a = bf16[192,768]{1,0:T(8,128)(2,1)S(1)} collective-permute-done((bf16[192,768]{1,0:T(8,128)(2,1)S(1)}, bf16[192,768]{1,0:T(8,128)(2,1)S(1)}, u32[]{:S(2)}, u32[]{:S(2)}) %collective-permute-start) | collective-permute-done | bytes 294944 | tf_op jit(solution)/shard_map/ppermute | solution.py:224
  56.2 3.2 %collective-permute-done.1.first_b = bf16[192,768]{1,0:T(8,128)(2,1)S(1)} collective-permute-done((bf16[192,768]{1,0:T(8,128)(2,1)S(1)}, bf16[192,768]{1,0:T(8,128)(2,1)S(1)}, u32[]{:S(2)}, u32[]{:S(2)}) %collective-permute-start.1) | collective-permute-done | bytes 294944 | tf_op jit(solution)/shard_map/ppermute | solution.py:224
  59.3 0.0 collective-permute-done.3.sib.cols
  59.3 0.2 collective-permute-done.2.second
  59.6 2.2 %shard_map.31 = (bf16[24,8,1344]{2,1,0:T(8,128)(2,1)S(1)}, bf16[24,8,1344]{2,1,0:T(8,128)(2,1)S(1)}) custom-call(bf16[384,768]{1,0:T(8,128)(2,1)S(1)} %get-tuple-element.10.own.cols, bf16[192,768]{1,0:T(8,128)(2,1)S(1)} %collective-permute-done.first_a, bf16[192,768]{1,0:T(8,128)(2,1)S(1)} %collective-permute-done.1.first_b, ...), custom_call_target="tpu_custom_call" | custom-call | flops 1358954496 | bytes 2359296 | tf_op jit(solution)/shard_map/pallas_call | solution.py:30
  61.8 3.2 %collective-permute-start.6 = (bf16[24,8,1344]{2,1,0:T(8,128)(2,1)S(1)}, bf16[24,8,1344]{2,1,0:T(8,128)(2,1)S(1)}, u32[]{:S(2)}, u32[]{:S(2)}) collective-permute-start(bf16[24,8,1344]{2,1,0:T(8,128)(2,1)S(1)} %get-tuple-element.14), channel_id=1, source_target_pairs={{0,1},{1,0},{2,3},{3,2},{4,5},{5,4},{6,7},{7,6},{8,9},{9,8},{10,11... | collective-permute-start | bytes 1548296 | tf_op jit(solution)/shard_map/ppermute | solution.py:245
  65.0 4.0 %collective-permute-start.4 = (bf16[192,768]{1,0:T(8,128)(2,1)S(1)}, bf16[192,768]{1,0:T(8,128)(2,1)S(1)}, u32[]{:S(2)}, u32[]{:S(2)}) collective-permute-start(bf16[192,768]{1,0:T(8,128)(2,1)S(1)} %collective-permute-done.first_a), channel_id=1, source_target_pairs={{0,6},{1,3},{2,4},{3,1},{4,2},{5,7},{6,0},{7,5},{8,14},{9,11},{10,... | collective-permute-start | bytes 884744 | tf_op jit(solution)/shard_map/ppermute | solution.py:224
  69.0 3.1 %collective-permute-start.5 = (bf16[192,768]{1,0:T(8,128)(2,1)S(1)}, bf16[192,768]{1,0:T(8,128)(2,1)S(1)}, u32[]{:S(2)}, u32[]{:S(2)}) collective-permute-start(bf16[192,768]{1,0:T(8,128)(2,1)S(1)} %collective-permute-done.1.first_b), channel_id=1, source_target_pairs={{0,6},{1,3},{2,4},{3,1},{4,2},{5,7},{6,0},{7,5},{8,14},{9,11},{10,... | collective-permute-start | bytes 884744 | tf_op jit(solution)/shard_map/ppermute | solution.py:224
  72.0 2.8 %collective-permute-done.4.far_a = bf16[192,768]{1,0:T(8,128)(2,1)S(1)} collective-permute-done((bf16[192,768]{1,0:T(8,128)(2,1)S(1)}, bf16[192,768]{1,0:T(8,128)(2,1)S(1)}, u32[]{:S(2)}, u32[]{:S(2)}) %collective-permute-start.4) | collective-permute-done | bytes 294944 | tf_op jit(solution)/shard_map/ppermute | solution.py:224
  74.8 4.0 %collective-permute-done.5.far_b = bf16[192,768]{1,0:T(8,128)(2,1)S(1)} collective-permute-done((bf16[192,768]{1,0:T(8,128)(2,1)S(1)}, bf16[192,768]{1,0:T(8,128)(2,1)S(1)}, u32[]{:S(2)}, u32[]{:S(2)}) %collective-permute-start.5) | collective-permute-done | bytes 294944 | tf_op jit(solution)/shard_map/ppermute | solution.py:224
  78.8 0.6 shard_map.33
  79.4 1.9 %collective-permute-start.7 = (bf16[8,8,1344]{2,1,0:T(8,128)(2,1)S(1)}, bf16[8,8,1344]{2,1,0:T(8,128)(2,1)S(1)}, u32[]{:S(2)}, u32[]{:S(2)}) collective-permute-start(bf16[8,8,1344]{2,1,0:T(8,128)(2,1)S(1)} %shard_map.33), channel_id=1, source_target_pairs={{0,1},{1,0},{2,3},{3,2},{4,5},{5,4},{6,7},{7,6},{8,9},{9,8},{10,11... | collective-permute-start | bytes 516104 | tf_op jit(solution)/shard_map/ppermute | solution.py:247
  81.3 0.6 shard_map.32.far
  81.9 0.8 collective-permute-done.7.far_s
  82.7 0.0 collective-permute-done.6.near_s
  82.7 0.2 shard_map.34
  82.9 28.0 %all_to_all.15.received = bf16[8,64,1344]{2,1,0:T(8,128)(2,1)S(1)} all-to-all(bf16[8,64,1344]{2,1,0:T(8,128)(2,1)S(1)} %bitcast.3), channel_id=1, replica_groups={{0,64,128,192,256,320,384,448},{8,72,136,200,264,328,392,456},{16,80,14..., dimensions={0} | all-to-all | bytes 2752512 | tf_op jit(solution)/shard_map/all_to_all | solution.py:261
  110.8 0.2 shard_map.35
  111.0 16.5 %all_to_all.16.received = bf16[8,8,1344]{2,1,0:T(8,128)(2,1)S(1)} all-to-all(bf16[8,8,1344]{2,1,0:T(8,128)(2,1)S(1)} %bitcast.4), channel_id=1, replica_groups={{0,8,16,24,32,40,48,56},{64,72,80,88,96,104,112,120},{128,136,144,152,1..., dimensions={0} | all-to-all | bytes 344064 | tf_op jit(solution)/shard_map/all_to_all | solution.py:272
  127.5 0.7 shard_map.36
Async XLA Ops:
  2.7 33.9 %all-to-all-start = ((bf16[8,15,64,128]{3,2,1,0:T(8,128)(2,1)}), bf16[8,15,64,128]{3,2,1,0:T(8,128)(2,1)}, u32[]{:S(2)}, u32[]{:S(2)}) async-start(bf16[8,15,64,128]{3,2,1,0:T(8,128)(2,1)} %shard_map.28), calls=%async_computation | async-start | bytes 3932160 | tf_op jit(solution)/shard_map/all_to_all | solution.py:196
  12.8 23.8 %copy-start = (bf16[3072,384]{1,0:T(8,128)(2,1)S(1)}, bf16[3072,384]{1,0:T(8,128)(2,1)}, u32[]{:S(2)}) copy-start(bf16[3072,384]{1,0:T(8,128)(2,1)} %coeffs.3) | copy-start | bytes 7077892
  39.8 19.6 %collective-permute-start.3 = (bf16[384,768]{1,0:T(8,128)(2,1)S(1)}, bf16[384,768]{1,0:T(8,128)(2,1)S(1)}, u32[]{:S(2)}, u32[]{:S(2)}) collective-permute-start(bf16[384,768]{1,0:T(8,128)(2,1)S(1)} %get-tuple-element.10.own.cols), channel_id=1, source_target_pairs={{0,1},{1,0},{2,3},{3,2},{4,5},{5,4},{6,7},{7,6},{8,9},{9,8},{10,11... | collective-permute-start | bytes 1769480 | tf_op jit(solution)/shard_map/ppermute | solution.py:231
  41.7 17.8 %collective-permute-start.2 = (bf16[384,768]{1,0:T(8,128)(2,1)S(1)}, bf16[384,768]{1,0:T(8,128)(2,1)S(1)}, u32[]{:S(2)}, u32[]{:S(2)}) collective-permute-start(bf16[384,768]{1,0:T(8,128)(2,1)S(1)} %get-tuple-element.10.own.cols), channel_id=1, source_target_pairs={{0,6},{1,3},{2,4},{3,1},{4,2},{5,7},{6,0},{7,5},{8,14},{9,11},{10,... | collective-permute-start | bytes 1769480 | tf_op jit(solution)/shard_map/ppermute | solution.py:224
  45.7 10.5 %collective-permute-start = (bf16[192,768]{1,0:T(8,128)(2,1)S(1)}, bf16[192,768]{1,0:T(8,128)(2,1)S(1)}, u32[]{:S(2)}, u32[]{:S(2)}) collective-permute-start(bf16[192,768]{1,0:T(8,128)(2,1)S(1)} %get-tuple-element.11), channel_id=1, source_target_pairs={{0,2},{1,7},{2,0},{3,5},{4,6},{5,3},{6,4},{7,1},{8,10},{9,15},{10,... | collective-permute-start | bytes 884744 | tf_op jit(solution)/shard_map/ppermute | solution.py:224
  47.6 11.7 %collective-permute-start.1 = (bf16[192,768]{1,0:T(8,128)(2,1)S(1)}, bf16[192,768]{1,0:T(8,128)(2,1)S(1)}, u32[]{:S(2)}, u32[]{:S(2)}) collective-permute-start(bf16[192,768]{1,0:T(8,128)(2,1)S(1)} %get-tuple-element.12), channel_id=1, source_target_pairs={{0,2},{1,7},{2,0},{3,5},{4,6},{5,3},{6,4},{7,1},{8,10},{9,15},{10,... | collective-permute-start | bytes 884744 | tf_op jit(solution)/shard_map/ppermute | solution.py:224
  61.8 20.9 %collective-permute-start.6 = (bf16[24,8,1344]{2,1,0:T(8,128)(2,1)S(1)}, bf16[24,8,1344]{2,1,0:T(8,128)(2,1)S(1)}, u32[]{:S(2)}, u32[]{:S(2)}) collective-permute-start(bf16[24,8,1344]{2,1,0:T(8,128)(2,1)S(1)} %get-tuple-element.14), channel_id=1, source_target_pairs={{0,1},{1,0},{2,3},{3,2},{4,5},{5,4},{6,7},{7,6},{8,9},{9,8},{10,11... | collective-permute-start | bytes 1548296 | tf_op jit(solution)/shard_map/ppermute | solution.py:245
  65.0 9.8 %collective-permute-start.4 = (bf16[192,768]{1,0:T(8,128)(2,1)S(1)}, bf16[192,768]{1,0:T(8,128)(2,1)S(1)}, u32[]{:S(2)}, u32[]{:S(2)}) collective-permute-start(bf16[192,768]{1,0:T(8,128)(2,1)S(1)} %collective-permute-done.first_a), channel_id=1, source_target_pairs={{0,6},{1,3},{2,4},{3,1},{4,2},{5,7},{6,0},{7,5},{8,14},{9,11},{10,... | collective-permute-start | bytes 884744 | tf_op jit(solution)/shard_map/ppermute | solution.py:224
  69.0 9.8 %collective-permute-start.5 = (bf16[192,768]{1,0:T(8,128)(2,1)S(1)}, bf16[192,768]{1,0:T(8,128)(2,1)S(1)}, u32[]{:S(2)}, u32[]{:S(2)}) collective-permute-start(bf16[192,768]{1,0:T(8,128)(2,1)S(1)} %collective-permute-done.1.first_b), channel_id=1, source_target_pairs={{0,6},{1,3},{2,4},{3,1},{4,2},{5,7},{6,0},{7,5},{8,14},{9,11},{10,... | collective-permute-start | bytes 884744 | tf_op jit(solution)/shard_map/ppermute | solution.py:224
  79.4 3.3 %collective-permute-start.7 = (bf16[8,8,1344]{2,1,0:T(8,128)(2,1)S(1)}, bf16[8,8,1344]{2,1,0:T(8,128)(2,1)S(1)}, u32[]{:S(2)}, u32[]{:S(2)}) collective-permute-start(bf16[8,8,1344]{2,1,0:T(8,128)(2,1)S(1)} %shard_map.33), channel_id=1, source_target_pairs={{0,1},{1,0},{2,3},{3,2},{4,5},{5,4},{6,7},{7,6},{8,9},{9,8},{10,11... | collective-permute-start | bytes 516104 | tf_op jit(solution)/shard_map/ppermute | solution.py:247

commit v10 on v9

--- a/solution.py
+++ b/solution.py
@@ -9,6 +9,7 @@
 
 
 NB = 6
+CUT = 4
 AXES = ("z", "y", "x", "core")
 F32 = jnp.float32
 BF16 = jnp.bfloat16
@@ -99,7 +100,7 @@
     for b in range(NB):
         both = own[b] if sums[b] is None else sums[b] + own[b]
         both = both.astype(BF16)
-        for ref, at in ((out, b), (out_a if b < NB // 2 else out_b, b % (NB // 2))):
+        for ref, at in ((out, b), (out_a, b) if b < CUT else (out_b, b - CUT)):
             ref[at * half : (at + 1) * half, :occ] = both[:half]
             ref[at * half : (at + 1) * half, occ:] = both[half:]
 
@@ -203,11 +204,12 @@
         52,
     )
     whole = jax.ShapeDtypeStruct((NB * width, slabs * occ), BF16)
-    side = jax.ShapeDtypeStruct((NB // 2 * width, slabs * occ), BF16)
+    low = jax.ShapeDtypeStruct((CUT * width, slabs * occ), BF16)
+    high = jax.ShapeDtypeStruct(((NB - CUT) * width, slabs * occ), BF16)
     in_hbm = lambda array: pltpu.with_memory_space_constraint(array, pltpu.HBM)
     half, half_a, half_b = call(
         lower_kernel,
-        (whole, side, side),
+        (whole, low, high),
         (in_hbm(received), orbitals, own),
         flops * len(OFF),
         2 * received.size + 2 * orbitals.size,

time: 129 us -> 124 us (0.961)
  the two profiles are of different devices: /device:TPU:6 before, /device:TPU:8 now
where the time goes in v10:
time: 124 us; the launch traced here: 123 us
  blocking collectives  48.7 us (39%)
  waiting for transfers between devices  34.3 us (28%)
  starting transfers between devices  26.1 us (21%)
  Pallas kernels  14.2 us (11%)
    all_to_all x1, blocking collectives, body(): lax.all_to_all(partial.reshape(zs, ys * rows, tile_count * width), AXES,...  33.2 us
    all_to_all x1, waiting for transfers between devices, body(): received = lax.all_to_all(packed, ('x', 'core'), 0, 0)  21.6 us
    all_to_all x1, blocking collectives, body(): lax.all_to_all(summed.reshape(ys, rows, tile_count * width), AXES, 0, 0,...  15.5 us
    ppermute x5, starting transfers between devices, exchange(): lax.ppermute(array, ('x', 'core'), [(a * cores + c, b * cores + d) for (a...  15.5 us
    pallas_call x9, Pallas kernels, call(): pl.pallas_call(kernel, out_shape=out_shape, compiler_params=pltpu.Compile...  14.2 us
    ppermute x5, waiting for transfers between devices, exchange(): lax.ppermute(array, ('x', 'core'), [(a * cores + c, b * cores + d) for (a...  11.9 us
    all_to_all x1, starting transfers between devices, body(): received = lax.all_to_all(packed, ('x', 'core'), 0, 0)  4.35 us
  transfers between devices with their start and end apart: 9, of which 4 were waited for; matrix products, arithmetic and copies ran while one was open for 0% of the time, Pallas kernels for 6%

profile of v10, /device:TPU:8, one launch (start us, length us, event | category | flops | bytes accessed | tf_op | source)
XLA Modules:
  0.0 123.5 jit_solution(11268197459310425209)
XLA Ops:
  0.0 2.7 %shard_map.28 = bf16[8,15,64,128]{3,2,1,0:T(8,128)(2,1)} custom-call(bf16[2,21,64,512]{3,2,1,0:T(8,128)(2,1)} %tiles.1), custom_call_target="tpu_custom_call" | custom-call | bytes 5505024 | tf_op jit(solution)/shard_map/pallas_call | solution.py:31
  2.7 4.4 %all-to-all-start = ((bf16[8,15,64,128]{3,2,1,0:T(8,128)(2,1)}), bf16[8,15,64,128]{3,2,1,0:T(8,128)(2,1)}, u32[]{:S(2)}, u32[]{:S(2)}) async-start(bf16[8,15,64,128]{3,2,1,0:T(8,128)(2,1)} %shard_map.28), calls=%async_computation | async-start | bytes 3932160 | tf_op jit(solution)/shard_map/all_to_all | solution.py:197
  7.1 0.0 copy-start
  7.1 4.2 %shard_map.29.own = f32[6,128,384]{2,1,0:T(8,128)S(1)} custom-call(bf16[2,21,64,512]{3,2,1,0:T(8,128)(2,1)} %tiles.1, bf16[3072,384]{1,0:T(8,128)(2,1)} %coeffs.3), custom_call_target="tpu_custom_call" | custom-call | flops 1056964608 | bytes 5111808 | tf_op jit(solution)/shard_map/pallas_call | solution.py:31
  11.3 21.6 %all-to-all-done.received_hbm = bf16[8,15,64,128]{3,2,1,0:T(8,128)(2,1)} async-done(((bf16[8,15,64,128]{3,2,1,0:T(8,128)(2,1)}), bf16[8,15,64,128]{3,2,1,0:T(8,128)(2,1)}, u32[]{:S(2)}, u32[]{:S(2)}) %all-to-all-start) | async-done | bytes 1966112 | tf_op jit(solution)/shard_map/all_to_all | solution.py:197
  32.9 0.0 copy-done
  32.9 3.2 %shard_map.30 = (bf16[384,768]{1,0:T(8,128)(2,1)S(1)}, bf16[256,768]{1,0:T(8,128)(2,1)S(1)}, bf16[128,768]{1,0:T(8,128)(2,1)S(1)}) custom-call(bf16[8,15,64,128]{3,2,1,0:T(8,128)(2,1)} %all-to-all-done.received_hbm, bf16[3072,384]{1,0:T(8,128)(2,1)S(1)} %copy-done, f32[6,128,384]{2,1,0:T(8,128)S(1)} %shard_map.29.own), custom_call_target="tpu_custom_call" | custom-call | flops 754974720 | bytes 4325376 | tf_op jit(solution)/shard_map/pallas_call | solution.py:31
  36.1 1.9 %collective-permute-start.3 = (bf16[384,768]{1,0:T(8,128)(2,1)S(1)}, bf16[384,768]{1,0:T(8,128)(2,1)S(1)}, u32[]{:S(2)}, u32[]{:S(2)}) collective-permute-start(bf16[384,768]{1,0:T(8,128)(2,1)S(1)} %get-tuple-element.10.own.cols), channel_id=1, source_target_pairs={{0,1},{1,0},{2,3},{3,2},{4,5},{5,4},{6,7},{7,6},{8,9},{9,8},{10,11... | collective-permute-start | bytes 1769480 | tf_op jit(solution)/shard_map/ppermute | solution.py:233
  38.0 3.1 %collective-permute-start.2 = (bf16[384,768]{1,0:T(8,128)(2,1)S(1)}, bf16[384,768]{1,0:T(8,128)(2,1)S(1)}, u32[]{:S(2)}, u32[]{:S(2)}) collective-permute-start(bf16[384,768]{1,0:T(8,128)(2,1)S(1)} %get-tuple-element.10.own.cols), channel_id=1, source_target_pairs={{0,6},{1,3},{2,4},{3,1},{4,2},{5,7},{6,0},{7,5},{8,14},{9,11},{10,... | collective-permute-start | bytes 1769480 | tf_op jit(solution)/shard_map/ppermute | solution.py:226
  41.1 1.9 %collective-permute-start = (bf16[256,768]{1,0:T(8,128)(2,1)S(1)}, bf16[256,768]{1,0:T(8,128)(2,1)S(1)}, u32[]{:S(2)}, u32[]{:S(2)}) collective-permute-start(bf16[256,768]{1,0:T(8,128)(2,1)S(1)} %get-tuple-element.11), channel_id=1, source_target_pairs={{0,2},{1,7},{2,0},{3,5},{4,6},{5,3},{6,4},{7,1},{8,10},{9,15},{10,... | collective-permute-start | bytes 1179656 | tf_op jit(solution)/shard_map/ppermute | solution.py:226
  43.0 3.9 %collective-permute-start.1 = (bf16[128,768]{1,0:T(8,128)(2,1)S(1)}, bf16[128,768]{1,0:T(8,128)(2,1)S(1)}, u32[]{:S(2)}, u32[]{:S(2)}) collective-permute-start(bf16[128,768]{1,0:T(8,128)(2,1)S(1)} %get-tuple-element.12), channel_id=1, source_target_pairs={{0,2},{1,7},{2,0},{3,5},{4,6},{5,3},{6,4},{7,1},{8,10},{9,15},{10,... | collective-permute-start | bytes 589832 | tf_op jit(solution)/shard_map/ppermute | solution.py:226
  47.0 6.6 %collective-permute-done.first_a = bf16[256,768]{1,0:T(8,128)(2,1)S(1)} collective-permute-done((bf16[256,768]{1,0:T(8,128)(2,1)S(1)}, bf16[256,768]{1,0:T(8,128)(2,1)S(1)}, u32[]{:S(2)}, u32[]{:S(2)}) %collective-permute-start) | collective-permute-done | bytes 393248 | tf_op jit(solution)/shard_map/ppermute | solution.py:226
  53.5 3.1 %collective-permute-start.4 = (bf16[256,768]{1,0:T(8,128)(2,1)S(1)}, bf16[256,768]{1,0:T(8,128)(2,1)S(1)}, u32[]{:S(2)}, u32[]{:S(2)}) collective-permute-start(bf16[256,768]{1,0:T(8,128)(2,1)S(1)} %collective-permute-done.first_a), channel_id=1, source_target_pairs={{0,6},{1,3},{2,4},{3,1},{4,2},{5,7},{6,0},{7,5},{8,14},{9,11},{10,... | collective-permute-start | bytes 1179656 | tf_op jit(solution)/shard_map/ppermute | solution.py:226
  56.6 0.0 collective-permute-done.1.first_b
  56.6 0.0 collective-permute-done.3.sib.cols
  56.6 0.0 collective-permute-done.2.second
  56.7 2.0 %shard_map.31 = (bf16[24,8,1344]{2,1,0:T(8,128)(2,1)S(1)}, bf16[24,8,1344]{2,1,0:T(8,128)(2,1)S(1)}) custom-call(bf16[384,768]{1,0:T(8,128)(2,1)S(1)} %get-tuple-element.10.own.cols, bf16[256,768]{1,0:T(8,128)(2,1)S(1)} %collective-permute-done.first_a, bf16[128,768]{1,0:T(8,128)(2,1)S(1)} %collective-permute-done.1.first_b, ...), custom_call_target="tpu_custom_call" | custom-call | flops 1358954496 | bytes 2359296 | tf_op jit(solution)/shard_map/pallas_call | solution.py:31
  58.6 2.4 %collective-permute-start.6 = (bf16[24,8,1344]{2,1,0:T(8,128)(2,1)S(1)}, bf16[24,8,1344]{2,1,0:T(8,128)(2,1)S(1)}, u32[]{:S(2)}, u32[]{:S(2)}) collective-permute-start(bf16[24,8,1344]{2,1,0:T(8,128)(2,1)S(1)} %get-tuple-element.14), channel_id=1, source_target_pairs={{0,1},{1,0},{2,3},{3,2},{4,5},{5,4},{6,7},{7,6},{8,9},{9,8},{10,11... | collective-permute-start | bytes 1548296 | tf_op jit(solution)/shard_map/ppermute | solution.py:247
  61.0 3.5 %collective-permute-start.5 = (bf16[128,768]{1,0:T(8,128)(2,1)S(1)}, bf16[128,768]{1,0:T(8,128)(2,1)S(1)}, u32[]{:S(2)}, u32[]{:S(2)}) collective-permute-start(bf16[128,768]{1,0:T(8,128)(2,1)S(1)} %collective-permute-done.1.first_b), channel_id=1, source_target_pairs={{0,6},{1,3},{2,4},{3,1},{4,2},{5,7},{6,0},{7,5},{8,14},{9,11},{10,... | collective-permute-start | bytes 589832 | tf_op jit(solution)/shard_map/ppermute | solution.py:226
  64.5 5.3 %collective-permute-done.5.far_b = bf16[128,768]{1,0:T(8,128)(2,1)S(1)} collective-permute-done((bf16[128,768]{1,0:T(8,128)(2,1)S(1)}, bf16[128,768]{1,0:T(8,128)(2,1)S(1)}, u32[]{:S(2)}, u32[]{:S(2)}) %collective-permute-start.5) | collective-permute-done | bytes 196640 | tf_op jit(solution)/shard_map/ppermute | solution.py:226
  69.8 0.0 collective-permute-done.4.far_a
  69.8 0.5 shard_map.33
  70.3 1.9 %collective-permute-start.7 = (bf16[8,8,1344]{2,1,0:T(8,128)(2,1)S(1)}, bf16[8,8,1344]{2,1,0:T(8,128)(2,1)S(1)}, u32[]{:S(2)}, u32[]{:S(2)}) collective-permute-start(bf16[8,8,1344]{2,1,0:T(8,128)(2,1)S(1)} %shard_map.33), channel_id=1, source_target_pairs={{0,1},{1,0},{2,3},{3,2},{4,5},{5,4},{6,7},{7,6},{8,9},{9,8},{10,11... | collective-permute-start | bytes 516104 | tf_op jit(solution)/shard_map/ppermute | solution.py:249
  72.3 0.5 shard_map.32.far
  72.8 0.9 collective-permute-done.7.far_s
  73.6 0.0 collective-permute-done.6.near_s
  73.7 0.2 shard_map.34
  73.8 33.2 %all_to_all.15.received = bf16[8,64,1344]{2,1,0:T(8,128)(2,1)S(1)} all-to-all(bf16[8,64,1344]{2,1,0:T(8,128)(2,1)S(1)} %bitcast.3), channel_id=1, replica_groups={{0,64,128,192,256,320,384,448},{8,72,136,200,264,328,392,456},{16,80,14..., dimensions={0} | all-to-all | bytes 2752512 | tf_op jit(solution)/shard_map/all_to_all | solution.py:263
  107.1 0.2 shard_map.35
  107.3 15.5 %all_to_all.16.received = bf16[8,8,1344]{2,1,0:T(8,128)(2,1)S(1)} all-to-all(bf16[8,8,1344]{2,1,0:T(8,128)(2,1)S(1)} %bitcast.4), channel_id=1, replica_groups={{0,8,16,24,32,40,48,56},{64,72,80,88,96,104,112,120},{128,136,144,152,1..., dimensions={0} | all-to-all | bytes 344064 | tf_op jit(solution)/shard_map/all_to_all | solution.py:274
  122.7 0.7 shard_map.36
Async XLA Ops:
  2.7 30.2 %all-to-all-start = ((bf16[8,15,64,128]{3,2,1,0:T(8,128)(2,1)}), bf16[8,15,64,128]{3,2,1,0:T(8,128)(2,1)}, u32[]{:S(2)}, u32[]{:S(2)}) async-start(bf16[8,15,64,128]{3,2,1,0:T(8,128)(2,1)} %shard_map.28), calls=%async_computation | async-start | bytes 3932160 | tf_op jit(solution)/shard_map/all_to_all | solution.py:197
  7.1 25.8 %copy-start = (bf16[3072,384]{1,0:T(8,128)(2,1)S(1)}, bf16[3072,384]{1,0:T(8,128)(2,1)}, u32[]{:S(2)}) copy-start(bf16[3072,384]{1,0:T(8,128)(2,1)} %coeffs.3) | copy-start | bytes 7077892
  36.1 20.5 %collective-permute-start.3 = (bf16[384,768]{1,0:T(8,128)(2,1)S(1)}, bf16[384,768]{1,0:T(8,128)(2,1)S(1)}, u32[]{:S(2)}, u32[]{:S(2)}) collective-permute-start(bf16[384,768]{1,0:T(8,128)(2,1)S(1)} %get-tuple-element.10.own.cols), channel_id=1, source_target_pairs={{0,1},{1,0},{2,3},{3,2},{4,5},{5,4},{6,7},{7,6},{8,9},{9,8},{10,11... | collective-permute-start | bytes 1769480 | tf_op jit(solution)/shard_map/ppermute | solution.py:233
  38.0 18.6 %collective-permute-start.2 = (bf16[384,768]{1,0:T(8,128)(2,1)S(1)}, bf16[384,768]{1,0:T(8,128)(2,1)S(1)}, u32[]{:S(2)}, u32[]{:S(2)}) collective-permute-start(bf16[384,768]{1,0:T(8,128)(2,1)S(1)} %get-tuple-element.10.own.cols), channel_id=1, source_target_pairs={{0,6},{1,3},{2,4},{3,1},{4,2},{5,7},{6,0},{7,5},{8,14},{9,11},{10,... | collective-permute-start | bytes 1769480 | tf_op jit(solution)/shard_map/ppermute | solution.py:226
  41.1 12.4 %collective-permute-start = (bf16[256,768]{1,0:T(8,128)(2,1)S(1)}, bf16[256,768]{1,0:T(8,128)(2,1)S(1)}, u32[]{:S(2)}, u32[]{:S(2)}) collective-permute-start(bf16[256,768]{1,0:T(8,128)(2,1)S(1)} %get-tuple-element.11), channel_id=1, source_target_pairs={{0,2},{1,7},{2,0},{3,5},{4,6},{5,3},{6,4},{7,1},{8,10},{9,15},{10,... | collective-permute-start | bytes 1179656 | tf_op jit(solution)/shard_map/ppermute | solution.py:226
  43.0 13.6 %collective-permute-start.1 = (bf16[128,768]{1,0:T(8,128)(2,1)S(1)}, bf16[128,768]{1,0:T(8,128)(2,1)S(1)}, u32[]{:S(2)}, u32[]{:S(2)}) collective-permute-start(bf16[128,768]{1,0:T(8,128)(2,1)S(1)} %get-tuple-element.12), channel_id=1, source_target_pairs={{0,2},{1,7},{2,0},{3,5},{4,6},{5,3},{6,4},{7,1},{8,10},{9,15},{10,... | collective-permute-start | bytes 589832 | tf_op jit(solution)/shard_map/ppermute | solution.py:226
  53.5 16.3 %collective-permute-start.4 = (bf16[256,768]{1,0:T(8,128)(2,1)S(1)}, bf16[256,768]{1,0:T(8,128)(2,1)S(1)}, u32[]{:S(2)}, u32[]{:S(2)}) collective-permute-start(bf16[256,768]{1,0:T(8,128)(2,1)S(1)} %collective-permute-done.first_a), channel_id=1, source_target_pairs={{0,6},{1,3},{2,4},{3,1},{4,2},{5,7},{6,0},{7,5},{8,14},{9,11},{10,... | collective-permute-start | bytes 1179656 | tf_op jit(solution)/shard_map/ppermute | solution.py:226
  58.6 15.0 %collective-permute-start.6 = (bf16[24,8,1344]{2,1,0:T(8,128)(2,1)S(1)}, bf16[24,8,1344]{2,1,0:T(8,128)(2,1)S(1)}, u32[]{:S(2)}, u32[]{:S(2)}) collective-permute-start(bf16[24,8,1344]{2,1,0:T(8,128)(2,1)S(1)} %get-tuple-element.14), channel_id=1, source_target_pairs={{0,1},{1,0},{2,3},{3,2},{4,5},{5,4},{6,7},{7,6},{8,9},{9,8},{10,11... | collective-permute-start | bytes 1548296 | tf_op jit(solution)/shard_map/ppermute | solution.py:247
  61.0 8.8 %collective-permute-start.5 = (bf16[128,768]{1,0:T(8,128)(2,1)S(1)}, bf16[128,768]{1,0:T(8,128)(2,1)S(1)}, u32[]{:S(2)}, u32[]{:S(2)}) collective-permute-start(bf16[128,768]{1,0:T(8,128)(2,1)S(1)} %collective-permute-done.1.first_b), channel_id=1, source_target_pairs={{0,6},{1,3},{2,4},{3,1},{4,2},{5,7},{6,0},{7,5},{8,14},{9,11},{10,... | collective-permute-start | bytes 589832 | tf_op jit(solution)/shard_map/ppermute | solution.py:226
  70.3 3.3 %collective-permute-start.7 = (bf16[8,8,1344]{2,1,0:T(8,128)(2,1)S(1)}, bf16[8,8,1344]{2,1,0:T(8,128)(2,1)S(1)}, u32[]{:S(2)}, u32[]{:S(2)}) collective-permute-start(bf16[8,8,1344]{2,1,0:T(8,128)(2,1)S(1)} %shard_map.33), channel_id=1, source_target_pairs={{0,1},{1,0},{2,3},{3,2},{4,5},{5,4},{6,7},{7,6},{8,9},{9,8},{10,11... | collective-permute-start | bytes 516104 | tf_op jit(solution)/shard_map/ppermute | solution.py:249
